TPU v7x, 32 devices: a whole 2x2x4 slice. The times are simulated.
32 devices in a mesh: sp: 8 (over z, y), tp: 4 (over x, core).
Axes of the slice: x: 2, y: 2, z: 4, core: 2. Of those that a mesh axis runs over, the one named last changes fastest.
Arguments:
- patches: float32 [160, 240, 256], P('sp', None, 'tp'), may hold values from -6 to 6
- merge_gain: float32 [4, 256], P(None, 'tp'), may hold values from 0.25 to 1.75
- merge_shift: float32 [4, 256], P(None, 'tp'), may hold values from -1.75 to 1.75
- merge_weight: float32 [4, 256, 512], P(None, 'tp'), may hold values from -0.1875 to 0.1875
- first_gain: float32 [2, 512], replicated, may hold values from 0.25 to 1.75
- first_shift: float32 [2, 512], replicated, may hold values from -1.75 to 1.75
- input_weight: float32 [2, 512, 3, 512], P(None, None, None, 'tp'), may hold values from -0.375 to 0.375
- input_bias: float32 [2, 2, 512], P(None, None, 'tp'), may hold values from -1.75 to 1.75
- position_table: float32 [2, 361, 16], P(None, None, 'tp'), may hold values from -6 to 6
- output_weight: float32 [2, 512, 512], P(None, 'tp'), may hold values from -0.75 to 0.75
- output_bias: float32 [2, 512], replicated, may hold values from -1.75 to 1.75
- second_gain: float32 [2, 512], replicated, may hold values from 0.25 to 1.75
- second_shift: float32 [2, 512], replicated, may hold values from -1.75 to 1.75
- expand_weight: float32 [2, 512, 2048], P(None, None, 'tp'), may hold values from -0.25 to 0.25
- expand_bias: float32 [2, 2048], P(None, 'tp'), may hold values from -1.75 to 1.75
- shrink_weight: float32 [2, 2048, 512], P(None, 'tp'), may hold values from -0.1875 to 0.1875
- shrink_bias: float32 [2, 512], replicated, may hold values from -1.75 to 1.75
- page_map: int32 [8, 12], replicated, may hold values from 0 to 58, as said below
- valid_flags: int32 [80, 120], P('sp'), may hold values from 0 to 1, as said below
- cotangent: float32 [80, 120, 512], P('sp', None, 'tp'), may hold values from -6 to 6
Outputs:
- output: float32 [80, 120, 512], P('sp', None, 'tp')
- patches_grad: float32 [160, 240, 256], P('sp', None, 'tp')
- merge_gain_grad: float32 [4, 256], P(None, 'tp')
- merge_shift_grad: float32 [4, 256], P(None, 'tp')
- merge_weight_grad: float32 [4, 256, 512], P(None, 'tp')
- first_gain_grad: float32 [2, 512], replicated
- first_shift_grad: float32 [2, 512], replicated
- input_weight_grad: float32 [2, 512, 3, 512], P(None, None, None, 'tp')
- input_bias_grad: float32 [2, 2, 512], P(None, None, 'tp')
- position_table_grad: float32 [2, 361, 16], P(None, None, 'tp')
- output_weight_grad: float32 [2, 512, 512], P(None, 'tp')
- output_bias_grad: float32 [2, 512], replicated
- second_gain_grad: float32 [2, 512], replicated
- second_shift_grad: float32 [2, 512], replicated
- expand_weight_grad: float32 [2, 512, 2048], P(None, None, 'tp')
- expand_bias_grad: float32 [2, 2048], P(None, 'tp')
- shrink_weight_grad: float32 [2, 2048, 512], P(None, 'tp')
- shrink_bias_grad: float32 [2, 512], replicated
- rms: float32 [5], replicated
Inputs may be any that keep to these rules, and one draw needn't show every extreme that they name: `page_map`: the windows of one page form a rectangle of whole windows; pages are numbered row_page * 13 + column_page, both never falling along their axis, starting at 0 in the first window, with exactly 4 row breaks and 6 column breaks, so the last window holds the largest number. `valid_flags`: the first patch of every window is valid.
All inputs are finite; a program needn't handle non-finite values.
Results may differ from a plain program's by a relative error of at most 0.0003.
Values sent between devices are 32-bit elements; how exact they have to be, the bound alone decides.
A program may use at most 192 MiB of HBM per device.

v0:
```python
import jax
import jax.numpy as jnp
from jax import lax
from jax.sharding import PartitionSpec as P

C = 512
HD = 32
C2 = 256
WIN = 10
SHIFT = 5


highest = lax.Precision.HIGHEST
epsilon = 1e-05
masked = -1000000000.0


def passed_along(block, axis, distance):
    devices = range(lax.axis_size(axis))
    route = [((i - distance) % len(devices), i) for i in devices]
    return lax.ppermute(block, axis, route)


def layer_norm(values, gain_row, offset):
    center = values - jnp.mean(values, axis=-1, keepdims=True)
    spread = jnp.mean(center * center, axis=-1, keepdims=True)
    return center * lax.rsqrt(spread + epsilon) * gain_row + offset


def exact_gelu(values):
    return jax.nn.gelu(values, approximate=False)


def relative_index():
    positions = jnp.arange(WIN * WIN, dtype=jnp.int32)
    row_of = positions // WIN
    column_of = positions % WIN
    row_offset = row_of[:, None] - row_of[None, :] + (WIN - 1)
    column_offset = column_of[:, None] - column_of[None, :] + (WIN - 1)
    return row_offset * (2 * WIN - 1) + column_offset


def window_attention(queries, key_rows, value_rows, bias_grid, region, validity):
    scores = (
        jnp.einsum("wqhd,wkhd->whqk", queries, key_rows, precision=highest) * HD ** (-0.5)
        + bias_grid[None]
    )
    same_region = region[:, :, None] == region[:, None, :]
    diagonal = jnp.eye(WIN * WIN, dtype=bool)[None]
    allowed = same_region & (validity[:, None, :] > 0) | diagonal
    scores = jnp.where(allowed[:, None], scores, masked)
    row_max = jnp.max(scores, axis=-1, keepdims=True)
    weights = jnp.exp(scores - row_max)
    weights = weights / jnp.sum(weights, axis=-1, keepdims=True)
    return jnp.einsum("whqk,wkhd->wqhd", weights, value_rows, precision=highest)


def to_windows(values):
    row_count, column_count = (values.shape[0], values.shape[1])
    trailing = values.shape[2:]
    windowed = values.reshape((row_count // WIN, WIN, column_count // WIN, WIN) + trailing)
    windowed = jnp.moveaxis(windowed, 2, 1)
    return windowed.reshape((row_count // WIN, column_count // WIN, WIN * WIN) + trailing)


def from_windows(windowed, row_count, column_count):
    trailing = windowed.shape[3:]
    values = windowed.reshape((row_count // WIN, column_count // WIN, WIN, WIN) + trailing)
    values = jnp.moveaxis(values, 1, 2)
    return values.reshape((row_count, column_count) + trailing)


def local_attention(window_grid, key_valid, region, table_here, bias_index):
    row_count, column_count = key_valid.shape
    window_count = row_count // WIN * (column_count // WIN)
    local_heads = table_here.shape[1]
    windowed = to_windows(window_grid).reshape(window_count, WIN * WIN, 3, local_heads, HD)
    bias_grid = jnp.transpose(table_here[bias_index], (2, 0, 1))
    attended = window_attention(
        windowed[:, :, 0],
        windowed[:, :, 1],
        windowed[:, :, 2],
        bias_grid,
        to_windows(region).reshape(window_count, WIN * WIN),
        to_windows(key_valid).reshape(window_count, WIN * WIN),
    )
    attended = attended.reshape(row_count // WIN, column_count // WIN, WIN * WIN, local_heads * HD)
    return from_windows(attended, row_count, column_count)


def shifted_region(page_map, sp_index, row_count, column_count, sp_count):
    total_rows = row_count * sp_count
    local_rows = jnp.arange(row_count, dtype=jnp.int32)[:, None]
    root_row = (sp_index * row_count + local_rows + SHIFT) % total_rows
    root_column = (jnp.arange(column_count, dtype=jnp.int32)[None, :] + SHIFT) % column_count
    flat_index = root_row // WIN * page_map.shape[1] + root_column // WIN
    page = jnp.take(page_map.reshape(-1), flat_index)
    wrap_row = (root_row < SHIFT).astype(jnp.int32)
    wrap_column = (root_column < SHIFT).astype(jnp.int32)
    return page * 4 + wrap_row * 2 + wrap_column


def branch_total(partial_value):
    return lax.psum(partial_value, "tp")


def input_total(partial_value):
    return lax.psum(partial_value, "tp")


def shards(
    patches,
    merge_gain,
    merge_shift,
    merge_weight,
    first_gain,
    first_shift,
    input_weight,
    input_bias,
    position_table,
    output_weight,
    output_bias,
    second_gain,
    second_shift,
    expand_weight,
    expand_bias,
    shrink_weight,
    shrink_bias,
    page_map,
    valid_flags,
    cotangent,
):
    row_count, column_count = valid_flags.shape
    tokens = row_count * column_count
    tp_index = lax.axis_index("tp")
    sp_index = lax.axis_index("sp")
    local_width = output_weight.shape[1]
    valid_float = valid_flags.astype(jnp.float32)
    valid_column = valid_float.reshape(tokens, 1)
    bias_index = relative_index()
    region_flat = jnp.zeros((row_count, column_count), jnp.int32)
    region_moved = shifted_region(page_map, sp_index, row_count, column_count, lax.axis_size("sp"))
    full_channels = 4 * C2
    quads = (
        patches.reshape(row_count, 2, column_count, 2, -1)
        .transpose(0, 2, 3, 1, 4)
        .reshape(tokens, 4, -1)
    )
    moments = lax.psum((jnp.sum(quads, axis=(1, 2)), jnp.sum(quads * quads, axis=(1, 2))), "tp")
    center_mean = moments[0] / full_channels
    inverse = lax.rsqrt(moments[1] / full_channels - center_mean * center_mean + epsilon)
    centered = (quads - center_mean[:, None, None]) * inverse[:, None, None]
    merged = centered * merge_gain + merge_shift
    field = branch_total(jnp.einsum("tkc,kcd->td", merged, merge_weight, precision=highest))
    stored = []
    square_list = []
    for block_index in range(2):
        shifted_block = block_index == 1
        normed = layer_norm(field, first_gain[block_index], first_shift[block_index])
        projected = jnp.einsum("td,dkf->tkf", normed, input_weight[block_index], precision=highest)
        bias_rows = jnp.stack(
            [
                input_bias[block_index, 0],
                jnp.zeros_like(input_bias[block_index, 0]),
                input_bias[block_index, 1],
            ]
        )
        window_grid = (projected + bias_rows).reshape(row_count, column_count, 3 * local_width)
        if shifted_block:
            top_rows = passed_along((window_grid[:SHIFT], valid_float[:SHIFT]), "sp", -1)
            window_grid = jnp.roll(
                jnp.concatenate([window_grid[SHIFT:], top_rows[0]], 0), -SHIFT, axis=1
            )
            key_valid = jnp.roll(
                jnp.concatenate([valid_float[SHIFT:], top_rows[1]], 0), -SHIFT, axis=1
            )
            region = region_moved
        else:
            key_valid = valid_float
            region = region_flat
        attended = local_attention(
            window_grid, key_valid, region, position_table[block_index], bias_index
        )
        if shifted_block:
            turned = jnp.roll(attended, SHIFT, axis=1)
            carried = passed_along(turned[row_count - SHIFT :], "sp", 1)
            attended = jnp.concatenate([carried, turned[: row_count - SHIFT]], 0)
        attended = attended.reshape(tokens, local_width)
        mixed_out = (
            branch_total(jnp.dot(attended, output_weight[block_index], precision=highest))
            + output_bias[block_index]
        )
        middle = field + mixed_out
        normed_two = layer_norm(middle, second_gain[block_index], second_shift[block_index])
        pre_act = (
            jnp.dot(normed_two, expand_weight[block_index], precision=highest)
            + expand_bias[block_index]
        )
        hidden = exact_gelu(pre_act)
        branch = (
            branch_total(jnp.dot(hidden, shrink_weight[block_index], precision=highest))
            + shrink_bias[block_index]
        )
        stored.append(
            (
                field,
                normed,
                window_grid,
                key_valid,
                region,
                attended,
                middle,
                normed_two,
                pre_act,
                hidden,
            )
        )
        square_list.append(jnp.sum(mixed_out * mixed_out * valid_column))
        square_list.append(jnp.sum(branch * branch * valid_column))
        field = middle + branch
    square_list.append(jnp.sum(field * field * valid_column))
    square_sums = jnp.stack(square_list)
    valid_count = jnp.sum(valid_float)
    output = lax.dynamic_slice_in_dim(
        field.reshape(row_count, column_count, C), tp_index * local_width, local_width, 2
    )

    def block_backward(block_index, grad_field):
        (
            field_in,
            normed,
            window_grid,
            key_valid,
            region,
            attended,
            middle,
            normed_two,
            pre_act,
            hidden,
        ) = stored[block_index]
        shrink_bias_g = jnp.sum(grad_field, axis=0)
        shrink_weight_g = jnp.dot(hidden.T, grad_field, precision=highest)
        grad_hidden = jnp.dot(grad_field, shrink_weight[block_index].T, precision=highest)
        grad_pre = jax.vjp(exact_gelu, pre_act)[1](grad_hidden)[0]
        expand_bias_g = jnp.sum(grad_pre, axis=0)
        expand_weight_g = jnp.dot(normed_two.T, grad_pre, precision=highest)
        grad_normed_two = input_total(
            jnp.dot(grad_pre, expand_weight[block_index].T, precision=highest)
        )
        pull_second = jax.vjp(
            layer_norm, middle, second_gain[block_index], second_shift[block_index]
        )[1]
        grad_inner, second_gain_g, second_shift_g = pull_second(grad_normed_two)
        grad_middle = grad_field + grad_inner
        output_bias_g = jnp.sum(grad_middle, axis=0)
        output_weight_g = jnp.dot(attended.T, grad_middle, precision=highest)
        grad_attended = jnp.dot(
            grad_middle, output_weight[block_index].T, precision=highest
        ).reshape(row_count, column_count, local_width)
        if block_index == 1:
            upper_rows = passed_along(grad_attended[:SHIFT], "sp", -1)
            grad_attended = jnp.roll(
                jnp.concatenate([grad_attended[SHIFT:], upper_rows], 0), -SHIFT, axis=1
            )

        def attend(grid_in, table_in):
            return local_attention(grid_in, key_valid, region, table_in, bias_index)

        pull_attention = jax.vjp(attend, window_grid, position_table[block_index])[1]
        grad_grid, table_g = pull_attention(grad_attended)
        if block_index == 1:
            turned = jnp.roll(grad_grid, SHIFT, axis=1)
            lower_rows = passed_along(turned[row_count - SHIFT :], "sp", 1)
            grad_grid = jnp.concatenate([lower_rows, turned[: row_count - SHIFT]], 0)
        grad_projected = grad_grid.reshape(tokens, 3, local_width)
        input_bias_g = jnp.stack(
            [jnp.sum(grad_projected[:, 0], axis=0), jnp.sum(grad_projected[:, 2], axis=0)]
        )
        input_weight_g = jnp.einsum("td,tkf->dkf", normed, grad_projected, precision=highest)
        grad_normed = input_total(
            jnp.einsum("tkf,dkf->td", grad_projected, input_weight[block_index], precision=highest)
        )
        pull_first = jax.vjp(
            layer_norm, field_in, first_gain[block_index], first_shift[block_index]
        )[1]
        grad_outer, first_gain_g, first_shift_g = pull_first(grad_normed)
        grads_here = (
            first_gain_g,
            first_shift_g,
            input_weight_g,
            input_bias_g,
            table_g,
            output_weight_g,
            output_bias_g,
            second_gain_g,
            second_shift_g,
            expand_weight_g,
            expand_bias_g,
            shrink_weight_g,
            shrink_bias_g,
        )
        return (grad_middle + grad_outer, grads_here)

    grad_field = lax.all_gather(cotangent, "tp", axis=2, tiled=True).reshape(tokens, C)
    grad_field, late_grads = block_backward(1, grad_field)
    grad_field, early_grads = block_backward(0, grad_field)
    merge_weight_g = jnp.einsum("tkc,td->kcd", merged, grad_field, precision=highest)
    grad_merged = jnp.einsum("td,kcd->tkc", grad_field, merge_weight, precision=highest)
    merge_gain_g = jnp.sum(grad_merged * centered, axis=0)
    merge_shift_g = jnp.sum(grad_merged, axis=0)
    grad_hat = grad_merged * merge_gain
    back_moments = lax.psum(
        (jnp.sum(grad_hat, axis=(1, 2)), jnp.sum(grad_hat * centered, axis=(1, 2))), "tp"
    )
    grad_quads = inverse[:, None, None] * (
        grad_hat
        - back_moments[0][:, None, None] / full_channels
        - centered * back_moments[1][:, None, None] / full_channels
    )
    patches_grad = (
        grad_quads.reshape(row_count, column_count, 2, 2, -1)
        .transpose(0, 3, 1, 2, 4)
        .reshape(2 * row_count, 2 * column_count, -1)
    )
    whole_total = lax.psum(
        (
            early_grads[0],
            early_grads[1],
            early_grads[2],
            early_grads[3],
            early_grads[4],
            early_grads[5],
            early_grads[6],
            early_grads[7],
            early_grads[8],
            early_grads[9],
            early_grads[10],
            early_grads[11],
            early_grads[12],
            late_grads[0],
            late_grads[1],
            late_grads[2],
            late_grads[3],
            late_grads[4],
            late_grads[5],
            late_grads[6],
            late_grads[7],
            late_grads[8],
            late_grads[9],
            late_grads[10],
            late_grads[11],
            late_grads[12],
            merge_gain_g,
            merge_shift_g,
            merge_weight_g,
            square_sums,
            valid_count,
        ),
        "sp",
    )
    early_grads = whole_total[:13]
    late_grads = whole_total[13:26]
    merge_gain_g = whole_total[26]
    merge_shift_g = whole_total[27]
    merge_weight_g = whole_total[28]
    square_sums = whole_total[29]
    valid_count = whole_total[30]
    stacked = [jnp.stack([early_grads[position], late_grads[position]]) for position in range(13)]
    rms = jnp.sqrt(square_sums / (valid_count * C))
    return (
        output,
        patches_grad,
        merge_gain_g,
        merge_shift_g,
        merge_weight_g,
        stacked[0],
        stacked[1],
        stacked[2],
        stacked[3],
        stacked[4],
        stacked[5],
        stacked[6],
        stacked[7],
        stacked[8],
        stacked[9],
        stacked[10],
        stacked[11],
        stacked[12],
        rms,
    )


def solution(mesh):
    placed = (
        P("sp", None, "tp"),
        P(None, "tp"),
        P(None, "tp"),
        P(None, "tp", None),
        P(),
        P(),
        P(None, None, None, "tp"),
        P(None, None, "tp"),
        P(None, None, "tp"),
        P(None, "tp", None),
        P(),
        P(),
        P(),
        P(None, None, "tp"),
        P(None, "tp"),
        P(None, "tp", None),
        P(),
        P(),
        P("sp", None),
        P("sp", None, "tp"),
    )
    return jax.shard_map(
        shards,
        mesh=mesh,
        in_specs=placed,
        out_specs=(
            P("sp", None, "tp"),
            P("sp", None, "tp"),
            P(None, "tp"),
            P(None, "tp"),
            P(None, "tp", None),
            P(),
            P(),
            P(None, None, None, "tp"),
            P(None, None, "tp"),
            P(None, None, "tp"),
            P(None, "tp", None),
            P(),
            P(),
            P(),
            P(None, None, "tp"),
            P(None, "tp"),
            P(None, "tp", None),
            P(),
            P(),
        ),
        check_vma=False,
    )
```

profile of v0, /device:TPU:0, one launch (start us, length us, event | category | flops | bytes accessed | tf_op | source)
XLA Modules:
  0.0 1262.3 jit_solution(3288617347281952883)
XLA Ops:
  8.6 6.0 collective-permute-start.1
  16.5 6.9 fusion.220
  29.1 10.6 all-reduce.9
  47.4 7.3 gather_fusion.1
  56.2 19.6 %gather_fusion = f32[10000,4]{1,0:T(8,128)} fusion(f32[361,4]{1,0:T(8,128)S(1)} %bitcast.327, s32[10240]{0:T(1024)S(1)} %pad_clamp_fusion), kind=kCustom, calls=%fused_computation | custom fusion | bytes 360000 | tf_op jit(solution)/shard_map/gather | solution.py:78
  82.7 16.0 %all-reduce.21.cloned.1.call-done = f32[1200,512]{1,0:T(8,128)} async-done(((f32[1200,512]{1,0:T(8,128)}), f32[1200,512]{1,0:T(8,128)}) %all-reduce.21.cloned.1.call-update) | async-done | bytes 2457616 | tf_op jit(solution)/shard_map/psum | solution.py:104
  117.2 6.9 reshape_reshape.21
  124.1 7.1 fusion.234
  138.7 5.9 fusion.246
  161.8 54.7 %all-reduce.23.cloned.1.call-done = f32[1200,512]{1,0:T(8,128)} async-done(((f32[1200,512]{1,0:T(8,128)}), f32[1200,512]{1,0:T(8,128)}) %all-reduce.23.cloned.1.call-update) | async-done | bytes 2457616 | tf_op jit(solution)/shard_map/psum | solution.py:104
  220.8 9.4 fusion
  232.6 5.8 fusion.120
  239.7 56.2 %all-reduce.25.cloned.1.call-done = f32[1200,512]{1,0:T(8,128)} async-done(((f32[1200,512]{1,0:T(8,128)}), f32[1200,512]{1,0:T(8,128)}) %all-reduce.25.cloned.1.call-update) | async-done | bytes 2457616 | tf_op jit(solution)/shard_map/psum | solution.py:104
  313.9 19.6 %gather_fusion.2 = f32[10000,4]{1,0:T(8,128)} fusion(f32[361,4]{1,0:T(8,128)S(1)} %bitcast.326, s32[10240]{0:T(1024)S(1)} %pad_clamp_fusion), kind=kCustom, calls=%fused_computation.2 | custom fusion | bytes 360000 | tf_op jit(solution)/shard_map/gather | solution.py:78
  353.2 6.8 reshape_reshape.24
  360.0 6.3 fusion.233
  375.3 5.9 fusion.247
  398.7 11.3 collective-permute-done.2
  416.4 53.2 %all-reduce.27.cloned.1.call-done = f32[1200,512]{1,0:T(8,128)} async-done(((f32[1200,512]{1,0:T(8,128)}), f32[1200,512]{1,0:T(8,128)}) %all-reduce.27.cloned.1.call-update) | async-done | bytes 2457616 | tf_op jit(solution)/shard_map/psum | solution.py:104
  474.8 11.0 fusion.1
  485.9 10.1 all-gather.2.cloned.1.call-done
  496.0 9.2 fusion.248
  512.6 57.1 %all-reduce.29.cloned.1.call-done = f32[1200,512]{1,0:T(8,128)} async-done(((f32[1200,512]{1,0:T(8,128)}), f32[1200,512]{1,0:T(8,128)}) %all-reduce.29.cloned.1.call-update) | async-done | bytes 2457616 | tf_op jit(solution)/shard_map/psum | solution.py:108
  583.6 5.8 collective-permute-done.3
  601.3 6.2 convolution_bitcast_fusion.7
  623.6 7.1 copy.141
  630.6 7.3 reshape.689
  648.1 24.0 %collective-permute-done.4 = f32[5,120,384]{2,1,0:T(8,128)S(1)} collective-permute-done((f32[5,120,384]{2,1,0:T(8,128)S(1)}, f32[5,120,384]{2,1,0:T(8,128)S(1)}, u32[]{:S(2)}, u32[]{:S(2)}) %collective-permute-start.4) | collective-permute-done | bytes 921632 | tf_op jit(solution)/shard_map/ppermute | solution.py:21
  677.5 7.4 convolution_bitcast_fusion.2
  685.2 55.1 %all-reduce.31.cloned.1.call-done = f32[1200,512]{1,0:T(8,128)} async-done(((f32[1200,512]{1,0:T(8,128)}), f32[1200,512]{1,0:T(8,128)}) %all-reduce.31.cloned.1.call-update) | async-done | bytes 2457616 | tf_op jit(solution)/shard_map/psum | solution.py:108
  763.7 8.3 fusion.111
  772.0 48.1 %all-reduce.33.cloned.1.call-done = f32[1200,512]{1,0:T(8,128)} async-done(((f32[1200,512]{1,0:T(8,128)}), f32[1200,512]{1,0:T(8,128)}) %all-reduce.33.cloned.1.call-update) | async-done | bytes 2457616 | tf_op jit(solution)/shard_map/psum | solution.py:108
  844.6 6.2 convolution_bitcast_fusion.6
  866.9 7.1 copy.150
  874.0 7.3 reshape.694
  889.4 7.4 convolution_bitcast_fusion.1
  897.6 8.4 fusion.49
  906.0 7.4 convolution_bitcast_fusion.3
  915.9 6.0 fusion.56
  921.9 5.9 fusion.50
  936.1 5.8 fusion.51
  942.0 52.5 %all-reduce.37.cloned.1.call-done = (f32[1200,512]{1,0:T(8,128)}, f32[1200,512]{1,0:T(8,128)}) async-done(((f32[1200,512]{1,0:T(8,128)}, f32[1200,512]{1,0:T(8,128)}), (f32[1200,512]{1,0:T(8,128)}, f32[1200,512]{1,0:T(8,128)})) %all-reduce.37.cloned.1.call-update) | async-done | bytes 4915216 | tf_op jit(solution)/shard_map/psum | solution.py:104
  1016.9 56.0 %scatter_custom_fusion.1 = f32[361,4]{1,0:T(8,128)} fusion(s32[10000]{0:T(1024)} %copy-done.91, f32[10000,4]{1,0:T(8,128)} %copy.159, f32[]{:T(128)} %constant.64.clone.1), kind=kCustom, calls=%fused_computation.286 | custom fusion | flops 40000 | bytes 6288 | tf_op jit(solution)/shard_map/transpose(jvp())/scatter-add | solution.py:78
  1082.9 55.5 %scatter_custom_fusion = f32[361,4]{1,0:T(8,128)S(1)} fusion(s32[10000]{0:T(1024)} %copy-done.91, f32[10000,4]{1,0:T(8,128)} %copy.157, f32[]{:T(128)} %constant.64.clone.1), kind=kCustom, calls=%fused_computation.288 | custom fusion | flops 40000 | bytes 6288 | tf_op jit(solution)/shard_map/transpose(jvp())/scatter-add | solution.py:78
  1142.2 7.0 multiply_reduce_fusion.2
  1152.7 6.0 multiply_reduce_fusion.20
  1158.8 51.2 %all-reduce.6 = (f32[4,64]{1,0:T(4,128)}, f32[4,64]{1,0:T(4,128)}, f32[1,512]{1,0:T(1,128)S(1)}, f32[1,512]{1,0:T(1,128)S(1)}, f32[1,512]{1,0:T(1,128)S(1)}, /*i...) all-reduce(f32[4,64]{1,0:T(4,128)S(1)} %get-tuple-element.65, ...), channel_id=1, replica_groups=mesh['sp'=8,'tp'=4] {'sp'}, use_global_device_ids=true, to_apply=%region_44.45 | all-reduce | flops 11086 | bytes 88688 | tf_op jit(solution)/shard_map/psum | solution.py:325
  1210.2 11.0 all-reduce.8
  (612 shorter events, 371.9 us)
Async XLA Ops:
  7.2 33.1 %copy-start = (f32[4,64,512]{2,1,0:T(8,128)S(1)}, f32[4,64,512]{2,1,0:T(8,128)}, u32[]{:S(2)}) copy-start(f32[4,64,512]{2,1,0:T(8,128)} %param.23) | copy-start | bytes 1572868
  7.2 91.4 %all-reduce.21.cloned.1.call-start = ((), (), s32[]{:S(2)}) async-start(), calls=%async_computation | async-start | bytes 4915200 | tf_op jit(solution)/shard_map/psum | solution.py:104
  8.6 71.9 %collective-permute-start.1 = (f32[5,120]{1,0:T(8,128)S(1)}, f32[5,120]{1,0:T(8,128)S(1)}, u32[]{:S(2)}, u32[]{:S(2)}) collective-permute-start(f32[5,120]{1,0:T(8,128)S(1)} %get-tuple-element.167), channel_id=1, source_target_pairs={{4,0},{8,4},{12,8},{16,12},{20,16},{24,20},{28,24},{0,28},{5,1},{9... | collective-permute-start | bytes 7208 | tf_op jit(solution)/shard_map/ppermute | solution.py:21
  26.8 13.5 %copy-start.117 = (f32[4,64]{1,0:T(4,128)S(1)}, f32[4,64]{1,0:T(4,128)}, u32[]{:S(2)}) copy-start(f32[4,64]{1,0:T(4,128)} %param.21) | copy-start | bytes 3076
  26.8 13.5 %copy-start.173 = (f32[4,64]{1,0:T(4,128)S(1)}, f32[4,64]{1,0:T(4,128)}, u32[]{:S(2)}) copy-start(f32[4,64]{1,0:T(4,128)} %param.22) | copy-start | bytes 3076
  28.9 15.5 %copy-start.18 = (f32[1200,4,64]{0,2,1:T(8,128)}, f32[1200,4,64]{0,2,1:T(8,128)S(1)}, u32[]{:S(2)}) copy-start(f32[1200,4,64]{0,2,1:T(8,128)S(1)} %reshape.680) | copy-start | bytes 3686404
  44.4 172.0 %all-reduce.23.cloned.1.call-start = ((), (), s32[]{:S(2)}) async-start(), calls=%async_computation.1 | async-start | bytes 4915200 | tf_op jit(solution)/shard_map/psum | solution.py:104
  45.8 55.8 %copy-start.133 = (f32[1,512]{1,0:T(1,128)}, f32[1,512]{1,0:T(1,128)S(1)}, u32[]{:S(2)}) copy-start(f32[1,512]{1,0:T(1,128)S(1)} %get-tuple-element.181) | copy-start | bytes 6148
  46.4 55.2 %copy-start.177 = (f32[1,512]{1,0:T(1,128)}, f32[1,512]{1,0:T(1,128)S(1)}, u32[]{:S(2)}) copy-start(f32[1,512]{1,0:T(1,128)S(1)} %get-tuple-element.183) | copy-start | bytes 6148
  158.9 137.0 %all-reduce.25.cloned.1.call-start = ((), (), s32[]{:S(2)}) async-start(), calls=%async_computation.2 | async-start | bytes 4915200 | tf_op jit(solution)/shard_map/psum | solution.py:104
  160.0 59.2 %copy-start.145 = (f32[1,512]{1,0:T(1,128)}, f32[1,512]{1,0:T(1,128)S(1)}, u32[]{:S(2)}) copy-start(f32[1,512]{1,0:T(1,128)S(1)} %get-tuple-element.179) | copy-start | bytes 6148
  160.6 59.2 %copy-start.138 = (f32[1,512]{1,0:T(1,128)}, f32[1,512]{1,0:T(1,128)S(1)}, u32[]{:S(2)}) copy-start(f32[1,512]{1,0:T(1,128)S(1)} %get-tuple-element.173) | copy-start | bytes 6148
  161.2 58.6 %copy-start.181 = (f32[1,512]{1,0:T(1,128)}, f32[1,512]{1,0:T(1,128)S(1)}, u32[]{:S(2)}) copy-start(f32[1,512]{1,0:T(1,128)S(1)} %get-tuple-element.175) | copy-start | bytes 6148
  219.2 11.0 copy-start.94
  219.7 10.5 copy-start.107
  219.8 10.5 copy-start.121
  220.8 11.8 copy-start.44
  238.4 231.1 %all-reduce.27.cloned.1.call-start = ((), (), s32[]{:S(2)}) async-start(), calls=%async_computation.3 | async-start | bytes 4915200 | tf_op jit(solution)/shard_map/psum | solution.py:104
  239.7 58.3 %copy-start.147 = (f32[1,512]{1,0:T(1,128)}, f32[1,512]{1,0:T(1,128)S(1)}, u32[]{:S(2)}) copy-start(f32[1,512]{1,0:T(1,128)S(1)} %get-tuple-element.171) | copy-start | bytes 6148
  309.5 34.0 %collective-permute-start = (f32[5,120,384]{2,1,0:T(8,128)}, f32[5,120,384]{2,1,0:T(8,128)}, u32[]{:S(2)}, u32[]{:S(2)}) collective-permute-start(f32[5,120,384]{2,1,0:T(8,128)} %slice.241), channel_id=1, source_target_pairs={{4,0},{8,4},{12,8},{16,12},{20,16},{24,20},{28,24},{0,28},{5,1},{9... | collective-permute-start | bytes 2764808 | tf_op jit(solution)/shard_map/ppermute | solution.py:21
  394.7 17.2 %copy-start.55 = (f32[2,128,512]{2,1,0:T(8,128)S(1)}, f32[2,128,512]{2,1,0:T(8,128)}, u32[]{:S(2)}) copy-start(f32[2,128,512]{2,1,0:T(8,128)} %param.29) | copy-start | bytes 1572868
  398.7 11.4 collective-permute-start.2
  415.6 80.4 %all-gather.2.cloned.1.call-start = ((), (), s32[]{:S(2)}) async-start(), calls=%async_computation.4 | async-start | bytes 3072000 | tf_op jit(solution)/shard_map/all_gather | solution.py:304
  416.2 153.5 %all-reduce.29.cloned.1.call-start = ((), (), s32[]{:S(2)}) async-start(), calls=%async_computation.5 | async-start | bytes 4915200 | tf_op jit(solution)/shard_map/psum | solution.py:108
  496.0 10.7 copy-start.58
  512.3 227.9 %all-reduce.31.cloned.1.call-start = ((), (), s32[]{:S(2)}) async-start(), calls=%async_computation.6 | async-start | bytes 4915200 | tf_op jit(solution)/shard_map/psum | solution.py:108
  576.5 12.9 %copy-start.10 = (f32[1200,512]{1,0:T(8,128)}, f32[1200,512]{1,0:T(8,128)S(1)}, u32[]{:S(2)}) copy-start(f32[1200,512]{1,0:T(8,128)S(1)} %get-tuple-element.127) | copy-start | bytes 7372804
  578.7 10.7 collective-permute-start.3
  645.1 27.0 %copy-start.32 = (f32[10,120,384]{2,1,0:T(8,128)S(1)}, f32[10,120,384]{2,1,0:T(8,128)}, u32[]{:S(2)}) copy-start(f32[10,120,384]{2,1,0:T(8,128)} %reshape.690) | copy-start | bytes 5529604
  647.4 24.7 %collective-permute-start.4 = (f32[5,120,384]{2,1,0:T(8,128)S(1)}, f32[5,120,384]{2,1,0:T(8,128)S(1)}, u32[]{:S(2)}, u32[]{:S(2)}) collective-permute-start(f32[5,120,384]{2,1,0:T(8,128)S(1)} %fusion.135), channel_id=1, source_target_pairs={{28,0},{0,4},{4,8},{8,12},{12,16},{16,20},{20,24},{24,28},{29,1},{... | collective-permute-start | bytes 2764808 | tf_op jit(solution)/shard_map/ppermute | solution.py:21
  684.9 55.4 %copy-start.97 = (f32[1200]{0:T(1024)S(1)}, f32[1200]{0:T(1024)}, u32[]{:S(2)}) copy-start(f32[1200]{0:T(1024)} %copy-done.96) | copy-start | bytes 14404
  684.9 55.4 %copy-start.125 = (f32[1200]{0:T(1024)S(1)}, f32[1200]{0:T(1024)}, u32[]{:S(2)}) copy-start(f32[1200]{0:T(1024)} %copy-done.124) | copy-start | bytes 14404
  684.9 59.5 %copy-start.110 = (f32[1200]{0:T(1024)S(1)}, f32[1200]{0:T(1024)}, u32[]{:S(2)}) copy-start(f32[1200]{0:T(1024)} %copy-done.109) | copy-start | bytes 14404
  684.9 135.2 %all-reduce.33.cloned.1.call-start = ((), (), s32[]{:S(2)}) async-start(), calls=%async_computation.7 | async-start | bytes 4915200 | tf_op jit(solution)/shard_map/psum | solution.py:108
  747.0 8.6 copy-start.13
  762.6 231.9 %all-reduce.37.cloned.1.call-start = ((), (), s32[]{:S(2)}) async-start(), calls=%async_computation.9 | async-start | bytes 9830400 | tf_op jit(solution)/shard_map/psum | solution.py:104
  763.7 56.4 %copy-start.95 = (f32[1200]{0:T(1024)S(1)}, f32[1200]{0:T(1024)}, u32[]{:S(2)}) copy-start(f32[1200]{0:T(1024)} %copy-done.94) | copy-start | bytes 14404
  772.0 51.5 %copy-start.108 = (f32[1200]{0:T(1024)S(1)}, f32[1200]{0:T(1024)}, u32[]{:S(2)}) copy-start(f32[1200]{0:T(1024)} %copy-done.107) | copy-start | bytes 14404
  896.9 349.2 %all-reduce.35.cloned.1.call-start = ((), (), s32[]{:S(2)}) async-start(), calls=%async_computation.8 | async-start | bytes 13631488 | tf_op jit(solution)/shard_map/psum | solution.py:325
  897.5 8.4 copy-start.17
  897.5 8.4 copy-start.30
  906.0 9.8 copy-start.33
  915.9 11.9 copy-start.29
  1013.5 63.1 %copy-start.104 = (f32[6,8,100]{2,1,0:T(8,128)S(1)}, f32[6,8,100]{2,1,0:T(8,128)}, u32[]{:S(2)}) copy-start(f32[6,8,100]{2,1,0:T(8,128)} %copy-done.103) | copy-start | bytes 57604
  1079.4 62.8 %copy-start.144 = (f32[1,512]{1,0:T(1,128)S(1)}, f32[1,512]{1,0:T(1,128)}, u32[]{:S(2)}) copy-start(f32[1,512]{1,0:T(1,128)} %get-tuple-element.178) | copy-start | bytes 6148
  1079.5 62.7 %copy-start.146 = (f32[1,512]{1,0:T(1,128)S(1)}, f32[1,512]{1,0:T(1,128)}, u32[]{:S(2)}) copy-start(f32[1,512]{1,0:T(1,128)} %copy-done.145) | copy-start | bytes 6148
  1079.5 62.7 %copy-start.148 = (f32[1,512]{1,0:T(1,128)S(1)}, f32[1,512]{1,0:T(1,128)}, u32[]{:S(2)}) copy-start(f32[1,512]{1,0:T(1,128)} %copy-done.147) | copy-start | bytes 6148
  1079.5 62.7 %copy-start.164 = (f32[1,512]{1,0:T(1,128)S(1)}, f32[1,512]{1,0:T(1,128)}, u32[]{:S(2)}) copy-start(f32[1,512]{1,0:T(1,128)} %get-tuple-element.170) | copy-start | bytes 6148
  (153 other events, 597.6 us)
Sparse Core Ops, SparseCore 0:
  44.5 54.0 all-reduce.20
  159.1 57.3 all-reduce.22
  238.6 57.3 all-reduce.24
  415.7 53.8 all-reduce.26
  470.9 25.0 all-gather.1
  512.4 57.2 all-reduce.28
  685.0 55.1 all-reduce.30
  762.7 57.3 all-reduce.32
  897.0 97.4 all-reduce.36
  1005.2 240.7 all-reduce.34
where the time goes:
time: 1270 us; the launch traced here: 1260 us
  waiting for transfers between devices  451 us (36%)
  local copies, waits for them, and re-layouts  279 us (22%)
  matrix products  214 us (17%)
  other arithmetic  211 us (17%)
  blocking collectives  72.8 us (6%)
  starting transfers between devices  17.9 us (1%)
  between operations  17.3 us (1%)
    psum x5, waiting for transfers between devices, branch_total(): return lax.psum(partial_value, 'tp')  233 us
    psum x3, waiting for transfers between devices, input_total(): return lax.psum(partial_value, 'tp')  160 us
    scatter-add x2, other arithmetic, local_attention(): bias_grid = jnp.transpose(table_here[bias_index], (2, 0, 1))  112 us
    psum x1, blocking collectives, shards(): lax.psum((early_grads[0], early_grads[1], early_grads[2], early_grads[3],...  51.2 us
    unnamed x384, local copies, waits for them, and re-layouts  47.3 us
    gather x6, local copies, waits for them, and re-layouts, local_attention(): bias_grid = jnp.transpose(table_here[bias_index], (2, 0, 1))  46.7 us
    ppermute x5, waiting for transfers between devices, passed_along(): return lax.ppermute(block, axis, route)  41.2 us
    dot_general x6, matrix products, window_attention(): return jnp.einsum('whqk,wkhd->wqhd', weights, value_rows, precision=highest)  29.6 us
  transfers between devices with their start and end apart: 15, of which 13 were waited for; matrix products, arithmetic and copies ran while one was open for 26% of the time, Pallas kernels for 0%

commit v1 on v0

v1 whole, which is shorter than its diff:
```python
import functools

import jax
import jax.numpy as jnp
import numpy as np
from jax import lax
from jax.experimental import pallas as pl
from jax.experimental.pallas import tpu as pltpu
from jax.sharding import PartitionSpec as P

C = 512
HD = 32
C2 = 256
WIN = 10
SHIFT = 5
SUB = 32
REAL = 25
WT = 128
TOK = 384
NW = 3
GROUP = 4

bf16 = jnp.bfloat16
f32 = jnp.float32
epsilon = 1e-05
masked = -1000000000.0

NN = (((1,), (0,)), ((), ()))
NT = (((1,), (1,)), ((), ()))
TN = (((0,), (0,)), ((), ()))


def split(x):
    high = x.astype(bf16)
    return high, (x - high.astype(f32)).astype(bf16)


def mm(a, b, dims):
    return lax.dot_general(a, b, dims, preferred_element_type=f32)


def mm3(a, b, dims):
    return mm(a[0], b[0], dims) + (mm(a[0], b[1], dims) + mm(a[1], b[0], dims))


def normalized(x):
    center = x - jnp.mean(x, axis=-1, keepdims=True)
    rho = lax.rsqrt(jnp.mean(center * center, axis=-1, keepdims=True) + epsilon)
    return center * rho, rho


def head_masks(dtype):
    lane = lax.broadcasted_iota(jnp.int32, (1, 128), 1) // HD
    return [(lane == h).astype(f32).astype(dtype) for h in range(GROUP)]


def stacked(pair, masks):
    return tuple(jnp.concatenate([part * m for m in masks], axis=0) for part in pair)


def side_by_side(pair):
    return tuple(
        jnp.concatenate([part[h * WT : (h + 1) * WT] for h in range(GROUP)], axis=1)
        for part in pair
    )


def colsum(x):
    return jnp.sum(x, axis=0, keepdims=True)


def attn_fwd_kernel(
    field_ref, gain_ref, shift_ref, wqkv_ref, bqkv_ref, wo_ref, bo_ref, bias_ref,
    regc_ref, regr_ref, valr_ref, valc_ref,
    middle_ref, qkv_ref, p_ref, att_ref, sq_ref,
    nh, nl, mixed,
):
    g = pl.program_id(0)

    @pl.when(g == 0)
    def _():
        xhat, _ = normalized(field_ref[...])
        nh[...], nl[...] = split(xhat * gain_ref[...] + shift_ref[...])
        mixed[...] = jnp.broadcast_to(bo_ref[...], mixed.shape)

    w = jnp.concatenate([wqkv_ref[0, j] for j in range(3)], axis=1)
    qkv = mm3((nh[...], nl[...]), split(w), NN) + bqkv_ref[0]
    lane = lax.broadcasted_iota(jnp.int32, (1, 3 * 128), 1)
    qkv = qkv * jnp.where(lane < 128, HD ** (-0.5), 1.0)
    qkv_ref[0] = qkv
    masks = head_masks(bf16)
    bias = bias_ref[...].reshape(GROUP * WT, WT)
    eye = lax.broadcasted_iota(jnp.int32, (WT, WT), 0) == lax.broadcasted_iota(jnp.int32, (WT, WT), 1)
    for i in range(NW):
        rows = pl.ds(i * WT, WT)
        here = qkv_ref[0, rows, :]
        q4 = stacked(split(here[:, :128]), masks)
        k = split(here[:, 128:256])
        v4 = stacked(split(here[:, 256:]), masks)
        allowed = (regc_ref[rows, :] == regr_ref[i]) & (valr_ref[i] > 0) | eye
        allowed = jnp.concatenate([allowed.astype(f32)] * GROUP, axis=0) > 0
        s = jnp.where(allowed, mm3(q4, k, NT) + bias, masked)
        e = jnp.exp(s - jnp.max(s, axis=-1, keepdims=True))
        p = e / jnp.sum(e, axis=-1, keepdims=True)
        p_ref[0, i] = p
        att_ref[0, rows, :] = mm3(side_by_side(split(p)), v4, NN)
    mixed[...] += mm3(split(att_ref[0]), split(wo_ref[0]), NN)

    @pl.when(g == GROUP - 1)
    def _():
        middle_ref[...] = field_ref[...] + mixed[...]
        sq_ref[...] = colsum(mixed[...] * mixed[...] * valc_ref[...])


def whole(shape):
    return pl.BlockSpec(shape, lambda g: (0,) * len(shape))


def part(shape):
    return pl.BlockSpec((1,) + shape, lambda g: (g,) + (0,) * len(shape))


def sds(*shape):
    return jax.ShapeDtypeStruct(shape, f32)


BIG = pltpu.CompilerParams(vmem_limit_bytes=56 << 20)


def attn_fwd(field, gain, shift, wqkv, bqkv, wo, bo, bias, masks):
    regc, regr, valr, valc = masks
    return pl.pallas_call(
        attn_fwd_kernel,
        grid=(4,),
        in_specs=[
            whole((TOK, C)), whole((1, C)), whole((1, C)), part((3, C, 128)), part((1, 384)),
            part((128, C)), whole((1, C)), pl.BlockSpec((GROUP, WT, WT), lambda g: (g, 0, 0)),
            whole((TOK, 1)), whole((NW, 1, WT)), whole((NW, 1, WT)), whole((TOK, 1)),
        ],
        out_specs=[
            whole((TOK, C)), part((TOK, 384)), part((NW, GROUP * WT, WT)), part((TOK, 128)),
            whole((1, C)),
        ],
        out_shape=[
            sds(TOK, C), sds(4, TOK, 384), sds(4, NW, GROUP * WT, WT), sds(4, TOK, 128), sds(1, C),
        ],
        scratch_shapes=[pltpu.VMEM((TOK, C), bf16), pltpu.VMEM((TOK, C), bf16), pltpu.VMEM((TOK, C), f32)],
        compiler_params=BIG,
        name="attn_fwd",
    )(field, gain, shift, wqkv, bqkv, wo, bo, bias, regc, regr, valr, valc)


def mlp_fwd_kernel(
    mid_ref, gain_ref, shift_ref, we_ref, be_ref, ws_ref, bs_ref, valc_ref,
    out_ref, hid_ref, slope_ref, sq_ref, sqo_ref,
    nh, nl, branch,
):
    g = pl.program_id(0)

    @pl.when(g == 0)
    def _():
        xhat, _ = normalized(mid_ref[...])
        nh[...], nl[...] = split(xhat * gain_ref[...] + shift_ref[...])
        branch[...] = jnp.broadcast_to(bs_ref[...], branch.shape)

    pre = mm3((nh[...], nl[...]), split(we_ref[0]), NN) + be_ref[0]
    phi = 0.5 * (1.0 + lax.erf(pre * (2 ** -0.5)))
    hidden = pre * phi
    hid_ref[0] = hidden
    slope_ref[0] = phi + pre * (jnp.exp(-0.5 * pre * pre) * ((2 * np.pi) ** -0.5))
    branch[...] += mm3(split(hidden), split(ws_ref[0]), NN)

    @pl.when(g == 3)
    def _():
        out = mid_ref[...] + branch[...]
        out_ref[...] = out
        sq_ref[...] = colsum(branch[...] * branch[...] * valc_ref[...])
        sqo_ref[...] = colsum(out * out * valc_ref[...])


def mlp_fwd(mid, gain, shift, we, be, ws, bs, valc):
    return pl.pallas_call(
        mlp_fwd_kernel,
        grid=(4,),
        in_specs=[
            whole((TOK, C)), whole((1, C)), whole((1, C)), part((C, 512)), part((1, 512)),
            part((512, C)), whole((1, C)), whole((TOK, 1)),
        ],
        out_specs=[whole((TOK, C)), part((TOK, 512)), part((TOK, 512)), whole((1, C)), whole((1, C))],
        out_shape=[sds(TOK, C), sds(4, TOK, 512), sds(4, TOK, 512), sds(1, C), sds(1, C)],
        scratch_shapes=[pltpu.VMEM((TOK, C), bf16), pltpu.VMEM((TOK, C), bf16), pltpu.VMEM((TOK, C), f32)],
        compiler_params=BIG,
        name="mlp_fwd",
    )(mid, gain, shift, we, be, ws, bs, valc)


def norm_back(x, gain, grad_y):
    xhat, rho = normalized(x)
    gh = grad_y * gain
    grad_x = rho * (
        gh - jnp.mean(gh, axis=-1, keepdims=True) - xhat * jnp.mean(gh * xhat, axis=-1, keepdims=True)
    )
    return grad_x, colsum(grad_y * xhat), colsum(grad_y)


def mlp_bwd_kernel(
    gf_ref, mid_ref, gain_ref, shift_ref, we_ref, ws_ref, hid_ref, slope_ref,
    gm_ref, pack_ref, dbe_ref, small_ref,
    nth, ntl, gh, gl, acc,
):
    g = pl.program_id(0)

    @pl.when(g == 0)
    def _():
        xhat, _ = normalized(mid_ref[...])
        nth[...], ntl[...] = split((xhat * gain_ref[...] + shift_ref[...]).T)
        gh[...], gl[...] = split(gf_ref[...])
        acc[...] = jnp.zeros_like(acc)

    grad = (gh[...], gl[...])
    dws = mm3(split(hid_ref[0].T), grad, NN)
    for j in range(4):
        pack_ref[0, 2048 + j * 512 : 2560 + j * 512, :] = dws[:, j * 128 : (j + 1) * 128]
    dpre = mm3(grad, split(ws_ref[0]), NT) * slope_ref[0]
    dbe_ref[0] = colsum(dpre)
    pair = split(dpre)
    dwe = mm3((nth[...], ntl[...]), pair, NN)
    for j in range(4):
        pack_ref[0, j * 512 : (j + 1) * 512, :] = dwe[:, j * 128 : (j + 1) * 128]
    acc[...] += mm3(pair, split(we_ref[0]), NT)

    @pl.when(g == 3)
    def _():
        grad_x, dgain, dshift = norm_back(mid_ref[...], gain_ref[...], acc[...])
        gm_ref[...] = gf_ref[...] + grad_x
        small_ref[0:1, :] = dgain
        small_ref[1:2, :] = dshift
        small_ref[2:3, :] = colsum(gf_ref[...])
        small_ref[3:8, :] = jnp.zeros((5, C), f32)


def mlp_bwd(gf, mid, gain, shift, we, ws, hid, slope, pack, place):
    body, more, extra, alias = mlp_bwd_kernel, (), [], {}
    if pack is not None:
        body = lambda *refs: mlp_bwd_kernel(*refs[:8], *refs[9:])
        more, extra, alias = (pack,), [ANY], {8: 1}
    return pl.pallas_call(
        body,
        grid=(4,),
        in_specs=[
            whole((TOK, C)), whole((TOK, C)), whole((1, C)), whole((1, C)), part((C, 512)),
            part((512, C)), part((TOK, 512)), part((TOK, 512)),
        ] + extra,
        out_specs=[
            whole((TOK, C)), pl.BlockSpec((1, 4096, 128), lambda g: (g, place, 0)), part((1, 512)), whole((8, C)),
        ],
        out_shape=[sds(TOK, C), sds(4, 12288, 128), sds(4, 1, 512), sds(8, C)],
        input_output_aliases=alias,
        scratch_shapes=[
            pltpu.VMEM((C, TOK), bf16), pltpu.VMEM((C, TOK), bf16),
            pltpu.VMEM((TOK, C), bf16), pltpu.VMEM((TOK, C), bf16), pltpu.VMEM((TOK, C), f32),
        ],
        compiler_params=BIG,
        name="mlp_bwd",
    )(gf, mid, gain, shift, we, ws, hid, slope, *more)


def attn_bwd_kernel(
    gm_ref, field_ref, gain_ref, shift_ref, wqkv_ref, wo_ref, qkv_ref, p_ref, att_ref, _,
    gf_ref, pack_ref, dbqkv_ref, dbias_ref, small_ref,
    nth, ntl, mh, ml, acc, dqkv,
):
    g = pl.program_id(0)

    @pl.when(g == 0)
    def _():
        xhat, _ = normalized(field_ref[...])
        nth[...], ntl[...] = split((xhat * gain_ref[...] + shift_ref[...]).T)
        mh[...], ml[...] = split(gm_ref[...])
        acc[...] = jnp.zeros_like(acc)

    grad = (mh[...], ml[...])
    dwo = mm3(split(att_ref[0].T), grad, NN)
    for j in range(4):
        pack_ref[0, 1536 + j * 128 : 1664 + j * 128, :] = dwo[:, j * 128 : (j + 1) * 128]
    dout = mm3(grad, split(wo_ref[0]), NT)
    masks = head_masks(bf16)
    dbias = jnp.zeros((GROUP * WT, WT), f32)
    for i in range(NW):
        rows = slice(i * WT, (i + 1) * WT)
        here = qkv_ref[0, pl.ds(i * WT, WT), :]
        q4 = stacked(split(here[:, :128]), masks)
        k4 = stacked(split(here[:, 128:256]), masks)
        v = split(here[:, 256:])
        p = p_ref[0, i]
        do4 = stacked(split(dout[rows]), masks)
        dp = mm3(do4, v, NT)
        ds = p * (dp - jnp.sum(p * dp, axis=-1, keepdims=True))
        dbias = dbias + ds
        dpair = split(ds)
        dqkv[pl.ds(i * WT, WT), 0:128] = mm3(side_by_side(dpair), k4, NN) * HD ** (-0.5)
        dqkv[pl.ds(i * WT, WT), 128:256] = mm3(dpair, q4, TN)
        dqkv[pl.ds(i * WT, WT), 256:384] = mm3(split(p), do4, TN)
    dbias_ref[...] = dbias.reshape(GROUP, WT, WT)
    grads = dqkv[...]
    dbqkv_ref[0] = colsum(grads)
    pair = split(grads)
    dw = mm3((nth[...], ntl[...]), pair, NN)
    for j in range(3):
        pack_ref[0, j * 512 : (j + 1) * 512, :] = dw[:, j * 128 : (j + 1) * 128]
    w = jnp.concatenate([wqkv_ref[0, j] for j in range(3)], axis=1)
    acc[...] += mm3(pair, split(w), NT)

    @pl.when(g == GROUP - 1)
    def _():
        grad_x, dgain, dshift = norm_back(field_ref[...], gain_ref[...], acc[...])
        gf_ref[...] = gm_ref[...] + grad_x
        small_ref[0:1, :] = dgain
        small_ref[1:2, :] = dshift
        small_ref[2:3, :] = colsum(gm_ref[...])
        small_ref[3:8, :] = jnp.zeros((5, C), f32)


def attn_bwd(gm, field, gain, shift, wqkv, wo, qkv, p, att, pack, place):
    return pl.pallas_call(
        attn_bwd_kernel,
        grid=(4,),
        in_specs=[
            whole((TOK, C)), whole((TOK, C)), whole((1, C)), whole((1, C)), part((3, C, 128)),
            part((128, C)), part((TOK, 384)), part((NW, GROUP * WT, WT)), part((TOK, 128)), ANY,
        ],
        out_specs=[
            whole((TOK, C)), pl.BlockSpec((1, 2048, 128), lambda g: (g, place, 0)), part((1, 384)),
            pl.BlockSpec((GROUP, WT, WT), lambda g: (g, 0, 0)), whole((8, C)),
        ],
        out_shape=[sds(TOK, C), sds(4, 12288, 128), sds(4, 1, 384), sds(16, WT, WT), sds(8, C)],
        input_output_aliases={9: 1},
        scratch_shapes=[
            pltpu.VMEM((C, TOK), bf16), pltpu.VMEM((C, TOK), bf16),
            pltpu.VMEM((TOK, C), bf16), pltpu.VMEM((TOK, C), bf16),
            pltpu.VMEM((TOK, C), f32), pltpu.VMEM((TOK, 384), f32),
        ],
        compiler_params=BIG,
        name="attn_bwd",
    )(gm, field, gain, shift, wqkv, wo, qkv, p, att, pack)


MESH = pl.DeviceIdType.MESH
ANY = pl.BlockSpec(memory_space=pl.ANY)
VM = pl.BlockSpec(memory_space=pltpu.VMEM)


def here():
    sp, tp = lax.axis_index("sp"), lax.axis_index("tp")
    return sp, tp, (sp, tp ^ 1), (sp, tp ^ 2), (sp ^ 1, tp)


def meet(peers):
    barrier = pltpu.get_barrier_semaphore()
    for peer in peers:
        pl.semaphore_signal(barrier, inc=1, device_id=peer, device_id_type=MESH)
    pl.semaphore_wait(barrier, len(peers))


def push(src, dst, send, recv, peer):
    return pltpu.make_async_remote_copy(
        src_ref=src, dst_ref=dst, send_sem=send, recv_sem=recv, device_id=peer, device_id_type=MESH
    )


def gather_kernel(axes, count, *refs):
    ins, outs = refs[:count], refs[count : 2 * count]
    send, recv, local = refs[2 * count :]
    sp, tp, sib, across, beside = here()
    par = sp & 1
    meet((sib, across, beside))

    def cut(ref, axis, half):
        if axis is None:
            return ref
        size = ref.shape[axis] // 2
        index = [slice(None)] * len(ref.shape)
        index[axis] = pl.ds(pl.multiple_of(half * size, size), size)
        return ref.at[tuple(index)]

    def own(i):
        return pltpu.make_async_copy(ins[i], outs[i].at[tp], local.at[i])

    def to_sib(i):
        return push(ins[i], outs[i].at[tp], send.at[0, i], recv.at[0, i], sib)

    def to_across(i):
        return push(
            cut(ins[i], axes[i], par), cut(outs[i].at[tp], axes[i], par), send.at[1, i], recv.at[1, i], across
        )

    def far(i, half):
        return cut(outs[i].at[tp ^ 2], axes[i], half)

    def to_beside(i):
        return push(far(i, par), far(i, par), send.at[2, i], recv.at[2, i], beside)

    def on_first(i):
        return push(far(i, par), far(i, par), send.at[3, i], recv.at[3, i], sib)

    def on_second(i):
        return push(far(i, 1 - par), far(i, 1 - par), send.at[4, i], recv.at[4, i], sib)

    for i in range(count):
        to_across(i).start()
        to_sib(i).start()
        own(i).start()
    for i in range(count + 1):
        if i < count:
            to_across(i).wait_recv()
            on_first(i).start()
            if axes[i] is not None:
                to_beside(i).start()
        if i > 0 and axes[i - 1] is not None:
            to_beside(i - 1).wait_recv()
            on_second(i - 1).start()
    for i in range(count):
        own(i).wait()
        to_sib(i).wait()
        to_across(i).wait_send()
        on_first(i).wait()
        if axes[i] is not None:
            to_beside(i).wait_send()
            on_second(i).wait()


def gather_all(arrays, axes, ident):
    count = len(arrays)
    return pl.pallas_call(
        functools.partial(gather_kernel, axes, count),
        in_specs=[ANY] * count,
        out_specs=[ANY] * count,
        out_shape=[jax.ShapeDtypeStruct((4,) + a.shape, a.dtype) for a in arrays],
        scratch_shapes=[
            pltpu.SemaphoreType.DMA((5, count)), pltpu.SemaphoreType.DMA((5, count)),
            pltpu.SemaphoreType.DMA((count,)),
        ],
        compiler_params=pltpu.CompilerParams(collective_id=ident, has_side_effects=True),
        name="gather",
    )(*arrays)


ROWS = 512


def reduce_kernel(n, chunks, tiny_rows, *refs):
    g_ref, t_ref, out_ref, tout_ref = refs[:4]
    loc, pair, xr, yr, zr, fin, ta, tx, tz, ss, rs, zs, zq, fs, fq, ls, os, ts, tq, tzs, tzq = refs[4:]
    sp, tp, sib, across, beside = here()
    par, mine = sp & 1, sp // 2
    m = n // 2
    half = ROWS // 2
    piece = half // m

    barrier = pltpu.get_barrier_semaphore()
    for peer in (sib, across, beside):
        pl.semaphore_signal(barrier, inc=1, device_id=peer, device_id_type=MESH)

    def member(j):
        return (mine + j) % m

    def device(q):
        return (q * 2 + par, tp)

    @pl.loop(1, m)
    def _(j):
        pl.semaphore_signal(barrier, inc=1, device_id=device(member(j)), device_id_type=MESH)

    pl.semaphore_wait(barrier, m + 2)

    def rows(c):
        return pl.ds(pl.multiple_of(c * ROWS, ROWS), ROWS)

    def load(c, k):
        return pltpu.make_async_copy(g_ref.at[tp ^ (2 * k), rows(c)], loc.at[c % 2, k], ls.at[c % 2, k])

    def swap(c, k):
        return push(g_ref.at[tp ^ 1 ^ (2 * k), rows(c)], pair.at[c, k], ss.at[k, c], rs.at[k, c], sib)

    def cross(c):
        return push(pair.at[c, 1], xr.at[c], ss.at[2, c], rs.at[2, c], across)

    def halves(h):
        return pl.ds(pl.multiple_of(h * half, half), half)

    def side(c):
        return push(pair.at[c, 0, halves(1 - par)], yr.at[c], ss.at[3, c], rs.at[3, c], beside)

    def bit(q):
        return pl.ds(pl.multiple_of(q * piece, piece), piece)

    def spread(c, q):
        return push(yr.at[c, bit(q)], zr.at[c, mine], zs.at[c, q], zq.at[c, mine], device(q))

    def spread_in(c, q):
        return push(yr.at[c, bit(q)], zr.at[c, q], zs.at[c, q], zq.at[c, q], device(q))

    def place(q):
        return pl.ds(pl.multiple_of(par * half + q * piece, piece), piece)

    def share(c, q):
        return push(fin.at[c, place(mine)], fin.at[c, place(mine)], fs.at[c, q], fq.at[c, mine], device(q))

    def share_in(c, q):
        return push(fin.at[c, place(q)], fin.at[c, place(q)], fs.at[c, q], fq.at[c, q], device(q))

    def back(c):
        return push(fin.at[c, halves(par)], fin.at[c, halves(par)], ss.at[4, c], rs.at[4, c], beside)

    def write(c):
        return pltpu.make_async_copy(fin.at[c], out_ref.at[rows(c)], os.at[c])

    def tiny(k, peer):
        return push(ta.at[k], tx.at[k], ts.at[k], tq.at[k], peer)

    def tiny_out(q):
        return push(ta.at[3], tz.at[mine], tzs.at[q], tzq.at[mine], device(q))

    def tiny_in(q):
        return push(ta.at[3], tz.at[q], tzs.at[q], tzq.at[q], device(q))

    peers = (sib, across, beside)
    ta[0] = t_ref[...]
    tiny(0, sib).start()

    @pl.loop(0, chunks + 6)
    def _(s):
        @pl.when(s < chunks)
        def _():
            for k in range(2):
                swap(s, k).start()
                load(s, k).start()

        for stage in (1, 2, 3):

            @pl.when(s == 2 * stage)
            def _():
                tiny(stage - 1, peers[stage - 1]).wait()
                ta[stage] = ta[stage - 1] + tx[stage - 1]
                if stage < 3:
                    tiny(stage, peers[stage]).start()
                else:

                    @pl.loop(1, m)
                    def _(j):
                        tiny_out(member(j)).start()

        c1 = s - 1

        @pl.when((c1 >= 0) & (c1 < chunks))
        def _():
            for k in (1, 0):
                load(c1, k).wait()
                swap(c1, k).wait_recv()
                pair[c1, k] = pair[c1, k] + loc[c1 % 2, k]
                if k == 1:
                    cross(c1).start()

        c2 = s - 2

        @pl.when((c2 >= 0) & (c2 < chunks))
        def _():
            cross(c2).wait_recv()
            pair[c2, 0] = pair[c2, 0] + xr[c2]
            side(c2).start()

        c3 = s - 3

        @pl.when((c3 >= 0) & (c3 < chunks))
        def _():
            side(c3).wait_recv()
            yr[c3] = yr[c3] + pair[c3, 0, halves(par)]

            @pl.loop(1, m)
            def _(j):
                spread(c3, member(j)).start()

        c4 = s - 4

        @pl.when((c4 >= 0) & (c4 < chunks))
        def _():
            fin[c4, place(mine)] = yr[c4, bit(mine)]

            @pl.loop(1, m)
            def _(j):
                spread_in(c4, member(j)).wait_recv()
                fin[c4, place(mine)] = fin[c4, place(mine)] + zr[c4, member(j)]

            @pl.loop(1, m)
            def _(j):
                share(c4, member(j)).start()

        c5 = s - 5

        @pl.when((c5 >= 0) & (c5 < chunks))
        def _():
            @pl.loop(1, m)
            def _(j):
                share_in(c5, member(j)).wait_recv()

            back(c5).start()

        c6 = s - 6

        @pl.when((c6 >= 0) & (c6 < chunks))
        def _():
            back(c6).wait_recv()
            write(c6).start()

    tz[mine] = ta[3]

    @pl.loop(1, m)
    def _(j):
        tiny_in(member(j)).wait_recv()

    tout_ref[...] = jnp.zeros_like(tout_ref)

    @pl.loop(0, m)
    def _(q):
        tout_ref[...] += tz[q]

    @pl.loop(1, m)
    def _(j):
        tiny_out(member(j)).wait_send()

    @pl.loop(0, chunks)
    def _(c):
        for k in range(2):
            swap(c, k).wait_send()
        cross(c).wait_send()
        side(c).wait_send()
        back(c).wait_send()
        write(c).wait()

        @pl.loop(1, m)
        def _(j):
            spread(c, member(j)).wait_send()
            share(c, member(j)).wait_send()


def reduce_all(grads, tiny, n, ident):
    chunks = grads.shape[1] // ROWS
    m = n // 2
    dma = pltpu.SemaphoreType.DMA
    tr = tiny.shape[0]
    return pl.pallas_call(
        functools.partial(reduce_kernel, n, chunks, tr),
        in_specs=[ANY, VM],
        out_specs=[ANY, VM],
        out_shape=[sds(grads.shape[1], 128), sds(tr, 128)],
        scratch_shapes=[
            pltpu.VMEM((2, 2, ROWS, 128), f32), pltpu.VMEM((chunks, 2, ROWS, 128), f32),
            pltpu.VMEM((chunks, ROWS, 128), f32), pltpu.VMEM((chunks, ROWS // 2, 128), f32),
            pltpu.VMEM((chunks, m, ROWS // 2 // m, 128), f32), pltpu.VMEM((chunks, ROWS, 128), f32),
            pltpu.VMEM((4, tr, 128), f32), pltpu.VMEM((3, tr, 128), f32), pltpu.VMEM((m, tr, 128), f32),
            dma((5, chunks)), dma((5, chunks)), dma((chunks, m)), dma((chunks, m)), dma((chunks, m)),
            dma((chunks, m)), dma((2, 2)), dma((chunks,)), dma((3,)), dma((3,)), dma((m,)), dma((m,)),
        ],
        compiler_params=pltpu.CompilerParams(
            collective_id=ident, has_side_effects=True, vmem_limit_bytes=60 << 20
        ),
        name="reduce",
    )(grads, tiny)


def column_pick():
    pick = np.zeros((19, WIN, WIN), np.float32)
    for a in range(WIN):
        for b in range(WIN):
            pick[a - b + WIN - 1, a, b] = 1.0
    return pick


def row_pick():
    pick = np.zeros((19, WIN, WIN, WIN, 2, 2, SUB), np.float32)
    for pr in range(WIN):
        for qr in range(WIN):
            for qc in range(WIN):
                pick[pr - qr + WIN - 1, qc, pr, 0, qr // 5, qc // 5, (qr % 5) * 5 + qc % 5] = 1.0
    return pick[:, :, :, 0].reshape(190, WIN * WT)


def bias_of(table):
    heads = table.shape[0]
    grid = table.reshape(heads, 19, 19)
    columns = jnp.einsum("hrd,dab->hary", grid, jnp.asarray(column_pick()).reshape(19, WIN, WIN).transpose(0, 1, 2), precision="highest") if False else jnp.einsum("hrd,dab->harb", grid, jnp.asarray(column_pick()), precision="highest")
    rows = jnp.dot(columns.reshape(heads * WIN, 190), jnp.asarray(row_pick()), precision="highest")
    rows = rows.reshape(heads, 2, 5, 2, 5, WT).transpose(0, 3, 1, 4, 2, 5)
    rows = rows.reshape(heads, 4, REAL, WT)
    return jnp.pad(rows, ((0, 0), (0, 0), (0, SUB - REAL), (0, 0))).reshape(heads, WT, WT)


def to_blocks(values):
    tail = values.shape[2:]
    return values.reshape((2, 2, NW, SUB) + tail) if False else values


def shift_along(x, axis, distance):
    count = lax.axis_size(axis)
    return lax.ppermute(x, axis, [((i - distance) % count, i) for i in range(count)])


def grid_of(tokens):
    return tokens.reshape(NW, 2, 2, SUB, -1).transpose(1, 0, 2, 3, 4).reshape(2, 6, SUB, -1)


def tokens_of(grid):
    return grid.reshape(2, NW, 2, SUB, -1).transpose(1, 0, 2, 3, 4).reshape(TOK, -1)


def shifted(tokens):
    grid = grid_of(tokens)
    right = shift_along(grid[:, :1], "tp", -1)
    grid = jnp.concatenate([grid[:, 1:], right], axis=1)
    below = shift_along(grid[:1], "sp", -1)
    return tokens_of(jnp.concatenate([grid[1:], below], axis=0))


def unshifted(tokens):
    grid = grid_of(tokens)
    above = shift_along(grid[1:], "sp", 1)
    grid = jnp.concatenate([above, grid[:1]], axis=0)
    left = shift_along(grid[:, 5:], "tp", 1)
    return tokens_of(jnp.concatenate([left, grid[:, :5]], axis=1))


def to_order(natural):
    values = natural.reshape(2, 5, NW, 2, 5, -1).transpose(2, 0, 3, 1, 4, 5).reshape(NW, 2, 2, REAL, -1)
    values = jnp.pad(values, ((0, 0), (0, 0), (0, 0), (0, SUB - REAL), (0, 0)))
    return values.reshape(TOK, -1)


def to_natural(tokens):
    values = tokens.reshape(NW, 2, 2, SUB, -1)[:, :, :, :REAL]
    values = values.reshape(NW, 2, 2, 5, 5, -1).transpose(1, 3, 0, 2, 4, 5)
    return values.reshape(10, 30, -1)


def shards(
    patches, merge_gain, merge_shift, merge_weight, first_gain, first_shift, input_weight,
    input_bias, position_table, output_weight, output_bias, second_gain, second_shift,
    expand_weight, expand_bias, shrink_weight, shrink_bias, page_map, valid_flags, cotangent,
):
    sp_count = lax.axis_size("sp")
    tp = lax.axis_index("tp")
    sp = lax.axis_index("sp")
    full_channels = 4.0 * C2

    small = jnp.concatenate(
        [input_bias.reshape(-1), expand_bias.reshape(-1), position_table.transpose(0, 2, 1).reshape(-1)]
    )
    small = jnp.pad(small, (0, 40 * 128 - small.shape[0])).reshape(40, 128)
    wqkv, wo, we, ws = [], [], [], []
    arrays = [small]
    for b in range(2):
        arrays += [input_weight[b].transpose(1, 0, 2), output_weight[b], expand_weight[b], shrink_weight[b]]
    full = gather_all(arrays, [None] + [1, 0, 0, 0] * 2, 1)
    small = full[0].reshape(4, 40 * 128)
    wqkv, wo, we, ws = full[1::4], full[2::4], full[3::4], full[4::4]
    bqkv, be, bias = [], [], []
    for b in range(2):
        ib = small[:, b * 256 : (b + 1) * 256].reshape(4, 2, 128)
        bqkv.append(jnp.concatenate([ib[:, :1], jnp.zeros((4, 1, 128), f32), ib[:, 1:]], axis=1).reshape(4, 1, 384))
        be.append(small[:, 512 + b * 512 : 1024 + b * 512].reshape(4, 1, 512))
    tables = small[:, 1536 : 1536 + 2888].reshape(4, 2, 4, 361).transpose(1, 0, 2, 3).reshape(2, 16, 361)
    bias, pull_bias = jax.vjp(lambda t: tuple(bias_of(t[b]) for b in range(2)), tables)

    valid = valid_flags.astype(f32)
    vgrid = valid.reshape(2, 5, 24, 5).transpose(0, 2, 1, 3).reshape(2, 24, REAL)
    vgrid = jnp.pad(vgrid, ((0, 0), (0, 0), (0, SUB - REAL)))
    below = shift_along(vgrid[:1], "sp", -1)
    vshift = jnp.roll(jnp.concatenate([vgrid[1:], below], axis=0), -1, axis=1)
    own = lambda grid: lax.dynamic_slice_in_dim(grid, 6 * tp, 6, 1)
    vtok = [tokens_of(own(vgrid)[..., None]), tokens_of(own(vshift)[..., None])]
    pages = jnp.concatenate([page_map, page_map[:1]], axis=0)
    pages = jnp.concatenate([pages, pages[:, :1]], axis=1)
    pages = lax.dynamic_slice(pages, (sp, 3 * tp), (2, 4))
    page = jnp.stack([pages[:, :3], pages[:, 1:]], axis=2).transpose(1, 0, 2)
    wrap_row = (jnp.arange(2) == 1) & (sp == sp_count - 1)
    wrap_col = (jnp.arange(2) == 1)[None, :] & (jnp.arange(NW) == NW - 1)[:, None] & (tp == 3)
    region = page * 4 + 2 * wrap_row[None, :, None].astype(jnp.int32) + wrap_col[:, None, :].astype(jnp.int32)
    region = jnp.broadcast_to(region[..., None], (NW, 2, 2, SUB)).reshape(TOK)
    regions = [jnp.zeros((TOK,), jnp.int32), region]
    mask_args = [
        (regions[b].reshape(TOK, 1), regions[b].reshape(NW, 1, WT), vtok[b].reshape(NW, 1, WT), vtok[b])
        for b in range(2)
    ]

    gain = merge_gain.reshape(2, 2, 64).transpose(1, 0, 2).reshape(256)
    offset = merge_shift.reshape(2, 2, 64).transpose(1, 0, 2).reshape(256)
    weight = merge_weight.reshape(2, 2, 64, C).transpose(1, 0, 2, 3).reshape(256, C)
    quads = patches.reshape(10, 2, 120, 128).transpose(0, 2, 1, 3).reshape(1200, 256)
    partial = jnp.dot(quads * gain, weight, precision="high").reshape(10, 4, 30, C).transpose(1, 0, 2, 3).reshape(4, 300, C)
    moment = lax.psum((jnp.sum(quads, axis=1), jnp.sum(quads * quads, axis=1)), "tp")
    vecs = lax.psum((jnp.dot(gain, weight, precision="highest"), jnp.dot(offset, weight, precision="highest")), "tp")
    mean = moment[0] / full_channels
    inverse = lax.rsqrt(moment[1] / full_channels - mean * mean + epsilon)
    total = lax.psum_scatter(partial, "tp", scatter_dimension=0, tiled=False)
    mine = lambda v: lax.dynamic_slice_in_dim(v.reshape(10, 4, 30), tp, 1, 1).reshape(300, 1)
    field_nat = mine(inverse) * (total - mine(mean) * vecs[0]) + vecs[1]
    field = to_order(field_nat)

    squares = []
    saved = []
    row = lambda x: x.reshape(1, C)
    for b in range(2):
        if b == 1:
            field = shifted(field)
        middle, qkv, p, att, sq = attn_fwd(
            field, row(first_gain[b]), row(first_shift[b]), wqkv[b], bqkv[b], wo[b], row(output_bias[b]),
            bias[b], mask_args[b],
        )
        out, hid, slope, sqb, sqo = mlp_fwd(
            middle, row(second_gain[b]), row(second_shift[b]), we[b], be[b], ws[b], row(shrink_bias[b]), vtok[b]
        )
        squares += [jnp.sum(sq), jnp.sum(sqb)]
        saved.append((field, qkv, p, att, middle, hid, slope))
        field = out
    squares.append(jnp.sum(sqo))
    out_nat = to_natural(unshifted(field))
    output = lax.all_to_all(out_nat.reshape(10, 30, 4, 128), "tp", 2, 1, tiled=True).reshape(10, 120, 128)

    cot = lax.all_to_all(cotangent.reshape(10, 120, 1, 128), "tp", 1, 2, tiled=True).reshape(10, 30, C)
    grad = shifted(to_order(cot))
    grads = [None, None]
    pack = None
    for b in (1, 0):
        field_in, qkv, p, att, middle, hid, slope = saved[b]
        gm, pack, dbe, small2 = mlp_bwd(
            grad, middle, row(second_gain[b]), row(second_shift[b]), we[b], ws[b], hid, slope, pack, 1 - b
        )
        grad, pack, dbqkv, dbias, small1 = attn_bwd(
            gm, field_in, row(first_gain[b]), row(first_shift[b]), wqkv[b], wo[b], qkv, p, att, pack, 5 - b
        )
        grads[b] = (dbqkv, dbe, dbias, small1, small2)
        if b == 1:
            grad = unshifted(grad)
    gf = to_natural(grad)
    m1 = jnp.sum(gf * vecs[0], axis=-1)
    m2 = jnp.sum(gf * (field_nat.reshape(10, 30, C) - vecs[1]), axis=-1)
    full = lax.all_gather(gf, "tp", axis=1, tiled=True).reshape(1200, C)
    m1 = lax.all_gather(m1, "tp", axis=1, tiled=True).reshape(1200, 1) / full_channels
    m2 = lax.all_gather(m2, "tp", axis=1, tiled=True).reshape(1200, 1) / full_channels
    xhat = (quads - mean[:, None]) * inverse[:, None]
    gmerged = lax.dot_general(full, weight, NT, precision="high")
    dmw = lax.dot_general(xhat * gain + offset, full, TN, precision="high")
    dmg = jnp.sum(gmerged * xhat, axis=0)
    dms = jnp.sum(gmerged, axis=0)
    gquads = inverse[:, None] * (gmerged * gain - m1 - xhat * m2)
    patches_grad = gquads.reshape(10, 120, 2, 128).transpose(0, 2, 1, 3).reshape(20, 240, 64)

    dtables = pull_bias((grads[0][2], grads[1][2]))[0]
    pieces = [
        jnp.stack([grads[b][0] for b in range(2)]), jnp.stack([grads[b][1] for b in range(2)]), dtables,
        jnp.stack([grads[b][3][:3] for b in range(2)]), jnp.stack([grads[b][4][:3] for b in range(2)]),
        jnp.stack(squares), jnp.sum(vtok[0]).reshape(1),
    ]
    line = jnp.concatenate([x.reshape(-1) for x in pieces])
    tiny = jnp.pad(line, (0, 200 * 128 - line.shape[0])).reshape(200, 128)
    packed, tiny = reduce_all(pack, tiny, sp_count, 2)
    line, parts, at = tiny.reshape(-1), [], 0
    for x in pieces:
        parts.append(line[at : at + x.size].reshape(x.shape))
        at += x.size
    dbqkv, dbe, dtab, small1, small2, sums, count = parts
    count = count[0]
    mlp = packed[:8192].reshape(2, 2, 4, 512, 128)[::-1]
    att = packed[8192:].reshape(2, 2048, 128)[::-1]
    g_qkv = att[:, :1536].reshape(2, 3, 512, 128).transpose(0, 2, 1, 3)
    g_wo = att[:, 1536:].reshape(2, 4, 128, 128).transpose(0, 2, 1, 3).reshape(2, 128, 512)
    g_we = mlp[:, 0].transpose(0, 2, 1, 3).reshape(2, 512, 512)
    g_ws = mlp[:, 1].transpose(0, 2, 1, 3).reshape(2, 512, 512)
    own4 = lambda x, axis: lax.dynamic_index_in_dim(x, tp, axis, keepdims=False)
    dbqkv = own4(dbqkv, 1).reshape(2, 3, 128)
    g_bias = jnp.stack([dbqkv[:, 0], dbqkv[:, 2]], axis=1)
    g_be = own4(dbe, 1).reshape(2, 512)
    g_tab = own4(dtab.reshape(2, 4, 4, 361), 1).transpose(0, 2, 1)
    dmw, dmg, dms = lax.psum((dmw, dmg, dms), "sp")
    back = lambda x: x.reshape((2, 2, 64) + x.shape[1:]).swapaxes(0, 1).reshape((4, 64) + x.shape[1:])
    rms = jnp.sqrt(sums / (count * C))
    return (
        output, patches_grad, back(dmg), back(dms), back(dmw), small1[:, 0], small1[:, 1], g_qkv, g_bias,
        g_tab, g_wo, small1[:, 2], small2[:, 0], small2[:, 1], g_we, g_be, g_ws, small2[:, 2], rms,
    )


def solution(mesh):
    placed = (
        P("sp", None, "tp"), P(None, "tp"), P(None, "tp"), P(None, "tp", None), P(), P(),
        P(None, None, None, "tp"), P(None, None, "tp"), P(None, None, "tp"), P(None, "tp", None),
        P(), P(), P(), P(None, None, "tp"), P(None, "tp"), P(None, "tp", None), P(), P(),
        P("sp", None), P("sp", None, "tp"),
    )
    results = (
        P("sp", None, "tp"), P("sp", None, "tp"), P(None, "tp"), P(None, "tp"), P(None, "tp", None),
        P(), P(), P(None, None, None, "tp"), P(None, None, "tp"), P(None, None, "tp"),
        P(None, "tp", None), P(), P(), P(), P(None, None, "tp"), P(None, "tp"), P(None, "tp", None),
        P(), P(),
    )
    return jax.shard_map(shards, mesh=mesh, in_specs=placed, out_specs=results, check_vma=False)
```

time: 1270 us -> 850 us (0.67)
  Pallas kernels: 0 us -> 516 us
  waiting for transfers between devices: 451 us -> 38 us
  other arithmetic: 211 us -> 24.4 us
  matrix products: 214 us -> 28.5 us
  local copies, waits for them, and re-layouts: 279 us -> 147 us
  blocking collectives: 72.8 us -> 47.9 us
    pallas_call x0 -> x10, Pallas kernels: none -> 516 us  [the longest x1 193 us: gather_all(): pl.pallas_call(functools.partial(gather_kernel, axes, count), in_specs=[A...]
    psum x9 -> x1, waiting for transfers between devices: 399 us -> 33 us  [shards(): dmw, dmg, dms = lax.psum((dmw, dmg, dms), 'sp')]
    dot_general x39 -> x13, matrix products: 214 us -> 28.5 us  [the longest x4 13.4 us: bias_of(): jnp.dot(columns.reshape(heads * WIN, 190), jnp.asarray(row_pick()), preci...]
    scatter-add x2 -> x0, other arithmetic: 112 us -> none  [local_attention(): bias_grid = jnp.transpose(table_here[bias_index], (2, 0, 1))]
    reduce_sum x31 -> x8, other arithmetic: 68.8 us -> 5.48 us  [the longest x4 2.44 us: shards(): squares += [jnp.sum(sq), jnp.sum(sqb)]]
    gather x8 -> x0, local copies, waits for them, and re-layouts: 54.2 us -> none  [the longest x6 46.7 us: local_attention(): bias_grid = jnp.transpose(table_here[bias_index], (2, 0, 1))]
    psum x3 -> x2, blocking collectives: 72.8 us -> 32.6 us  [the longest x1 20.2 us: shards(): dmw, dmg, dms = lax.psum((dmw, dmg, dms), 'sp')]
    ppermute x5 -> x9, waiting for transfers between devices: 41.2 us -> 4.91 us  [shift_along(): lax.ppermute(x, axis, [((i - distance) % count, i) for i in range(count)])]
  transfers between devices with their start and end apart: 15 -> 14, of which waited for: 13 -> 3; matrix products, arithmetic and copies ran while one was open for 26% -> 23% of each run, Pallas kernels for 0% -> 58%
where the time goes in v1:
time: 850 us; the launch traced here: 841 us
  Pallas kernels  516 us (61%)
  local copies, waits for them, and re-layouts  147 us (17%)
  blocking collectives  47.9 us (6%)
  waiting for transfers between devices  38 us (4%)
  matrix products  28.5 us (3%)
  other arithmetic  24.4 us (3%)
  starting transfers between devices  23.9 us (3%)
  between operations  15.9 us (2%)
    pallas_call x1, Pallas kernels, gather_all(): pl.pallas_call(functools.partial(gather_kernel, axes, count), in_specs=[A...  193 us
    pallas_call x1, Pallas kernels, reduce_all(): pl.pallas_call(functools.partial(reduce_kernel, n, chunks, tr), in_specs=...  190 us
    pallas_call x2, Pallas kernels, attn_bwd(): pl.pallas_call(attn_bwd_kernel, grid=(4,), in_specs=[whole((TOK, C)), who...  44.6 us
    pallas_call x2, Pallas kernels, mlp_bwd(): pl.pallas_call(body, grid=(4,), in_specs=[whole((TOK, C)), whole((TOK, C)...  37.2 us
    psum x1, waiting for transfers between devices, shards(): dmw, dmg, dms = lax.psum((dmw, dmg, dms), 'sp')  33 us
    pallas_call x2, Pallas kernels, attn_fwd(): pl.pallas_call(attn_fwd_kernel, grid=(4,), in_specs=[whole((TOK, C)), who...  27.8 us
    pallas_call x2, Pallas kernels, mlp_fwd(): pl.pallas_call(mlp_fwd_kernel, grid=(4,), in_specs=[whole((TOK, C)), whol...  22.7 us
    psum x1, blocking collectives, shards(): dmw, dmg, dms = lax.psum((dmw, dmg, dms), 'sp')  20.2 us
  transfers between devices with their start and end apart: 14, of which 3 were waited for; matrix products, arithmetic and copies ran while one was open for 23% of the time, Pallas kernels for 58%

profile of v1, /device:TPU:0, one launch (start us, length us, event | category | flops | bytes accessed | tf_op | source)
XLA Modules:
  0.0 841.0 jit_solution(14961416390596604720)
XLA Ops:
  8.8 6.0 collective-permute-start.2
  14.8 2.5 copy.428
  17.4 4.2 all-to-all-start.1
  23.4 2.0 copy.387
  27.8 12.3 %all-reduce.11 = (f32[512]{0:T(512)}, f32[512]{0:T(512)}, f32[1200]{0:T(1024)S(1)}, f32[1200]{0:T(1024)S(1)}) all-reduce(f32[512]{0:T(512)S(1)} %bitcast.450, f32[512]{0:T(512)S(1)} %bitcast.451, f32[1200]{0:T(1024)S(1)} %reduce_sum.119, f32[1200]{0:T(1024)S(1)} %reduce_sum.117), channel_id=1, replica_groups=mesh['sp'=8,'tp'=4] {'tp'}, use_global_device_ids=true, to_apply=%region_6.7 | all-reduce | flops 3424 | bytes 27392 | tf_op jit(solution)/shard_map/psum | solution.py:800
  43.4 2.3 mul.139
  47.0 3.0 copy.391
  51.9 2.9 slice_bitcast_fusion.4
  54.8 2.1 slice_bitcast_fusion
  57.6 193.3 %gather.1 = (f32[4,40,128]{2,1,0:T(8,128)}, f32[4,3,512,128]{3,2,1,0:T(8,128)}, f32[4,128,512]{2,1,0:T(8,128)}, f32[4,512,512]{2,1,0:T(8,128)}, f32[4,512,512]{2...) custom-call(f32[40,128]{1,0:T(8,128)} %fusion.25.refs_0_, ...), custom_call_target="tpu_custom_call" | custom-call | tf_op jit(solution)/shard_map/gather/pallas_call | solution.py:434
  258.0 2.2 copy.398
  260.2 2.7 reshape.610
  262.9 2.3 convolution_bitcast_fusion.1
  280.8 2.2 copy.413
  283.0 2.0 reshape.613
  293.9 4.1 dynamic-slice_reduce_fusion
  302.0 13.9 %attn_fwd.2 = (f32[384,512]{1,0:T(8,128)}, f32[4,384,384]{2,1,0:T(8,128)}, f32[4,3,512,128]{3,2,1,0:T(8,128)}, f32[4,384,128]{2,1,0:T(8,128)}, f32[1,512]{1,0:T(1,128)}) custom-call(f32[384,512]{1,0:T(8,128)} %bitcast.371, f32[1,512]{1,0:T(1,128)} %get-tuple-element.297.gain_ref, f32[1,512]{1,0:T(1,128)} %get-tuple-element.312.shift_ref, ...), custom_call_target="tpu_custom_call" | custom-call | tf_op jit(solution)/shard_map/attn_fwd/pallas_call | solution.py:132
  315.9 11.4 %mlp_fwd.2 = (f32[384,512]{1,0:T(8,128)}, f32[4,384,512]{2,1,0:T(8,128)}, f32[4,384,512]{2,1,0:T(8,128)}, f32[1,512]{1,0:T(1,128)}, f32[1,512]{1,0:T(1,128)}) custom-call(f32[384,512]{1,0:T(8,128)} %get-tuple-element.70.mid_ref.refs_1_, f32[1,512]{1,0:T(1,128)} %get-tuple-element.289.gain_ref.refs_2_, f32[1,512]{1,0:T(1,128)} %get-tuple-element.314.shift_ref.refs_3_, ...), custom_call_target="tpu_custom_call" | custom-call | tf_op jit(solution)/shard_map/mlp_fwd/pallas_call | solution.py:182
  352.8 13.9 %attn_fwd.3 = (f32[384,512]{1,0:T(8,128)}, f32[4,384,384]{2,1,0:T(8,128)}, f32[4,3,512,128]{3,2,1,0:T(8,128)}, f32[4,384,128]{2,1,0:T(8,128)}, f32[1,512]{1,0:T(1,128)}) custom-call(f32[384,512]{1,0:T(8,128)} %bitcast.373, f32[1,512]{1,0:T(1,128)} %get-tuple-element.296.gain_ref, f32[1,512]{1,0:T(1,128)} %get-tuple-element.313.shift_ref, ...), custom_call_target="tpu_custom_call" | custom-call | tf_op jit(solution)/shard_map/attn_fwd/pallas_call | solution.py:132
  366.8 11.3 %mlp_fwd.3 = (f32[384,512]{1,0:T(8,128)}, f32[4,384,512]{2,1,0:T(8,128)}, f32[4,384,512]{2,1,0:T(8,128)}, f32[1,512]{1,0:T(1,128)}, f32[1,512]{1,0:T(1,128)}) custom-call(f32[384,512]{1,0:T(8,128)} %get-tuple-element.76.mid_ref, f32[1,512]{1,0:T(1,128)} %get-tuple-element.288.gain_ref, f32[1,512]{1,0:T(1,128)} %get-tuple-element.315.shift_ref, ...), custom_call_target="tpu_custom_call" | custom-call | tf_op jit(solution)/shard_map/mlp_fwd/pallas_call | solution.py:182
  380.1 2.7 collective-permute-start.3
  382.7 18.6 %mlp_bwd.2 = (f32[384,512]{1,0:T(8,128)}, f32[4,12288,128]{2,1,0:T(8,128)}, f32[4,1,512]{2,1,0:T(1,128)}, f32[8,512]{1,0:T(8,128)}) custom-call(f32[384,512]{1,0:T(8,128)} %bitcast.397, f32[384,512]{1,0:T(8,128)} %get-tuple-element.76.mid_ref, f32[1,512]{1,0:T(1,128)} %get-tuple-element.288.gain_ref, f32[1,512]{1,0:T(1,128)} %get-tuple-element.315.shift_ref, ...), custom_call_target="tpu_custom_call" | custom-call | tf_op jit(solution)/shard_map/mlp_bwd/pallas_call | solution.py:247
  401.4 22.1 %attn_bwd.2 = (f32[384,512]{1,0:T(8,128)}, f32[4,12288,128]{2,1,0:T(8,128)}, f32[4,1,384]{2,1,0:T(1,128)}, f32[16,128,128]{2,1,0:T(8,128)}, f32[8,512]{1,0:T(8,128)}) custom-call(f32[384,512]{1,0:T(8,128)} %get-tuple-element.82.gm_ref, f32[384,512]{1,0:T(8,128)} %bitcast.374, f32[1,512]{1,0:T(1,128)} %get-tuple-element.296.gain_ref, ...), custom_call_target="tpu_custom_call", output_to_operand_aliasing={{1}: (9, {})} | custom-call | tf_op jit(solution)/shard_map/attn_bwd/pallas_call | solution.py:325
  423.4 2.0 fusion.39
  428.2 5.0 convolution_bitcast_fusion.6
  434.4 4.7 collective-permute-done.7
  440.0 2.2 fusion.8
  448.4 18.6 %mlp_bwd.3 = (f32[384,512]{1,0:T(8,128)}, f32[4,12288,128]{2,1,0:T(8,128)}, f32[4,1,512]{2,1,0:T(1,128)}, f32[8,512]{1,0:T(8,128)}) custom-call(f32[384,512]{1,0:T(8,128)} %bitcast.406, f32[384,512]{1,0:T(8,128)} %get-tuple-element.70.mid_ref.refs_1_, f32[1,512]{1,0:T(1,128)} %get-tuple-element.289.gain_ref.refs_2_, ...), custom_call_target="tpu_custom_call", output_to_operand_aliasing={{1}: (8, {})} | custom-call | tf_op jit(solution)/shard_map/mlp_bwd/pallas_call | solution.py:247
  467.0 22.5 %attn_bwd.3 = (f32[384,512]{1,0:T(8,128)}, f32[4,12288,128]{2,1,0:T(8,128)}, f32[4,1,384]{2,1,0:T(1,128)}, f32[16,128,128]{2,1,0:T(8,128)}, f32[8,512]{1,0:T(8,128)}) custom-call(f32[384,512]{1,0:T(8,128)} %get-tuple-element.91.gm_ref, f32[384,512]{1,0:T(8,128)} %bitcast.372, f32[1,512]{1,0:T(1,128)} %get-tuple-element.297.gain_ref, ...), custom_call_target="tpu_custom_call", output_to_operand_aliasing={{1}: (9, {})} | custom-call | tf_op jit(solution)/shard_map/attn_bwd/pallas_call | solution.py:325
  492.3 2.5 copy.437
  496.8 5.0 convolution_bitcast_fusion.5
  501.9 2.2 fusion.11
  504.5 3.9 concatenate.64
  509.1 190.2 %reduce.14 = (f32[12288,128]{1,0:T(8,128)}, f32[200,128]{1,0:T(8,128)}) custom-call(f32[4,12288,128]{2,1,0:T(8,128)} %get-tuple-element.97.refs_0_, f32[200,128]{1,0:T(8,128)} %pad_bitcast_fusion.1.refs_1_), custom_call_target="tpu_custom_call" | custom-call | tf_op jit(solution)/shard_map/reduce/pallas_call | solution.py:651
  704.5 4.5 slice.367
  713.5 2.3 reshape_reshape.25
  715.8 2.1 copy.426
  717.9 4.2 all-to-all-start
  723.2 10.2 %all-gather.1 = f32[4,30,10]{1,2,0:T(8,128)S(1)} all-gather(f32[1,30,10]{1,2,0:T(8,128)S(1)} %bitcast.441), channel_id=1, replica_groups=mesh['sp'=8,'tp'=4] {'tp'}, dimensions={0}, use_global_device_ids=true | all-gather | bytes 6000 | tf_op jit(solution)/shard_map/all_gather | solution.py:848
  733.6 5.2 all-gather
  748.8 3.9 fusion.38
  755.6 3.6 copy.438
  761.5 3.2 copy_bitcast_fusion.1
  764.7 2.1 copy.427
  766.8 2.0 reshape.546
  768.7 3.8 fusion.36
  779.2 20.2 %all-reduce.10 = (f32[4,64]{1,0:T(4,128)}, f32[4,64]{1,0:T(4,128)}) all-reduce(f32[4,64]{1,0:T(4,128)S(1)} %bitcast.453, f32[4,64]{1,0:T(4,128)S(1)} %bitcast.452), channel_id=1, replica_groups=mesh['sp'=8,'tp'=4] {'sp'}, use_global_device_ids=true, to_apply=%region_10.11 | all-reduce | flops 512 | bytes 4096 | tf_op jit(solution)/shard_map/psum | solution.py:883
  799.4 33.0 %all-reduce.15.cloned.1.call-done = f32[4,64,512]{2,1,0:T(8,128)} async-done(((f32[4,64,512]{2,1,0:T(8,128)}), f32[4,64,512]{2,1,0:T(8,128)}) %all-reduce.15.cloned.1.call-update) | async-done | bytes 524304 | tf_op jit(solution)/shard_map/psum | solution.py:883
  (383 shorter events, 126.0 us)
Async XLA Ops:
  8.0 13.6 %copy-start.70 = (f32[4,64]{1,0:T(4,128)S(1)}, f32[4,64]{1,0:T(4,128)}, u32[]{:S(2)}) copy-start(f32[4,64]{1,0:T(4,128)} %param.25) | copy-start | bytes 3076
  8.0 13.7 %copy-start.71 = (f32[4,64]{1,0:T(4,128)S(1)}, f32[4,64]{1,0:T(4,128)}, u32[]{:S(2)}) copy-start(f32[4,64]{1,0:T(4,128)} %param.26) | copy-start | bytes 3076
  8.0 13.8 %copy-start.2 = (f32[4,64,512]{2,1,0:T(8,128)S(1)}, f32[4,64,512]{2,1,0:T(8,128)}, u32[]{:S(2)}) copy-start(f32[4,64,512]{2,1,0:T(8,128)} %param.27) | copy-start | bytes 1572868
  8.8 335.2 %collective-permute-start.2 = (f32[1,24,32]{1,0,2:T(1,128)}, f32[1,24,32]{1,0,2:T(1,128)}, u32[]{:S(2)}, u32[]{:S(2)}) collective-permute-start(f32[1,24,32]{1,0,2:T(1,128)} %get-tuple-element.273), channel_id=1, source_target_pairs={{4,0},{8,4},{12,8},{16,12},{20,16},{24,20},{28,24},{0,28},{5,1},{9... | collective-permute-start | bytes 9224 | tf_op jit(solution)/shard_map/ppermute | solution.py:705
  17.4 272.4 %all-to-all-start.1 = ((f32[10,120,1,128]{3,2,0,1:T(1,128)}), f32[10,120,1,128]{3,2,0,1:T(1,128)}, u32[]{:S(2)}, u32[]{:S(2)}) async-start(f32[10,120,1,128]{3,2,0,1:T(1,128)} %copy.428), calls=%async_computation.1 | async-start | bytes 1228800 | tf_op jit(solution)/shard_map/all_to_all | solution.py:828
  21.5 272.4 %all-reduce.17.cloned.1.call-start = ((), (), s32[]{:S(2)}) async-start(), calls=%async_computation.4 | async-start | bytes 4915200
  50.0 705.5 %all-gather.4.cloned.1.call-start = ((), (), s32[]{:S(2)}) async-start(), calls=%async_computation.2 | async-start | bytes 4915200 | tf_op jit(solution)/shard_map/all_gather | solution.py:846
  51.1 3.8 copy-start.11
  57.6 194.8 %copy-start.41 = (s32[8,12]{1,0:T(8,128)S(1)}, s32[8,12]{1,0:T(8,128)}, u32[]{:S(2)}) copy-start(s32[8,12]{1,0:T(8,128)} %param.41) | copy-start | bytes 1156
  57.6 194.8 %copy-start.54 = (f32[2,512]{1,0:T(2,128)S(1)}, f32[2,512]{1,0:T(2,128)}, u32[]{:S(2)}) copy-start(f32[2,512]{1,0:T(2,128)} %param.28) | copy-start | bytes 12292
  57.6 195.4 %copy-start.55 = (f32[2,512]{1,0:T(2,128)S(1)}, f32[2,512]{1,0:T(2,128)}, u32[]{:S(2)}) copy-start(f32[2,512]{1,0:T(2,128)} %param.35) | copy-start | bytes 12292
  57.6 199.2 %copy-start.16 = (f32[19,10,10,1]{0,2,1,3:T(8,128)S(1)}, f32[19,10,10,1]{0,2,1,3:T(8,128)}, u32[]{:S(2)}) copy-start(f32[19,10,10,1]{0,2,1,3:T(8,128)} %constant.99) | copy-start | bytes 22804
  265.1 5.4 copy-start.29
  265.2 6.1 copy-start.32
  274.2 24.0 %copy-start.23 = (f32[2,5,3,2,5]{4,3,2,1,0:T(2,128)}, f32[2,5,3,2,5]{4,3,2,1,0:T(2,128)S(1)}, u32[]{:S(2)}) copy-start(f32[2,5,3,2,5]{4,3,2,1,0:T(2,128)S(1)} %mul.140) | copy-start | bytes 3604
  283.0 3.8 copy-start.59
  283.0 3.8 copy-start.60
  283.0 4.4 copy-start.72
  283.0 4.4 copy-start.73
  293.3 37.0 %collective-permute-start.5 = (f32[2,1,32,512]{3,2,1,0:T(8,128)}, f32[2,1,32,512]{3,2,1,0:T(8,128)}, u32[]{:S(2)}, u32[]{:S(2)}) collective-permute-start(f32[2,1,32,512]{3,2,1,0:T(8,128)} %slice.397), channel_id=1, source_target_pairs={{1,0},{2,1},{3,2},{0,3},{5,4},{6,5},{7,6},{4,7},{9,8},{10,9},{11,1... | collective-permute-start | bytes 393224 | tf_op jit(solution)/shard_map/ppermute | solution.py:705
  293.9 4.2 copy-start.25
  328.5 4.4 collective-permute-start
  332.2 3.4 copy-start.36
  332.2 15.3 %collective-permute-start.6 = (f32[1,6,32,512]{3,2,1,0:T(8,128)}, f32[1,6,32,512]{3,2,1,0:T(8,128)}, u32[]{:S(2)}, u32[]{:S(2)}) collective-permute-start(f32[1,6,32,512]{3,2,1,0:T(8,128)} %get-tuple-element.257), channel_id=1, source_target_pairs={{4,0},{8,4},{12,8},{16,12},{20,16},{24,20},{28,24},{0,28},{5,1},{9... | collective-permute-start | bytes 1179656 | tf_op jit(solution)/shard_map/ppermute | solution.py:705
  333.8 17.0 %collective-permute-start.1 = (f32[1,6,32,512]{3,2,1,0:T(8,128)}, f32[1,6,32,512]{3,2,1,0:T(8,128)}, u32[]{:S(2)}, u32[]{:S(2)}) collective-permute-start(f32[1,6,32,512]{3,2,1,0:T(8,128)} %get-tuple-element.261), channel_id=1, source_target_pairs={{4,0},{8,4},{12,8},{16,12},{20,16},{24,20},{28,24},{0,28},{5,1},{9... | collective-permute-start | bytes 1179656 | tf_op jit(solution)/shard_map/ppermute | solution.py:705
  342.9 4.5 copy-start.14
  380.1 64.8 %copy-start.6 = (f32[1,3,2,32,512]{4,3,2,0,1:T(8,128)}, f32[1,3,2,32,512]{4,3,2,0,1:T(8,128)S(1)}, u32[]{:S(2)}) copy-start(f32[1,3,2,32,512]{4,3,2,0,1:T(8,128)S(1)} %get-tuple-element.259) | copy-start | bytes 1179652
  380.1 64.8 %collective-permute-start.3 = (f32[1,6,32,512]{3,2,1,0:T(8,128)}, f32[1,6,32,512]{3,2,1,0:T(8,128)S(1)}, u32[]{:S(2)}, u32[]{:S(2)}) collective-permute-start(f32[1,6,32,512]{3,2,1,0:T(8,128)} %bitcast.80), channel_id=1, source_target_pairs={{28,0},{0,4},{4,8},{8,12},{12,16},{16,20},{20,24},{24,28},{29,1},{... | collective-permute-start | bytes 1179656 | tf_op jit(solution)/shard_map/ppermute | solution.py:705
  425.5 13.7 %collective-permute-start.7 = (f32[1,6,32,512]{3,2,1,0:T(8,128)}, f32[1,6,32,512]{3,2,1,0:T(8,128)}, u32[]{:S(2)}, u32[]{:S(2)}) collective-permute-start(f32[1,6,32,512]{3,2,1,0:T(8,128)} %bitcast.101), channel_id=1, source_target_pairs={{28,0},{0,4},{4,8},{8,12},{12,16},{16,20},{20,24},{24,28},{29,1},{... | collective-permute-start | bytes 1179656 | tf_op jit(solution)/shard_map/ppermute | solution.py:705
  428.2 5.0 copy-start.51
  428.2 5.6 copy-start.50
  428.2 11.9 %copy-start.17 = (f32[19,10,10,1]{0,2,1,3:T(8,128)S(1)}, f32[19,10,10,1]{0,2,1,3:T(8,128)}, u32[]{:S(2)}) copy-start(f32[19,10,10,1]{0,2,1,3:T(8,128)} %constant.99) | copy-start | bytes 22804
  433.2 9.1 %copy-start.67 = (f32[1,512]{1,0:T(1,128)S(1)}, f32[1,512]{1,0:T(1,128)}, u32[]{:S(2)}) copy-start(f32[1,512]{1,0:T(1,128)} %get-tuple-element.110) | copy-start | bytes 6148
  433.2 9.7 %copy-start.69 = (f32[1,512]{1,0:T(1,128)S(1)}, f32[1,512]{1,0:T(1,128)}, u32[]{:S(2)}) copy-start(f32[1,512]{1,0:T(1,128)} %get-tuple-element.112) | copy-start | bytes 6148
  433.2 10.3 %copy-start.68 = (f32[1,512]{1,0:T(1,128)S(1)}, f32[1,512]{1,0:T(1,128)}, u32[]{:S(2)}) copy-start(f32[1,512]{1,0:T(1,128)} %get-tuple-element.111) | copy-start | bytes 6148
  440.0 6.4 collective-permute-start.8
  445.5 264.4 %collective-permute-start.4 = (f32[2,1,32,512]{3,2,1,0:T(8,128)}, f32[2,1,32,512]{3,2,1,0:T(8,128)}, u32[]{:S(2)}, u32[]{:S(2)}) collective-permute-start(f32[2,1,32,512]{3,2,1,0:T(8,128)} %pad_maximum_fusion.7), channel_id=1, source_target_pairs={{3,0},{0,1},{1,2},{2,3},{7,4},{4,5},{5,6},{6,7},{11,8},{8,9},{9,10... | collective-permute-start | bytes 393224 | tf_op jit(solution)/shard_map/ppermute | solution.py:705
  715.8 6.5 copy-start.24
  715.8 6.5 copy-start.26
  715.8 6.5 copy-start.45
  715.8 6.5 copy-start.46
  717.9 46.8 %all-to-all-start = ((f32[10,30,4,128]{3,1,0,2:T(8,128)}), f32[10,30,4,128]{3,1,0,2:T(8,128)}, u32[]{:S(2)}, u32[]{:S(2)}) async-start(f32[10,30,4,128]{3,1,0,2:T(8,128)} %copy.426), calls=%async_computation | async-start | bytes 1310720 | tf_op jit(solution)/shard_map/all_to_all | solution.py:826
  722.1 110.3 %all-reduce.15.cloned.1.call-start = ((), (), s32[]{:S(2)}) async-start(), calls=%async_computation.3 | async-start | bytes 1048576 | tf_op jit(solution)/shard_map/psum | solution.py:883
  755.6 3.6 copy-start.1
  764.7 4.0 copy-start.4
  764.7 4.0 copy-start.30
  764.7 4.0 copy-start.33
  764.7 4.0 copy-start.63
  (42 other events, 94.9 us)
Sparse Core Ops, SparseCore 0:
  50.2 90.3 all-reduce.16
  494.9 38.8 all-gather.3
  761.6 70.7 all-reduce.14

commit v2 on v1

v2 whole, which is shorter than its diff:
```python
import functools

import jax
import jax.numpy as jnp
import numpy as np
from jax import lax
from jax.experimental import pallas as pl
from jax.experimental.pallas import tpu as pltpu
from jax.sharding import PartitionSpec as P

C = 512
HD = 32
C2 = 256
WIN = 10
SHIFT = 5
SUB = 32
REAL = 25
WT = 128
TOK = 384
NW = 3
GROUP = 4

bf16 = jnp.bfloat16
f32 = jnp.float32
epsilon = 1e-05
masked = -1000000000.0

NN = (((1,), (0,)), ((), ()))
NT = (((1,), (1,)), ((), ()))
TN = (((0,), (0,)), ((), ()))


def split(x):
    high = x.astype(bf16)
    return high, (x - high.astype(f32)).astype(bf16)


def mm(a, b, dims):
    return lax.dot_general(a, b, dims, preferred_element_type=f32)


def mm3(a, b, dims):
    return mm(a[0], b[0], dims) + (mm(a[0], b[1], dims) + mm(a[1], b[0], dims))


def normalized(x):
    center = x - jnp.mean(x, axis=-1, keepdims=True)
    rho = lax.rsqrt(jnp.mean(center * center, axis=-1, keepdims=True) + epsilon)
    return center * rho, rho


def head_masks(dtype):
    lane = lax.broadcasted_iota(jnp.int32, (1, 128), 1) // HD
    return [(lane == h).astype(f32).astype(dtype) for h in range(GROUP)]


def stacked(pair, masks):
    return tuple(jnp.concatenate([part * m for m in masks], axis=0) for part in pair)


def side_by_side(pair):
    return tuple(
        jnp.concatenate([part[h * WT : (h + 1) * WT] for h in range(GROUP)], axis=1)
        for part in pair
    )


def colsum(x):
    return jnp.sum(x, axis=0, keepdims=True)


def attn_fwd_kernel(
    field_ref, gain_ref, shift_ref, wqkv_ref, bqkv_ref, wo_ref, bo_ref, bias_ref,
    regc_ref, regr_ref, valr_ref, valc_ref,
    middle_ref, qkv_ref, p_ref, att_ref, sq_ref,
    nh, nl, mixed,
):
    g = pl.program_id(0)

    @pl.when(g == 0)
    def _():
        xhat, _ = normalized(field_ref[...])
        nh[...], nl[...] = split(xhat * gain_ref[...] + shift_ref[...])
        mixed[...] = jnp.broadcast_to(bo_ref[...], mixed.shape)

    w = jnp.concatenate([wqkv_ref[0, j] for j in range(3)], axis=1)
    qkv = mm3((nh[...], nl[...]), split(w), NN) + bqkv_ref[0]
    lane = lax.broadcasted_iota(jnp.int32, (1, 3 * 128), 1)
    qkv = qkv * jnp.where(lane < 128, HD ** (-0.5), 1.0)
    qkv_ref[0] = qkv
    masks = head_masks(bf16)
    bias = bias_ref[...].reshape(GROUP * WT, WT)
    eye = lax.broadcasted_iota(jnp.int32, (WT, WT), 0) == lax.broadcasted_iota(jnp.int32, (WT, WT), 1)
    for i in range(NW):
        rows = pl.ds(i * WT, WT)
        here = qkv_ref[0, rows, :]
        q4 = stacked(split(here[:, :128]), masks)
        k = split(here[:, 128:256])
        v4 = stacked(split(here[:, 256:]), masks)
        allowed = (regc_ref[rows, :] == regr_ref[i]) & (valr_ref[i] > 0) | eye
        allowed = jnp.concatenate([allowed.astype(f32)] * GROUP, axis=0) > 0
        s = jnp.where(allowed, mm3(q4, k, NT) + bias, masked)
        e = jnp.exp(s - jnp.max(s, axis=-1, keepdims=True))
        p = e / jnp.sum(e, axis=-1, keepdims=True)
        p_ref[0, i] = p
        att_ref[0, rows, :] = mm3(side_by_side(split(p)), v4, NN)
    mixed[...] += mm3(split(att_ref[0]), split(wo_ref[0]), NN)

    @pl.when(g == GROUP - 1)
    def _():
        middle_ref[...] = field_ref[...] + mixed[...]
        sq_ref[...] = colsum(mixed[...] * mixed[...] * valc_ref[...])


def whole(shape):
    return pl.BlockSpec(shape, lambda g: (0,) * len(shape))


def part(shape):
    return pl.BlockSpec((1,) + shape, lambda g: (g,) + (0,) * len(shape))


def sds(*shape):
    return jax.ShapeDtypeStruct(shape, f32)


BIG = pltpu.CompilerParams(vmem_limit_bytes=56 << 20)


def attn_fwd(field, gain, shift, wqkv, bqkv, wo, bo, bias, masks):
    regc, regr, valr, valc = masks
    return pl.pallas_call(
        attn_fwd_kernel,
        grid=(4,),
        in_specs=[
            whole((TOK, C)), whole((1, C)), whole((1, C)), part((3, C, 128)), part((1, 384)),
            part((128, C)), whole((1, C)), pl.BlockSpec((GROUP, WT, WT), lambda g: (g, 0, 0)),
            whole((TOK, 1)), whole((NW, 1, WT)), whole((NW, 1, WT)), whole((TOK, 1)),
        ],
        out_specs=[
            whole((TOK, C)), part((TOK, 384)), part((NW, GROUP * WT, WT)), part((TOK, 128)),
            whole((1, C)),
        ],
        out_shape=[
            sds(TOK, C), sds(4, TOK, 384), sds(4, NW, GROUP * WT, WT), sds(4, TOK, 128), sds(1, C),
        ],
        scratch_shapes=[pltpu.VMEM((TOK, C), bf16), pltpu.VMEM((TOK, C), bf16), pltpu.VMEM((TOK, C), f32)],
        compiler_params=BIG,
        name="attn_fwd",
    )(field, gain, shift, wqkv, bqkv, wo, bo, bias, regc, regr, valr, valc)


def mlp_fwd_kernel(
    mid_ref, gain_ref, shift_ref, we_ref, be_ref, ws_ref, bs_ref, valc_ref,
    out_ref, hid_ref, slope_ref, sq_ref, sqo_ref,
    nh, nl, branch,
):
    g = pl.program_id(0)

    @pl.when(g == 0)
    def _():
        xhat, _ = normalized(mid_ref[...])
        nh[...], nl[...] = split(xhat * gain_ref[...] + shift_ref[...])
        branch[...] = jnp.broadcast_to(bs_ref[...], branch.shape)

    pre = mm3((nh[...], nl[...]), split(we_ref[0]), NN) + be_ref[0]
    phi = 0.5 * (1.0 + lax.erf(pre * (2 ** -0.5)))
    hidden = pre * phi
    hid_ref[0] = hidden
    slope_ref[0] = phi + pre * (jnp.exp(-0.5 * pre * pre) * ((2 * np.pi) ** -0.5))
    branch[...] += mm3(split(hidden), split(ws_ref[0]), NN)

    @pl.when(g == 3)
    def _():
        out = mid_ref[...] + branch[...]
        out_ref[...] = out
        sq_ref[...] = colsum(branch[...] * branch[...] * valc_ref[...])
        sqo_ref[...] = colsum(out * out * valc_ref[...])


def mlp_fwd(mid, gain, shift, we, be, ws, bs, valc):
    return pl.pallas_call(
        mlp_fwd_kernel,
        grid=(4,),
        in_specs=[
            whole((TOK, C)), whole((1, C)), whole((1, C)), part((C, 512)), part((1, 512)),
            part((512, C)), whole((1, C)), whole((TOK, 1)),
        ],
        out_specs=[whole((TOK, C)), part((TOK, 512)), part((TOK, 512)), whole((1, C)), whole((1, C))],
        out_shape=[sds(TOK, C), sds(4, TOK, 512), sds(4, TOK, 512), sds(1, C), sds(1, C)],
        scratch_shapes=[pltpu.VMEM((TOK, C), bf16), pltpu.VMEM((TOK, C), bf16), pltpu.VMEM((TOK, C), f32)],
        compiler_params=BIG,
        name="mlp_fwd",
    )(mid, gain, shift, we, be, ws, bs, valc)


def norm_back(x, gain, grad_y):
    xhat, rho = normalized(x)
    gh = grad_y * gain
    grad_x = rho * (
        gh - jnp.mean(gh, axis=-1, keepdims=True) - xhat * jnp.mean(gh * xhat, axis=-1, keepdims=True)
    )
    return grad_x, colsum(grad_y * xhat), colsum(grad_y)


MESH = pl.DeviceIdType.MESH
ANY = pl.BlockSpec(memory_space=pl.ANY)
VM = pl.BlockSpec(memory_space=pltpu.VMEM)


def here():
    sp, tp = lax.axis_index("sp"), lax.axis_index("tp")
    return sp, tp, (sp, tp ^ 1), (sp, tp ^ 2), (sp ^ 1, tp)


def meet(peers):
    barrier = pltpu.get_barrier_semaphore()
    for peer in peers:
        pl.semaphore_signal(barrier, inc=1, device_id=peer, device_id_type=MESH)
    pl.semaphore_wait(barrier, len(peers))


def push(src, dst, send, recv, peer):
    return pltpu.make_async_remote_copy(
        src_ref=src, dst_ref=dst, send_sem=send, recv_sem=recv, device_id=peer, device_id_type=MESH
    )


def gather_kernel(axes, count, *refs):
    ins, outs = refs[:count], refs[count : 2 * count]
    send, recv, local = refs[2 * count :]
    sp, tp, sib, across, beside = here()
    par = sp & 1
    meet((sib, across, beside))

    def cut(ref, axis, half):
        if axis is None:
            return ref
        size = ref.shape[axis] // 2
        index = [slice(None)] * len(ref.shape)
        index[axis] = pl.ds(pl.multiple_of(half * size, size), size)
        return ref.at[tuple(index)]

    def own(i):
        return pltpu.make_async_copy(ins[i], outs[i].at[tp], local.at[i])

    def to_sib(i):
        return push(ins[i], outs[i].at[tp], send.at[0, i], recv.at[0, i], sib)

    def to_across(i):
        return push(
            cut(ins[i], axes[i], par), cut(outs[i].at[tp], axes[i], par), send.at[1, i], recv.at[1, i], across
        )

    def far(i, half):
        return cut(outs[i].at[tp ^ 2], axes[i], half)

    def to_beside(i):
        return push(far(i, par), far(i, par), send.at[2, i], recv.at[2, i], beside)

    def on_first(i):
        return push(far(i, par), far(i, par), send.at[3, i], recv.at[3, i], sib)

    def on_second(i):
        return push(far(i, 1 - par), far(i, 1 - par), send.at[4, i], recv.at[4, i], sib)

    for i in range(count):
        to_across(i).start()
        to_sib(i).start()
        own(i).start()
    for i in range(count + 1):
        if i < count:
            to_across(i).wait_recv()
            on_first(i).start()
            if axes[i] is not None:
                to_beside(i).start()
        if i > 0 and axes[i - 1] is not None:
            to_beside(i - 1).wait_recv()
            on_second(i - 1).start()
    for i in range(count):
        own(i).wait()
        to_sib(i).wait()
        to_across(i).wait_send()
        on_first(i).wait()
        if axes[i] is not None:
            to_beside(i).wait_send()
            on_second(i).wait()


def gather_all(arrays, axes, ident):
    count = len(arrays)
    return pl.pallas_call(
        functools.partial(gather_kernel, axes, count),
        in_specs=[ANY] * count,
        out_specs=[ANY] * count,
        out_shape=[jax.ShapeDtypeStruct((4,) + a.shape, a.dtype) for a in arrays],
        scratch_shapes=[
            pltpu.SemaphoreType.DMA((5, count)), pltpu.SemaphoreType.DMA((5, count)),
            pltpu.SemaphoreType.DMA((count,)),
        ],
        compiler_params=pltpu.CompilerParams(collective_id=ident, has_side_effects=True),
        name="gather",
    )(*arrays)


ROWS = 512
HALF = ROWS // 2
MLP_ROWS, ATT_ROWS = 4096, 2560
MLP_CH, ATT_CH = MLP_ROWS // ROWS, ATT_ROWS // ROWS
FULL_CH = 2 * (MLP_CH + ATT_CH)
CHUNKS = FULL_CH + 2
BASE = (0, MLP_ROWS, MLP_ROWS + ATT_ROWS, 2 * MLP_ROWS + ATT_ROWS)
FIRST = 4
AG_STEP = 15
MERGE_STEP = 20
TINY_STEP = 25
STEPS = FIRST + CHUNKS + 6
TINY = 40
COLS = [(0, 0, 0, 1), (0, 1, 1, 0), (1, 0, 1, 1), (1, 1, 2, 0), (2, 0, 2, 1)]


def at(w, sr, sc):
    return pl.ds(w * WT + sr * 64 + sc * SUB, SUB)


def bwd_kernel(n, *refs):
    (
        cot_ref, mid_ref, field_ref, g1_ref, b1_ref, g2_ref, b2_ref, we_ref, ws_ref, wqkv_ref, wo_ref,
        hid_ref, slope_ref, qkv_ref, p_ref, att_ref, sq_ref, q_ref, mw_ref, vec_ref, mg_ref, stat_ref, f0_ref,
    ) = refs[:23]
    pack, gall, exall, out_ref, gq_ref, tout_ref = refs[23:29]
    (
        nth, ntl, gh, gl, acc, dqkv, gf, gbuf, moved, ext, extin, qbuf,
        loc, pair, yr, zr, fin, ta, tx, tz,
        gsem, mvs, mvr, ags, agr, agl, msem, ss, rs, zs, zq, fs, fq, ls, os, ts, tq, tzs, tzq,
    ) = refs[29:]
    step = pl.program_id(0)
    dmw, gqbuf = moved.at[pl.ds(0, 256)], dqkv.at[:, pl.ds(0, 256)]
    sp, tp, sib, across, beside = here()
    par, mine = sp & 1, sp // 2
    m = n // 2
    piece = HALF // m
    up, right = lax.rem(sp + 1, n), lax.rem(tp + 1, 4)
    down, left = lax.rem(sp + n - 1, n), lax.rem(tp + 3, 4)

    def member(j):
        return lax.rem(mine + j, m)

    def device(q):
        return (q * 2 + par, tp)

    @pl.when(step == 0)
    def _():
        barrier = pltpu.get_barrier_semaphore()
        near = [sib, across, beside, (up, tp), (down, tp), (sp, right), (sp, left), (up, right), (down, left)]
        for peer in near:
            pl.semaphore_signal(barrier, inc=1, device_id=peer, device_id_type=MESH)

        @pl.loop(1, m)
        def _(j):
            pl.semaphore_signal(barrier, inc=1, device_id=device(member(j)), device_id_type=MESH)

        pl.semaphore_wait(barrier, len(near) + m - 1)
        ta[...] = jnp.zeros_like(ta)
        ta[0, 28:36, :] = sq_ref[...]
        gf[...] = cot_ref[...]

    def packed(kind, t):
        size = MLP_ROWS if kind % 2 == 0 else ATT_ROWS
        slot = t % 2
        return pltpu.make_async_copy(
            gbuf.at[slot, pl.ds(0, size)], pack.at[t, pl.ds(BASE[kind], size)], gsem.at[slot]
        )

    def moves():
        todo = [
            (at(2, 0, 1), at(0, 1, 0), (sp, right)),
            (at(2, 1, 1), at(0, 0, 0), (up, right)),
        ]
        for w0, s0, w1, s1 in COLS:
            todo.append((at(w0, 1, s0), at(w1, 0, s1), (up, tp)))
        return [push(acc.at[src], moved.at[dst], mvs.at[i], mvr.at[i], peer) for i, (src, dst, peer) in enumerate(todo)]

    def kept():
        for w0, s0, w1, s1 in COLS:
            moved[at(w1, 1, s1), :] = acc[at(w0, 0, s0), :]

    for kind, b in ((0, 1), (2, 0)):
        lo = 4 * kind

        @pl.when((step >= lo) & (step < lo + 4))
        def _(kind=kind, b=b, lo=lo):
            t = step - lo

            @pl.when(step == lo)
            def _():
                if b == 0:
                    for copy in moves():
                        copy.wait()
                    gf[...] = moved[...]
                xhat, _ = normalized(mid_ref[0])
                nth[...], ntl[...] = split((xhat * g2_ref[b] + b2_ref[b]).T)
                gh[...], gl[...] = split(gf[...])
                acc[...] = jnp.zeros_like(acc)

            slot = t % 2
            grad = (gh[...], gl[...])
            dws = mm3(split(hid_ref[0].T), grad, NN)
            for j in range(4):
                gbuf[slot, 2048 + j * 512 : 2560 + j * 512, :] = dws[:, j * 128 : (j + 1) * 128]
            dpre = mm3(grad, split(ws_ref[0]), NT) * slope_ref[0]
            ta[0, pl.ds(12 + b * 4 + t, 1), :] = colsum(dpre)
            pair_ = split(dpre)
            dwe = mm3((nth[...], ntl[...]), pair_, NN)
            for j in range(4):
                gbuf[slot, j * 512 : (j + 1) * 512, :] = dwe[:, j * 128 : (j + 1) * 128]
            acc[...] += mm3(pair_, split(we_ref[0]), NT)

            @pl.when(t > 0)
            def _():
                packed(kind, t - 1).wait()

            packed(kind, t).start()

            @pl.when(t == 3)
            def _():
                grad_x, dgain, dshift = norm_back(mid_ref[0], g2_ref[b], acc[...])
                ta[0, 6 + 3 * b : 7 + 3 * b, :] = dgain
                ta[0, 7 + 3 * b : 8 + 3 * b, :] = dshift
                ta[0, 8 + 3 * b : 9 + 3 * b, :] = colsum(gf[...])
                gf[...] = gf[...] + grad_x
                packed(kind, 3).wait()

    for kind, b in ((1, 1), (3, 0)):
        lo = 4 * kind

        @pl.when((step >= lo) & (step < lo + 4))
        def _(kind=kind, b=b, lo=lo):
            t = step - lo

            @pl.when(step == lo)
            def _():
                xhat, _ = normalized(field_ref[0])
                nth[...], ntl[...] = split((xhat * g1_ref[b] + b1_ref[b]).T)
                gh[...], gl[...] = split(gf[...])
                acc[...] = jnp.zeros_like(acc)

            slot = t % 2
            grad = (gh[...], gl[...])
            dwo = mm3(split(att_ref[0].T), grad, NN)
            for j in range(4):
                gbuf[slot, 1536 + j * 128 : 1664 + j * 128, :] = dwo[:, j * 128 : (j + 1) * 128]
            dout = mm3(grad, split(wo_ref[0]), NT)
            masks = head_masks(bf16)
            dbias = jnp.zeros((GROUP * WT, WT), f32)
            for i in range(NW):
                rows = slice(i * WT, (i + 1) * WT)
                seen = qkv_ref[0, pl.ds(i * WT, WT), :]
                q4 = stacked(split(seen[:, :128]), masks)
                k4 = stacked(split(seen[:, 128:256]), masks)
                v = split(seen[:, 256:])
                p = p_ref[0, i]
                do4 = stacked(split(dout[rows]), masks)
                dp = mm3(do4, v, NT)
                ds = p * (dp - jnp.sum(p * dp, axis=-1, keepdims=True))
                dbias = dbias + ds
                dpair = split(ds)
                dqkv[pl.ds(i * WT, WT), 0:128] = mm3(side_by_side(dpair), k4, NN) * HD ** (-0.5)
                dqkv[pl.ds(i * WT, WT), 128:256] = mm3(dpair, q4, TN)
                dqkv[pl.ds(i * WT, WT), 256:384] = mm3(split(p), do4, TN)
            gbuf[slot, 2048:2560, :] = dbias
            grads = dqkv[...]
            ta[0, pl.ds(20 + b * 4 + t, 1), 0:384] = colsum(grads)
            pair_ = split(grads)
            dw = mm3((nth[...], ntl[...]), pair_, NN)
            for j in range(3):
                gbuf[slot, j * 512 : (j + 1) * 512, :] = dw[:, j * 128 : (j + 1) * 128]
            w = jnp.concatenate([wqkv_ref[0, j] for j in range(3)], axis=1)
            acc[...] += mm3(pair_, split(w), NT)

            @pl.when(t > 0)
            def _():
                packed(kind, t - 1).wait()

            packed(kind, t).start()

            @pl.when(t == 3)
            def _():
                grad_x, dgain, dshift = norm_back(field_ref[0], g1_ref[b], acc[...])
                ta[0, 3 * b : 1 + 3 * b, :] = dgain
                ta[0, 1 + 3 * b : 2 + 3 * b, :] = dshift
                ta[0, 2 + 3 * b : 3 + 3 * b, :] = colsum(gf[...])
                acc[...] = gf[...] + grad_x
                if b == 1:
                    for copy in moves():
                        copy.start()
                    kept()
                packed(kind, 3).wait()

    def ag(k, src, dst, peer, which):
        return push(src, dst, ags.at[which, k], agr.at[which, k], peer)

    def ag_copies(k):
        own = (acc, ext)
        whole_ = (gall, exall)
        return [
            ag(k, own[w], whole_[w].at[tp], (sib, across)[k], w) if k < 2
            else ag(k, whole_[w].at[tp ^ 2], whole_[w].at[tp ^ 2], sib, w)
            for w in range(2)
        ]

    @pl.when(step == AG_STEP)
    def _():
        m2 = jnp.sum(acc[...] * (f0_ref[...] - vec_ref[1:2, :]), axis=-1, keepdims=True)
        lane = lax.broadcasted_iota(jnp.int32, (TOK, 128), 1)
        tall = jnp.where(lane == 2, m2, stat_ref[...])
        ext[...] = tall.T[0:8, :]
        for k in range(2):
            for copy in ag_copies(k):
                copy.start()

    @pl.when(step == MERGE_STEP - 1)
    def _():
        for copy in ag_copies(1):
            copy.wait()
        for copy in ag_copies(2):
            copy.start()
        for copy in ag_copies(0):
            copy.wait()

    @pl.when((step >= MERGE_STEP) & (step < MERGE_STEP + 4))
    def _():
        i = step - MERGE_STEP
        t = tp ^ i

        @pl.when(i == 2)
        def _():
            for copy in ag_copies(2):
                copy.wait()

        fetch = [pltpu.make_async_copy(q_ref.at[t], qbuf, msem.at[0])]
        fetch[0].start()

        @pl.when(i == 0)
        def _():
            dmw[...] = jnp.zeros((256, C), f32)
            gf[...] = acc[...]
            extin[...] = ext[...]

        @pl.when(i > 0)
        def _():
            two = [
                pltpu.make_async_copy(gall.at[t], gf, msem.at[1]),
                pltpu.make_async_copy(exall.at[t], extin, msem.at[2]),
            ]
            for copy in two:
                copy.start()
            for copy in two:
                copy.wait()

        fetch[0].wait()
        wide = jnp.concatenate([extin[...], jnp.zeros((120, TOK), f32)], axis=0).T
        mean, inv, m2 = wide[:, 0:1], wide[:, 1:2], wide[:, 2:3]
        full = gf[...]
        m1 = jnp.sum(full * vec_ref[0:1, :], axis=-1, keepdims=True) / (4.0 * C2)
        m2 = m2 / (4.0 * C2)
        fpair = split(full)
        xhat = (qbuf[...] - mean) * inv
        gmerged = mm3(fpair, split(mw_ref[...]), NT)
        dmw[...] += mm3(split((xhat * mg_ref[0:1, :] + mg_ref[1:2, :]).T), fpair, NN)
        row = pl.ds(36 + tp, 1)
        ta[0, row, 0:256] += colsum(gmerged * xhat)
        ta[0, row, 256:512] += colsum(gmerged)

        @pl.when(i > 0)
        def _():
            pltpu.make_async_copy(gqbuf, gq_ref.at[t], msem.at[3]).wait()

        gqbuf[...] = inv * (gmerged * mg_ref[0:1, :] - m1 - xhat * m2)
        pltpu.make_async_copy(gqbuf, gq_ref.at[t], msem.at[3]).start()

        @pl.when(i == 3)
        def _():
            pltpu.make_async_copy(gqbuf, gq_ref.at[t], msem.at[3]).wait()
            for k in range(2):
                for j in range(2):
                    low = (2 * k + j) * 128
                    pair[FULL_CH + k, 0, j * 256 : (j + 1) * 256, :] = dmw[:, low : low + 128]

    def rows(c):
        return pl.ds(pl.multiple_of(c * ROWS, ROWS), ROWS)

    def load(c, k):
        return pltpu.make_async_copy(pack.at[tp ^ (2 * k), rows(c)], loc.at[c % 2, k], ls.at[c % 2, k])

    def swap(c, k):
        return push(pack.at[tp ^ 1 ^ (2 * k), rows(c)], pair.at[c, k], ss.at[k, c], rs.at[k, c], sib)

    def cross(c):
        return push(pair.at[c, 1], fin.at[c], ss.at[2, c], rs.at[2, c], across)

    def halves(h):
        return pl.ds(pl.multiple_of(h * HALF, HALF), HALF)

    def side(c):
        return push(pair.at[c, 0, halves(1 - par)], yr.at[c], ss.at[3, c], rs.at[3, c], beside)

    def bit(q):
        return pl.ds(pl.multiple_of(q * piece, piece), piece)

    def spread(c, q, slot):
        return push(yr.at[c, bit(q)], zr.at[c, slot], zs.at[c % 4, q], zq.at[c, slot], device(q))

    def place(q):
        return pl.ds(pl.multiple_of(par * HALF + q * piece, piece), piece)

    def share(c, q, slot):
        return push(fin.at[c, place(slot)], fin.at[c, place(slot)], fs.at[c % 4, q], fq.at[c, slot], device(q))

    def back(c):
        return push(fin.at[c, halves(par)], fin.at[c, halves(par)], ss.at[4, c], rs.at[4, c], beside)

    def write(c):
        return pltpu.make_async_copy(fin.at[c], out_ref.at[rows(c)], os.at[c])

    def tiny(k, peer):
        return push(ta.at[k], tx.at[k], ts.at[k], tq.at[k], peer)

    def tiny_z(q, slot):
        return push(ta.at[3], tz.at[slot], tzs.at[q], tzq.at[slot], device(q))

    def stage(lag, first, last):
        c = step - FIRST - lag
        return c, (c >= first) & (c < last)

    peers = (sib, across, beside)
    for k in range(4):

        @pl.when(step == TINY_STEP + 2 * k)
        def _(k=k):
            if k > 0:
                tiny(k - 1, peers[k - 1]).wait()
                ta[k] = ta[k - 1] + tx[k - 1]
            if k < 3:
                tiny(k, peers[k]).start()
            else:
                tz[mine] = ta[3]

                @pl.loop(1, m)
                def _(j):
                    tiny_z(member(j), mine).start()

    c0, on0 = stage(0, 0, FULL_CH)

    @pl.when(on0)
    def _():
        for k in (1, 0):
            swap(c0, k).start()
            load(c0, k).start()

    c1, on1 = stage(1, 0, FULL_CH)

    @pl.when(on1)
    def _():
        for k in (1, 0):
            load(c1, k).wait()
            swap(c1, k).wait_recv()
            pair[c1, k] = pair[c1, k] + loc[c1 % 2, k]
            if k == 1:
                cross(c1).start()

    c2, on2 = stage(2, 0, CHUNKS)

    @pl.when(on2)
    def _():
        @pl.when(c2 < FULL_CH)
        def _():
            cross(c2).wait_recv()
            pair[c2, 0] = pair[c2, 0] + fin[c2]

        side(c2).start()

    c3, on3 = stage(3, 0, CHUNKS)

    @pl.when(on3)
    def _():
        side(c3).wait_recv()
        yr[c3] = yr[c3] + pair[c3, 0, halves(par)]

        @pl.loop(1, m)
        def _(j):
            spread(c3, member(j), mine).start()

    c4, on4 = stage(4, 0, CHUNKS)

    @pl.when(on4)
    def _():
        fin[c4, place(mine)] = yr[c4, bit(mine)]

        @pl.loop(1, m)
        def _(j):
            spread(c4, member(j), member(j)).wait_recv()
            fin[c4, place(mine)] = fin[c4, place(mine)] + zr[c4, member(j)]

        @pl.loop(1, m)
        def _(j):
            share(c4, member(j), mine).start()

    c5, on5 = stage(5, 0, CHUNKS)

    @pl.when(on5)
    def _():
        @pl.loop(1, m)
        def _(j):
            share(c5, member(j), member(j)).wait_recv()
            spread(c5, member(j), mine).wait_send()

        back(c5).start()

    c6, on6 = stage(6, 0, CHUNKS)

    @pl.when(on6)
    def _():
        back(c6).wait_recv()
        write(c6).start()

        @pl.loop(1, m)
        def _(j):
            share(c6, member(j), mine).wait_send()

    @pl.when(step == STEPS - 1)
    def _():
        @pl.loop(1, m)
        def _(j):
            tiny_z(member(j), member(j)).wait_recv()
            tiny_z(member(j), mine).wait_send()

        total = tz[0]
        for q in range(1, m):
            total = total + tz[q]
        tout_ref[...] = total

        @pl.loop(0, CHUNKS)
        def _(c):
            @pl.when(c < FULL_CH)
            def _():
                for k in range(2):
                    swap(c, k).wait_send()
                cross(c).wait_send()

            side(c).wait_send()
            back(c).wait_send()
            write(c).wait()


def backward(n, args, ident):
    m = n // 2
    dma = pltpu.SemaphoreType.DMA

    def fixed(shape):
        return pl.BlockSpec(shape, lambda s: (0,) * len(shape), pipeline_mode=pl.Buffered(1))

    def mlp_at(s):
        return jnp.where(s < 4, 4 + s, jnp.where(s < 8, 0, jnp.where(s < 12, s - 8, 3)))

    def att_at(s):
        return jnp.where(s < 4, 4, jnp.where(s < 8, s, jnp.where(s < 12, 0, jnp.where(s < 16, s - 12, 3))))

    def by(index, shape, mode=None):
        zeros = (0,) * len(shape)
        return pl.BlockSpec((1,) + shape, lambda s: (index(s),) + zeros, pipeline_mode=mode)

    one = pl.Buffered(1)
    lanes = (CHUNKS, ROWS, 128)
    in_specs = [
        fixed((TOK, C)), by(lambda s: jnp.where(s < 4, 1, 0), (TOK, C), one),
        by(lambda s: jnp.where(s < 8, 1, 0), (TOK, C), one),
        fixed((2, 1, C)), fixed((2, 1, C)), fixed((2, 1, C)), fixed((2, 1, C)),
        by(mlp_at, (C, 512)), by(mlp_at, (512, C)), by(att_at, (3, C, 128)), by(att_at, (128, C)),
        by(mlp_at, (TOK, 512)), by(mlp_at, (TOK, 512)), by(att_at, (TOK, 384)),
        by(att_at, (NW, GROUP * WT, WT)), by(att_at, (TOK, 128)),
        fixed((8, C)), ANY, fixed((256, C)), fixed((8, C)), fixed((8, 256)), fixed((TOK, 128)), fixed((TOK, C)),
    ]
    return pl.pallas_call(
        functools.partial(bwd_kernel, n),
        grid=(STEPS,),
        in_specs=in_specs,
        out_specs=[ANY, ANY, ANY, ANY, ANY, fixed((TINY, C))],
        out_shape=[
            sds(4, FULL_CH * ROWS, 128), sds(4, TOK, C), sds(4, 8, TOK), sds(CHUNKS * ROWS, 128),
            sds(4, TOK, 256), sds(TINY, C),
        ],
        scratch_shapes=[
            pltpu.VMEM((C, TOK), bf16), pltpu.VMEM((C, TOK), bf16), pltpu.VMEM((TOK, C), bf16),
            pltpu.VMEM((TOK, C), bf16), pltpu.VMEM((TOK, C), f32), pltpu.VMEM((TOK, 384), f32),
            pltpu.VMEM((TOK, C), f32), pltpu.VMEM((2, MLP_ROWS, 128), f32), pltpu.VMEM((TOK, C), f32),
            pltpu.VMEM((8, TOK), f32), pltpu.VMEM((8, TOK), f32), pltpu.VMEM((TOK, 256), f32),
            pltpu.VMEM((2, 2, ROWS, 128), f32), pltpu.VMEM((CHUNKS, 2, ROWS, 128), f32),
            pltpu.VMEM((CHUNKS, HALF, 128), f32), pltpu.VMEM((CHUNKS, m, HALF // m, 128), f32),
            pltpu.VMEM(lanes, f32), pltpu.VMEM((4, TINY, C), f32), pltpu.VMEM((3, TINY, C), f32),
            pltpu.VMEM((m, TINY, C), f32),
            dma((2,)), dma((7,)), dma((7,)), dma((2, 3)), dma((2, 3)), dma((2,)), dma((4,)),
            dma((5, CHUNKS)), dma((5, CHUNKS)), dma((4, m)), dma((CHUNKS, m)), dma((4, m)),
            dma((CHUNKS, m)), dma((2, 2)), dma((CHUNKS,)), dma((3,)), dma((3,)), dma((m,)), dma((m,)),
        ],
        compiler_params=pltpu.CompilerParams(
            collective_id=ident, has_side_effects=True, vmem_limit_bytes=60 << 20,
            dimension_semantics=("arbitrary",),
        ),
        name="backward",
    )(*args)


def column_pick():
    pick = np.zeros((19, WIN, WIN), np.float32)
    for a in range(WIN):
        for b in range(WIN):
            pick[a - b + WIN - 1, a, b] = 1.0
    return pick


def row_pick():
    pick = np.zeros((19, WIN, WIN, WIN, 2, 2, SUB), np.float32)
    for pr in range(WIN):
        for qr in range(WIN):
            for qc in range(WIN):
                pick[pr - qr + WIN - 1, qc, pr, 0, qr // 5, qc // 5, (qr % 5) * 5 + qc % 5] = 1.0
    return pick[:, :, :, 0].reshape(190, WIN * WT)


def bias_of(table):
    heads = table.shape[0]
    grid = table.reshape(heads, 19, 19)
    columns = jnp.einsum("hrd,dab->harb", grid, jnp.asarray(column_pick()), precision="highest")
    rows = jnp.dot(columns.reshape(heads * WIN, 190), jnp.asarray(row_pick()), precision="highest")
    rows = rows.reshape(heads, 2, 5, 2, 5, WT).transpose(0, 3, 1, 4, 2, 5)
    rows = rows.reshape(heads, 4, REAL, WT)
    return jnp.pad(rows, ((0, 0), (0, 0), (0, SUB - REAL), (0, 0))).reshape(heads, WT, WT)


def table_of(dbias):
    heads = dbias.shape[0]
    rows = dbias.reshape(heads, 4, SUB, WT)[:, :, :REAL].reshape(heads, 2, 2, 5, 5, WT)
    rows = rows.transpose(0, 2, 4, 1, 3, 5).reshape(heads * WIN, WIN * WT)
    columns = lax.dot_general(rows, jnp.asarray(row_pick()), NT, precision="highest")
    columns = columns.reshape(heads, WIN, 19, WIN)
    return jnp.einsum("harb,dab->hrd", columns, jnp.asarray(column_pick()), precision="highest")


def shift_along(x, axis, distance):
    count = lax.axis_size(axis)
    return lax.ppermute(x, axis, [((i - distance) % count, i) for i in range(count)])


def grid_of(tokens):
    return tokens.reshape(NW, 2, 2, SUB, -1).transpose(1, 0, 2, 3, 4).reshape(2, 6, SUB, -1)


def tokens_of(grid):
    return grid.reshape(2, NW, 2, SUB, -1).transpose(1, 0, 2, 3, 4).reshape(TOK, -1)


def shifted(tokens):
    grid = grid_of(tokens)
    right = shift_along(grid[:, :1], "tp", -1)
    grid = jnp.concatenate([grid[:, 1:], right], axis=1)
    below = shift_along(grid[:1], "sp", -1)
    return tokens_of(jnp.concatenate([grid[1:], below], axis=0))


def unshifted(tokens):
    grid = grid_of(tokens)
    above = shift_along(grid[1:], "sp", 1)
    grid = jnp.concatenate([above, grid[:1]], axis=0)
    left = shift_along(grid[:, 5:], "tp", 1)
    return tokens_of(jnp.concatenate([left, grid[:, :5]], axis=1))


def to_order(natural):
    values = natural.reshape(2, 5, NW, 2, 5, -1).transpose(2, 0, 3, 1, 4, 5).reshape(NW, 2, 2, REAL, -1)
    values = jnp.pad(values, ((0, 0), (0, 0), (0, 0), (0, SUB - REAL), (0, 0)))
    return values.reshape(TOK, -1)


def to_natural(tokens):
    values = tokens.reshape(NW, 2, 2, SUB, -1)[:, :, :, :REAL]
    values = values.reshape(NW, 2, 2, 5, 5, -1).transpose(1, 3, 0, 2, 4, 5)
    return values.reshape(10, 30, -1)


def shards(
    patches, merge_gain, merge_shift, merge_weight, first_gain, first_shift, input_weight,
    input_bias, position_table, output_weight, output_bias, second_gain, second_shift,
    expand_weight, expand_bias, shrink_weight, shrink_bias, page_map, valid_flags, cotangent,
):
    sp_count = lax.axis_size("sp")
    tp = lax.axis_index("tp")
    sp = lax.axis_index("sp")
    full_channels = 4.0 * C2

    small = jnp.concatenate(
        [input_bias.reshape(-1), expand_bias.reshape(-1), position_table.transpose(0, 2, 1).reshape(-1)]
    )
    small = jnp.pad(small, (0, 40 * 128 - small.shape[0])).reshape(40, 128)
    wqkv, wo, we, ws = [], [], [], []
    arrays = [small]
    for b in range(2):
        arrays += [input_weight[b].transpose(1, 0, 2), output_weight[b], expand_weight[b], shrink_weight[b]]
    full = gather_all(arrays, [None] + [1, 0, 0, 0] * 2, 1)
    small = full[0].reshape(4, 40 * 128)
    wqkv, wo, we, ws = full[1::4], full[2::4], full[3::4], full[4::4]
    bqkv, be, bias = [], [], []
    for b in range(2):
        ib = small[:, b * 256 : (b + 1) * 256].reshape(4, 2, 128)
        bqkv.append(jnp.concatenate([ib[:, :1], jnp.zeros((4, 1, 128), f32), ib[:, 1:]], axis=1).reshape(4, 1, 384))
        be.append(small[:, 512 + b * 512 : 1024 + b * 512].reshape(4, 1, 512))
    tables = small[:, 1536 : 1536 + 2888].reshape(4, 2, 4, 361).transpose(1, 0, 2, 3).reshape(2, 16, 361)
    bias = [bias_of(tables[b]) for b in range(2)]

    valid = valid_flags.astype(f32)
    vgrid = valid.reshape(2, 5, 24, 5).transpose(0, 2, 1, 3).reshape(2, 24, REAL)
    vgrid = jnp.pad(vgrid, ((0, 0), (0, 0), (0, SUB - REAL)))
    below = shift_along(vgrid[:1], "sp", -1)
    vshift = jnp.roll(jnp.concatenate([vgrid[1:], below], axis=0), -1, axis=1)
    own = lambda grid: lax.dynamic_slice_in_dim(grid, 6 * tp, 6, 1)
    vtok = [tokens_of(own(vgrid)[..., None]), tokens_of(own(vshift)[..., None])]
    pages = jnp.concatenate([page_map, page_map[:1]], axis=0)
    pages = jnp.concatenate([pages, pages[:, :1]], axis=1)
    pages = lax.dynamic_slice(pages, (sp, 3 * tp), (2, 4))
    page = jnp.stack([pages[:, :3], pages[:, 1:]], axis=2).transpose(1, 0, 2)
    wrap_row = (jnp.arange(2) == 1) & (sp == sp_count - 1)
    wrap_col = (jnp.arange(2) == 1)[None, :] & (jnp.arange(NW) == NW - 1)[:, None] & (tp == 3)
    region = page * 4 + 2 * wrap_row[None, :, None].astype(jnp.int32) + wrap_col[:, None, :].astype(jnp.int32)
    region = jnp.broadcast_to(region[..., None], (NW, 2, 2, SUB)).reshape(TOK)
    regions = [jnp.zeros((TOK,), jnp.int32), region]
    mask_args = [
        (regions[b].reshape(TOK, 1), regions[b].reshape(NW, 1, WT), vtok[b].reshape(NW, 1, WT), vtok[b])
        for b in range(2)
    ]

    gain = merge_gain.reshape(2, 2, 64).transpose(1, 0, 2).reshape(256)
    offset = merge_shift.reshape(2, 2, 64).transpose(1, 0, 2).reshape(256)
    weight = merge_weight.reshape(2, 2, 64, C).transpose(1, 0, 2, 3).reshape(256, C)
    quads = patches.reshape(2, 5, 2, 4, NW, 2, 5, 128).transpose(3, 4, 0, 5, 1, 6, 2, 7).reshape(4, NW, 4, REAL, 256)
    quads = jnp.pad(quads, ((0, 0), (0, 0), (0, 0), (0, SUB - REAL), (0, 0))).reshape(4, TOK, 256)
    partial = jnp.einsum("tpk,kd->tpd", quads * gain, weight, precision="high")
    moment = lax.psum((jnp.sum(quads, axis=2), jnp.sum(quads * quads, axis=2)), "tp")
    vecs = lax.psum((jnp.dot(gain, weight, precision="highest"), jnp.dot(offset, weight, precision="highest")), "tp")
    mean = moment[0] / full_channels
    inverse = lax.rsqrt(moment[1] / full_channels - mean * mean + epsilon)
    total = lax.psum_scatter(partial, "tp", scatter_dimension=0, tiled=False)
    mean, inverse = mean[tp][:, None], inverse[tp][:, None]
    field = inverse * (total - mean * vecs[0]) + vecs[1]
    field0 = field
    stat = jnp.concatenate([mean, inverse, jnp.zeros((TOK, 126), f32)], axis=1)

    squares = []
    saved = []
    row = lambda x: x.reshape(1, C)
    for b in range(2):
        if b == 1:
            field = shifted(field)
        middle, qkv, p, att, sq = attn_fwd(
            field, row(first_gain[b]), row(first_shift[b]), wqkv[b], bqkv[b], wo[b], row(output_bias[b]),
            bias[b], mask_args[b],
        )
        out, hid, slope, sqb, sqo = mlp_fwd(
            middle, row(second_gain[b]), row(second_shift[b]), we[b], be[b], ws[b], row(shrink_bias[b]), vtok[b]
        )
        squares += [sq, sqb]
        saved.append((field, qkv, p, att, middle, hid, slope))
        field = out
    squares.append(sqo)
    out_nat = to_natural(unshifted(field))
    output = lax.all_to_all(out_nat.reshape(10, 30, 4, 128), "tp", 2, 1, tiled=True).reshape(10, 120, 128)

    cot = lax.all_to_all(cotangent.reshape(10, 120, 1, 128), "tp", 1, 2, tiled=True).reshape(10, 30, C)
    cot = shifted(to_order(cot))
    count = jnp.pad(jnp.sum(vtok[0]).reshape(1, 1), ((0, 0), (0, C - 1)))
    squares = jnp.concatenate(squares + [count, jnp.zeros((2, C), f32)], axis=0)
    both = lambda i: jnp.concatenate([saved[0][i], saved[1][i]], axis=0)
    pile = lambda i: jnp.stack([saved[0][i], saved[1][i]], axis=0)
    join = lambda xs: jnp.concatenate(xs, axis=0)
    three = lambda x: x.reshape(2, 1, C)
    zero = jnp.zeros((6, C), f32)
    _, _, _, packed, gquads, tiny = backward(
        sp_count,
        (
            cot, pile(4), pile(0), three(first_gain), three(first_shift), three(second_gain), three(second_shift),
            join(we), join(ws), join(wqkv), join(wo), both(5), both(6), both(1), both(2), both(3),
            squares, quads, weight, jnp.concatenate([vecs[0][None], vecs[1][None], zero], axis=0),
            jnp.concatenate([gain[None], offset[None], zero[:, :256]], axis=0), stat, field0,
        ),
        2,
    )
    gquads = gquads.reshape(4, NW, 4, SUB, 256)[:, :, :, :REAL].reshape(4, NW, 2, 2, 5, 5, 2, 128)
    patches_grad = gquads.transpose(2, 4, 6, 0, 1, 3, 5, 7).reshape(20, 240, 64)
    small1, small2 = tiny[0:6].reshape(2, 3, C), tiny[6:12].reshape(2, 3, C)
    dbe, dbqkv = tiny[12:20].reshape(2, 4, 512), tiny[20:28, :384].reshape(2, 4, 384)
    sums, count = jnp.sum(tiny[28:33], axis=1), tiny[33, 0]
    dmgs = lax.dynamic_index_in_dim(tiny[36:40], tp, 0, keepdims=False)
    dmg, dms = dmgs[:256], dmgs[256:]
    blocks = packed.reshape(CHUNKS, ROWS, 128)
    cut = lambda lo, hi: jnp.stack([blocks[13 + lo : 13 + hi], blocks[lo:hi]])
    lanes = lambda x: x.transpose(0, 2, 1, 3).reshape(2, x.shape[2], C)
    g_we, g_ws = lanes(cut(0, 4)), lanes(cut(4, 8))
    g_qkv = cut(8, 11).transpose(0, 2, 1, 3)
    g_wo = lanes(cut(11, 12).reshape(2, 4, 128, 128))
    dbias = cut(12, 13).reshape(8, WT, WT)
    g_tab = table_of(dbias).reshape(2, 4, 361).transpose(0, 2, 1)
    dmw = blocks[26:28].reshape(4, 256, 128).transpose(1, 0, 2).reshape(256, C)
    own4 = lambda x, axis: lax.dynamic_index_in_dim(x, tp, axis, keepdims=False)
    dbqkv = own4(dbqkv, 1).reshape(2, 3, 128)
    g_bias = jnp.stack([dbqkv[:, 0], dbqkv[:, 2]], axis=1)
    g_be = own4(dbe, 1).reshape(2, 512)
    back = lambda x: x.reshape((2, 2, 64) + x.shape[1:]).swapaxes(0, 1).reshape((4, 64) + x.shape[1:])
    rms = jnp.sqrt(sums / (count * C))
    return (
        output, patches_grad, back(dmg), back(dms), back(dmw), small1[:, 0], small1[:, 1], g_qkv, g_bias,
        g_tab, g_wo, small1[:, 2], small2[:, 0], small2[:, 1], g_we, g_be, g_ws, small2[:, 2], rms,
    )


def solution(mesh):
    placed = (
        P("sp", None, "tp"), P(None, "tp"), P(None, "tp"), P(None, "tp", None), P(), P(),
        P(None, None, None, "tp"), P(None, None, "tp"), P(None, None, "tp"), P(None, "tp", None),
        P(), P(), P(), P(None, None, "tp"), P(None, "tp"), P(None, "tp", None), P(), P(),
        P("sp", None), P("sp", None, "tp"),
    )
    results = (
        P("sp", None, "tp"), P("sp", None, "tp"), P(None, "tp"), P(None, "tp"), P(None, "tp", None),
        P(), P(), P(None, None, None, "tp"), P(None, None, "tp"), P(None, None, "tp"),
        P(None, "tp", None), P(), P(), P(), P(None, None, "tp"), P(None, "tp"), P(None, "tp", None),
        P(), P(),
    )
    return jax.shard_map(shards, mesh=mesh, in_specs=placed, out_specs=results, check_vma=False)
```

time: 850 us -> 739 us (0.87)
  local copies, waits for them, and re-layouts: 147 us -> 88.4 us
  blocking collectives: 47.9 us -> 10.4 us
  other arithmetic: 24.4 us -> 55.8 us
  waiting for transfers between devices: 38 us -> 18.4 us
  matrix products: 28.5 us -> 13.6 us
    concatenate x0 -> x11, other arithmetic: none -> 35.6 us  [the longest x3 17.1 us: shards(): join = lambda xs: jnp.concatenate(xs, axis=0)]
    psum x1 -> x0, waiting for transfers between devices: 33 us -> none  [shards(): dmw, dmg, dms = lax.psum((dmw, dmg, dms), 'sp')]
    psum x1 -> x0, blocking collectives: 20.2 us -> none  [shards(): dmw, dmg, dms = lax.psum((dmw, dmg, dms), 'sp')]
    all_gather x2 -> x0, blocking collectives: 15.4 us -> none  [the longest x1 10.2 us: shards(): lax.all_gather(m2, 'tp', axis=1, tiled=True).reshape(1200, 1)]
    dot_general x4 -> x2, matrix products: 13.4 us -> 1.67 us  [bias_of(): jnp.dot(columns.reshape(heads * WIN, 190), jnp.asarray(row_pick()), preci...]
    pallas_call x5 -> x1, Pallas kernels: 272 us -> 265 us  [backward(): pl.pallas_call(functools.partial(bwd_kernel, n), grid=(STEPS,), in_specs=...]
    reshape x23 -> x16, local copies, waits for them, and re-layouts: 19.4 us -> 14.1 us  [the longest x3 5.07 us: shards(): patches.reshape(2, 5, 2, 4, NW, 2, 5, 128).transpose(3, 4, 0, 5, 1, 6, 2, 7)]
    unnamed x173 -> x127, local copies, waits for them, and re-layouts: 20.1 us -> 16.3 us
  transfers between devices with their start and end apart: 14 -> 10, of which waited for: 3 -> 4; matrix products, arithmetic and copies ran while one was open for 23% -> 14% of each run, Pallas kernels for 58% -> 30%
where the time goes in v2:
time: 739 us; the launch traced here: 732 us
  Pallas kernels  510 us (69%)
  local copies, waits for them, and re-layouts  88.4 us (12%)
  other arithmetic  55.8 us (8%)
  starting transfers between devices  19.5 us (3%)
  waiting for transfers between devices  18.4 us (2%)
  between operations  15.9 us (2%)
  matrix products  13.6 us (2%)
  blocking collectives  10.4 us (1%)
    pallas_call x1, Pallas kernels, backward(): pl.pallas_call(functools.partial(bwd_kernel, n), grid=(STEPS,), in_specs=...  265 us
    pallas_call x1, Pallas kernels, gather_all(): pl.pallas_call(functools.partial(gather_kernel, axes, count), in_specs=[A...  195 us
    pallas_call x2, Pallas kernels, attn_fwd(): pl.pallas_call(attn_fwd_kernel, grid=(4,), in_specs=[whole((TOK, C)), who...  27.8 us
    pallas_call x2, Pallas kernels, mlp_fwd(): pl.pallas_call(mlp_fwd_kernel, grid=(4,), in_specs=[whole((TOK, C)), whol...  22.8 us
    concatenate x3, other arithmetic, shards(): join = lambda xs: jnp.concatenate(xs, axis=0)  17.1 us
    concatenate x5, other arithmetic, shards(): both = lambda i: jnp.concatenate([saved[0][i], saved[1][i]], axis=0)  16.4 us
    unnamed x127, local copies, waits for them, and re-layouts  16.3 us
  transfers between devices with their start and end apart: 10, of which 4 were waited for; matrix products, arithmetic and copies ran while one was open for 14% of the time, Pallas kernels for 30%

profile of v2, /device:TPU:0, one launch (start us, length us, event | category | flops | bytes accessed | tf_op | source)
XLA Modules:
  0.0 732.5 jit_solution(8438222885383509319)
XLA Ops:
  7.2 1.9 copy.435
  9.1 1.5 reshape.406
  10.7 2.6 copy.512
  14.4 1.6 multiply_reduce_fusion
  16.0 3.0 fusion.48
  20.0 6.1 collective-permute-start.2
  26.0 1.5 copy.478
  27.5 4.5 all-to-all-start.1
  32.0 2.8 slice_bitcast_fusion.4
  35.7 1.5 slice_bitcast_fusion.1
  43.2 3.0 slice_bitcast_fusion
  46.2 195.2 %gather.1 = (f32[4,40,128]{2,1,0:T(8,128)}, f32[4,3,512,128]{3,2,1,0:T(8,128)}, f32[4,128,512]{2,1,0:T(8,128)}, f32[4,512,512]{2,1,0:T(8,128)}, f32[4,512,512]{2...) custom-call(f32[40,128]{1,0:T(8,128)} %fusion.14.refs_0_, ...), custom_call_target="tpu_custom_call" | custom-call | tf_op jit(solution)/shard_map/gather/pallas_call | solution.py:292
  261.4 10.4 %all-reduce.7 = (f32[512]{0:T(512)S(1)}, f32[512]{0:T(512)S(1)}, f32[4,384]{1,0:T(4,128)S(1)}, f32[4,384]{1,0:T(4,128)S(1)}) all-reduce(f32[512]{0:T(512)S(1)} %bitcast.356, f32[512]{0:T(512)S(1)} %bitcast.357, f32[4,384]{1,0:T(4,128)S(1)} %reduce_sum.43, f32[4,384]{1,0:T(4,128)S(1)} %reduce_sum.41), channel_id=1, replica_groups=mesh['sp'=8,'tp'=4] {'tp'}, use_global_device_ids=true, to_apply=%region_6.7 | all-reduce | flops 4096 | bytes 32768 | tf_op jit(solution)/shard_map/psum | solution.py:948
  276.8 6.8 pad_maximum_fusion.2.refs_9_
  283.8 1.7 copy-done.2
  285.6 8.7 %pad_maximum_fusion = (f32[8,512,512]{2,1,0:T(8,128)}, f32[8,512,512]{2,1,0:T(8,128)}) fusion(f32[4,512,512]{2,1,0:T(8,128)S(1)} %copy-done, f32[4,512,512]{2,1,0:T(8,128)S(1)} %copy-done.2, f32[4,512,512]{2,1,0:T(8,128)S(1)} %copy-done.1, f32[4,512,512]{2,1,0:T(8,128)} %get-tuple-element.55.ws_ref), kind=kLoop, calls=%fused_computation | loop fusion | flops 4194304 | bytes 33554432 | tf_op jit(solution)/shard_map/concatenate | solution.py:983
  294.2 1.5 copy.479
  297.7 1.6 pad_maximum_fusion.7.refs_10_
  299.7 1.9 collective-permute-start.6
  301.6 2.2 fusion.2.field_ref.refs_22_
  305.1 13.9 %attn_fwd.2 = (f32[384,512]{1,0:T(8,128)}, f32[4,384,384]{2,1,0:T(8,128)}, f32[4,3,512,128]{3,2,1,0:T(8,128)}, f32[4,384,128]{2,1,0:T(8,128)}, f32[1,512]{1,0:T(1,128)}) custom-call(f32[384,512]{1,0:T(8,128)} %fusion.2.field_ref.refs_22_, f32[1,512]{1,0:T(1,128)} %get-tuple-element.287.gain_ref, f32[1,512]{1,0:T(1,128)} %get-tuple-element.302.shift_ref, ...), custom_call_target="tpu_custom_call" | custom-call | tf_op jit(solution)/shard_map/attn_fwd/pallas_call | solution.py:132
  319.0 11.3 %mlp_fwd.2 = (f32[384,512]{1,0:T(8,128)}, f32[4,384,512]{2,1,0:T(8,128)}, f32[4,384,512]{2,1,0:T(8,128)}, f32[1,512]{1,0:T(1,128)}, f32[1,512]{1,0:T(1,128)}) custom-call(f32[384,512]{1,0:T(8,128)} %get-tuple-element.53.mid_ref, f32[1,512]{1,0:T(1,128)} %get-tuple-element.279.gain_ref, f32[1,512]{1,0:T(1,128)} %get-tuple-element.304.shift_ref, ...), custom_call_target="tpu_custom_call" | custom-call | tf_op jit(solution)/shard_map/mlp_fwd/pallas_call | solution.py:182
  331.6 1.6 collective-permute-start
  338.2 10.0 %collective-permute-done.1 = f32[1,6,32,512]{3,2,1,0:T(8,128)S(1)} collective-permute-done((f32[1,6,32,512]{3,2,1,0:T(8,128)S(1)}, f32[1,6,32,512]{3,2,1,0:T(8,128)S(1)}, u32[]{:S(2)}, u32[]{:S(2)}) %collective-permute-start.1) | collective-permute-done | bytes 393248 | tf_op jit(solution)/shard_map/ppermute | solution.py:852
  349.3 13.9 %attn_fwd.3 = (f32[384,512]{1,0:T(8,128)}, f32[4,384,384]{2,1,0:T(8,128)}, f32[4,3,512,128]{3,2,1,0:T(8,128)}, f32[4,384,128]{2,1,0:T(8,128)}, f32[1,512]{1,0:T(1,128)}) custom-call(f32[384,512]{1,0:T(8,128)} %bitcast.286, f32[1,512]{1,0:T(1,128)} %get-tuple-element.286.gain_ref, f32[1,512]{1,0:T(1,128)} %get-tuple-element.303.shift_ref, ...), custom_call_target="tpu_custom_call" | custom-call | tf_op jit(solution)/shard_map/attn_fwd/pallas_call | solution.py:132
  363.3 2.5 pad_maximum_fusion.8.refs_1_
  367.0 11.4 %mlp_fwd.3 = (f32[384,512]{1,0:T(8,128)}, f32[4,384,512]{2,1,0:T(8,128)}, f32[4,384,512]{2,1,0:T(8,128)}, f32[1,512]{1,0:T(1,128)}, f32[1,512]{1,0:T(1,128)}) custom-call(f32[384,512]{1,0:T(8,128)} %get-tuple-element.59.mid_ref, f32[1,512]{1,0:T(1,128)} %get-tuple-element.278.gain_ref, f32[1,512]{1,0:T(1,128)} %get-tuple-element.305.shift_ref, ...), custom_call_target="tpu_custom_call" | custom-call | tf_op jit(solution)/shard_map/mlp_fwd/pallas_call | solution.py:182
  378.5 5.5 pad_maximum_fusion.3.refs_11_
  384.0 3.8 pad_maximum_fusion.4.refs_12_
  387.8 2.7 pad_maximum_fusion.6.refs_13_
  392.4 3.0 pad_maximum_fusion.5.refs_14_
  397.4 264.7 %backward.1 = (f32[4,13312,128]{2,1,0:T(8,128)}, f32[4,384,512]{2,1,0:T(8,128)}, f32[4,8,384]{2,1,0:T(8,128)}, f32[14336,128]{1,0:T(8,128)}, f32[4,384,256]{2,1,0:T(8,128)}, /*index=5*/f32[40,512]{1,0:T(8,128)}) custom-call(f32[384,512]{1,0:T(8,128)} %bitcast.307, f32[2,384,512]{2,1,0:T(8,128)} %pad_maximum_fusion.8.refs_1_, ...), custom_call_target="tpu_custom_call" | custom-call | tf_op jit(solution)/shard_map/backward/pallas_call | solution.py:784
  663.7 2.6 fusion.31
  666.3 2.1 fusion.30
  668.4 3.5 fusion.29
  674.9 3.9 fusion.49
  678.8 1.8 convolution_bitcast_fusion.4
  682.1 1.6 copy_bitcast_fusion.1
  683.7 1.5 pad_maximum_fusion.17
  685.2 1.9 slice.331
  687.6 2.0 reshape.495
  689.6 1.5 copy.488
  691.2 2.5 reshape.455
  693.6 1.8 copy.500
  708.6 2.0 copy.476
  710.6 3.6 all-to-all-start
  714.8 1.6 copy_bitcast_fusion
  717.0 7.5 %all-to-all-done = f32[10,30,4,128]{3,1,0,2:T(8,128)S(1)} async-done(((f32[10,30,4,128]{3,1,0,2:T(8,128)}), f32[10,30,4,128]{3,1,0,2:T(8,128)S(1)}, u32[]{:S(2)}, u32[]{:S(2)}) %all-to-all-start) | async-done | bytes 614432 | tf_op jit(solution)/shard_map/all_to_all | solution.py:975
  (288 shorter events, 70.5 us)
Async XLA Ops:
  7.2 294.4 %reduce-scatter.2.cloned.1.call-start = ((), (), s32[]{:S(2)}) async-start(), calls=%async_computation.3 | async-start | bytes 3932160 | tf_op jit(solution)/shard_map/reduce_scatter | solution.py:951
  10.7 3.6 copy-start.54
  10.7 3.7 copy-start.5
  19.0 7.1 copy-start.33
  20.0 313.2 %collective-permute-start.2 = (f32[1,24,32]{1,0,2:T(1,128)S(1)}, f32[1,24,32]{1,0,2:T(1,128)S(1)}, u32[]{:S(2)}, u32[]{:S(2)}) collective-permute-start(f32[1,24,32]{1,0,2:T(1,128)S(1)} %get-tuple-element.261), channel_id=1, source_target_pairs={{4,0},{8,4},{12,8},{16,12},{20,16},{24,20},{28,24},{0,28},{5,1},{9... | collective-permute-start | bytes 9224 | tf_op jit(solution)/shard_map/ppermute | solution.py:852
  27.5 7.4 %copy-start.34 = (f32[2,128,512]{2,1,0:T(8,128)S(1)}, f32[2,128,512]{2,1,0:T(8,128)}, u32[]{:S(2)}) copy-start(f32[2,128,512]{2,1,0:T(8,128)} %param.35) | copy-start | bytes 1572868
  27.5 266.7 %all-to-all-start.1 = ((f32[10,120,1,128]{3,2,0,1:T(1,128)}), f32[10,120,1,128]{3,2,0,1:T(1,128)}, u32[]{:S(2)}, u32[]{:S(2)}) async-start(f32[10,120,1,128]{3,2,0,1:T(1,128)} %copy.478), calls=%async_computation.2 | async-start | bytes 1228800 | tf_op jit(solution)/shard_map/all_to_all | solution.py:977
  32.0 3.7 copy-start.24
  35.7 6.6 copy-start.55
  35.7 6.8 copy-start.42
  35.7 6.9 copy-start.44
  35.7 6.9 copy-start.48
  46.2 197.1 %copy-start.31 = (f32[19,10,10,1]{0,2,1,3:T(8,128)S(1)}, f32[19,10,10,1]{0,2,1,3:T(8,128)}, u32[]{:S(2)}) copy-start(f32[19,10,10,1]{0,2,1,3:T(8,128)} %constant.89) | copy-start | bytes 22804
  255.4 3.2 copy-start.39
  255.4 3.8 copy-start.41
  255.4 5.2 copy-start.6
  255.4 18.0 %copy-start.47 = (f32[1,256]{1,0:T(1,128)S(1)}, f32[1,256]{1,0:T(1,128)}, u32[]{:S(2)}) copy-start(f32[1,256]{1,0:T(1,128)} %broadcast_in_dim_reshape.7) | copy-start | bytes 3076
  255.5 18.7 %copy-start.45 = (f32[2,512]{1,0:T(2,128)S(1)}, f32[2,512]{1,0:T(2,128)}, u32[]{:S(2)}) copy-start(f32[2,512]{1,0:T(2,128)} %param.36) | copy-start | bytes 12292
  255.5 19.2 %copy-start.46 = (f32[2,512]{1,0:T(2,128)S(1)}, f32[2,512]{1,0:T(2,128)}, u32[]{:S(2)}) copy-start(f32[2,512]{1,0:T(2,128)} %param.42) | copy-start | bytes 12292
  276.8 6.8 copy-start
  276.8 7.0 copy-start.1
  276.8 8.8 %copy-start.2 = (f32[4,512,512]{2,1,0:T(8,128)S(1)}, f32[4,512,512]{2,1,0:T(8,128)}, u32[]{:S(2)}) copy-start(f32[4,512,512]{2,1,0:T(8,128)} %get-tuple-element.54.we_ref) | copy-start | bytes 12582916
  297.1 2.6 collective-permute-start.5
  299.7 37.3 %collective-permute-start.6 = (f32[1,6,32,512]{3,2,1,0:T(8,128)S(1)}, f32[1,6,32,512]{3,2,1,0:T(8,128)S(1)}, u32[]{:S(2)}, u32[]{:S(2)}) collective-permute-start(f32[1,6,32,512]{3,2,1,0:T(8,128)S(1)} %get-tuple-element.245), channel_id=1, source_target_pairs={{4,0},{8,4},{12,8},{16,12},{20,16},{24,20},{28,24},{0,28},{5,1},{9... | collective-permute-start | bytes 1179656 | tf_op jit(solution)/shard_map/ppermute | solution.py:852
  331.6 4.2 collective-permute-start
  335.8 12.4 %collective-permute-start.1 = (f32[1,6,32,512]{3,2,1,0:T(8,128)S(1)}, f32[1,6,32,512]{3,2,1,0:T(8,128)S(1)}, u32[]{:S(2)}, u32[]{:S(2)}) collective-permute-start(f32[1,6,32,512]{3,2,1,0:T(8,128)S(1)} %get-tuple-element.249), channel_id=1, source_target_pairs={{4,0},{8,4},{12,8},{16,12},{20,16},{24,20},{28,24},{0,28},{5,1},{9... | collective-permute-start | bytes 1179656 | tf_op jit(solution)/shard_map/ppermute | solution.py:852
  349.3 14.0 %copy-start.21 = (f32[384,512]{1,0:T(8,128)S(1)}, f32[384,512]{1,0:T(8,128)}, u32[]{:S(2)}) copy-start(f32[384,512]{1,0:T(8,128)} %get-tuple-element.53.mid_ref) | copy-start | bytes 2359300
  367.0 11.4 %copy-start.16 = (f32[4,384,512]{2,1,0:T(8,128)S(1)}, f32[4,384,512]{2,1,0:T(8,128)}, u32[]{:S(2)}) copy-start(f32[4,384,512]{2,1,0:T(8,128)} %get-tuple-element.63) | copy-start | bytes 9437188
  378.4 5.5 copy-start.15
  378.5 5.5 copy-start.18
  384.0 3.9 copy-start.22
  384.0 3.9 copy-start.23
  387.8 3.4 copy-start.14
  387.8 4.5 copy-start.17
  392.4 3.1 copy-start.30
  668.4 3.5 copy-start.28
  672.9 10.8 %collective-permute-start.3 = (f32[1,6,32,512]{3,2,1,0:T(8,128)}, f32[1,6,32,512]{3,2,1,0:T(8,128)}, u32[]{:S(2)}, u32[]{:S(2)}) collective-permute-start(f32[1,6,32,512]{3,2,1,0:T(8,128)} %bitcast.76), channel_id=1, source_target_pairs={{28,0},{0,4},{4,8},{8,12},{12,16},{16,20},{20,24},{24,28},{29,1},{... | collective-permute-start | bytes 1179656 | tf_op jit(solution)/shard_map/ppermute | solution.py:852
  673.5 5.3 copy-start.32
  674.6 6.1 copy-start.19
  674.6 6.1 copy-start.20
  678.8 3.1 copy-start.36
  685.2 20.5 %collective-permute-start.4 = (f32[2,1,32,512]{3,2,1,0:T(8,128)}, f32[2,1,32,512]{3,2,1,0:T(8,128)}, u32[]{:S(2)}, u32[]{:S(2)}) collective-permute-start(f32[2,1,32,512]{3,2,1,0:T(8,128)} %pad_maximum_fusion.17), channel_id=1, source_target_pairs={{3,0},{0,1},{1,2},{2,3},{7,4},{4,5},{5,6},{6,7},{11,8},{8,9},{9,10... | collective-permute-start | bytes 393224 | tf_op jit(solution)/shard_map/ppermute | solution.py:852
  695.4 5.1 copy-start.35
  695.4 9.4 %copy-start.26 = (f32[512,128]{1,0:T(8,128)S(1)}, f32[512,128]{1,0:T(8,128)}, u32[]{:S(2)}) copy-start(f32[512,128]{1,0:T(8,128)} %get-tuple-element.230) | copy-start | bytes 786436
  695.4 9.4 %copy-start.27 = (f32[512,128]{1,0:T(8,128)S(1)}, f32[512,128]{1,0:T(8,128)}, u32[]{:S(2)}) copy-start(f32[512,128]{1,0:T(8,128)} %get-tuple-element.231) | copy-start | bytes 786436
  695.4 10.3 %copy-start.12 = (f32[1,3,2,32,512]{4,3,2,0,1:T(8,128)S(1)}, f32[1,3,2,32,512]{4,3,2,0,1:T(8,128)}, u32[]{:S(2)}) copy-start(f32[1,3,2,32,512]{4,3,2,0,1:T(8,128)} %get-tuple-element.247) | copy-start | bytes 1179652
  707.5 7.4 %copy-start.9 = (f32[2048,128]{1,0:T(8,128)S(1)}, f32[2048,128]{1,0:T(8,128)}, u32[]{:S(2)}) copy-start(f32[2048,128]{1,0:T(8,128)} %get-tuple-element.227) | copy-start | bytes 3145732
  710.6 13.9 %all-to-all-start = ((f32[10,30,4,128]{3,1,0,2:T(8,128)}), f32[10,30,4,128]{3,1,0,2:T(8,128)S(1)}, u32[]{:S(2)}, u32[]{:S(2)}) async-start(f32[10,30,4,128]{3,1,0,2:T(8,128)} %copy.476), calls=%async_computation.1 | async-start | bytes 1310720 | tf_op jit(solution)/shard_map/all_to_all | solution.py:975
  (18 other events, 30.1 us)
Sparse Core Ops, SparseCore 0:
  19.1 49.6 reduce-scatter.1

commit v3 on v2

v3 whole, which is shorter than its diff:
```python
import functools

import jax
import jax.numpy as jnp
import numpy as np
from jax import lax
from jax.experimental import pallas as pl
from jax.experimental.pallas import tpu as pltpu
from jax.sharding import PartitionSpec as P

C = 512
HD = 32
C2 = 256
WIN = 10
SHIFT = 5
SUB = 32
REAL = 25
WT = 128
TOK = 384
NW = 3
GROUP = 4

bf16 = jnp.bfloat16
f32 = jnp.float32
epsilon = 1e-05
masked = -1000000000.0

NN = (((1,), (0,)), ((), ()))
NT = (((1,), (1,)), ((), ()))
TN = (((0,), (0,)), ((), ()))


def split(x):
    high = x.astype(bf16)
    return high, (x - high.astype(f32)).astype(bf16)


def mm(a, b, dims):
    return lax.dot_general(a, b, dims, preferred_element_type=f32)


def mm3(a, b, dims):
    return mm(a[0], b[0], dims) + (mm(a[0], b[1], dims) + mm(a[1], b[0], dims))


def normalized(x):
    center = x - jnp.mean(x, axis=-1, keepdims=True)
    rho = lax.rsqrt(jnp.mean(center * center, axis=-1, keepdims=True) + epsilon)
    return center * rho, rho


def head_masks(dtype):
    lane = lax.broadcasted_iota(jnp.int32, (1, 128), 1) // HD
    return [(lane == h).astype(f32).astype(dtype) for h in range(GROUP)]


def stacked(pair, masks):
    return tuple(jnp.concatenate([part * m for m in masks], axis=0) for part in pair)


def side_by_side(pair):
    return tuple(
        jnp.concatenate([part[h * WT : (h + 1) * WT] for h in range(GROUP)], axis=1)
        for part in pair
    )


def colsum(x):
    return jnp.sum(x, axis=0, keepdims=True)


def sds(*shape):
    return jax.ShapeDtypeStruct(shape, f32)


def norm_back(x, gain, grad_y):
    xhat, rho = normalized(x)
    gh = grad_y * gain
    grad_x = rho * (
        gh - jnp.mean(gh, axis=-1, keepdims=True) - xhat * jnp.mean(gh * xhat, axis=-1, keepdims=True)
    )
    return grad_x, colsum(grad_y * xhat), colsum(grad_y)


MESH = pl.DeviceIdType.MESH
ANY = pl.BlockSpec(memory_space=pl.ANY)
VM = pl.BlockSpec(memory_space=pltpu.VMEM)


def here():
    sp, tp = lax.axis_index("sp"), lax.axis_index("tp")
    return sp, tp, (sp, tp ^ 1), (sp, tp ^ 2), (sp ^ 1, tp)


def meet(peers):
    barrier = pltpu.get_barrier_semaphore()
    for peer in peers:
        pl.semaphore_signal(barrier, inc=1, device_id=peer, device_id_type=MESH)
    pl.semaphore_wait(barrier, len(peers))


def push(src, dst, send, recv, peer):
    return pltpu.make_async_remote_copy(
        src_ref=src, dst_ref=dst, send_sem=send, recv_sem=recv, device_id=peer, device_id_type=MESH
    )


ROWS = 512
HALF = ROWS // 2
MLP_ROWS, ATT_ROWS = 4096, 2560
MLP_CH, ATT_CH = MLP_ROWS // ROWS, ATT_ROWS // ROWS
FULL_CH = 2 * (MLP_CH + ATT_CH)
CHUNKS = FULL_CH + 2
FIRST = 4
AG_STEP = 15
MERGE_STEP = 20
TINY_STEP = 25
STEPS = FIRST + CHUNKS + 6
TINY = 40
COLS = [(0, 0, 0, 1), (0, 1, 1, 0), (1, 0, 1, 1), (1, 1, 2, 0), (2, 0, 2, 1)]


def at(w, sr, sc):
    return pl.ds(w * WT + sr * 64 + sc * SUB, SUB)


NCH = 13
GCH = 2 * NCH
F_STEPS = 31


def fwd_order(s):
    att = jnp.where(s < 3, 0, jnp.where(s < 7, 1, jnp.where(s < 8, 2, jnp.where(s < 17, 3, jnp.where(
        s < 18, 4, jnp.where(s < 20, 5, jnp.where(s < 21, 6, 7)))))))
    mlp = jnp.where(s < 10, 0, jnp.where(s < 15, 1, jnp.where(s < 16, 2, jnp.where(s < 22, 3, jnp.where(
        s < 23, 4, jnp.where(s < 28, 5, jnp.where(s < 29, 6, 7)))))))
    return att, mlp


def among(step, steps):
    found = step == steps[0]
    for s in steps[1:]:
        found = found | (step == s)
    return found


def fwd_kernel(n, *refs):
    (
        q_ref, mw_ref, mg_ref, wi_ref, bi_ref, wo_ref, we_ref, ws_ref, sm_ref, g1_ref, b1_ref, bo_ref,
        g2_ref, b2_ref, bs_ref, regc_ref, regr_ref, v0_ref, v1_ref, vs_ref, cot_ref,
    ) = refs[:21]
    (
        nall, wall, cb, field_out, mid_out, qkv_ref, p_ref, att_ref, hid_ref, slope_ref, stat_ref, vec_ref,
        sq_ref, os_ref,
    ) = refs[21:35]
    (
        nb, wb, smb, pb, pr, px, stb, str_, stx, vp, vr, vc, field, nh, nl, mixed, moved,
        lsem, ss, sr, xs, xr, ys, yr, s2s, s2r, s3s, s3r, sms, smr, rss, rsr, vps, vpr, vvs, vvr,
        mvs, mvr, cbs, cbr, cbl, hn, hw,
    ) = refs[35:]
    step = pl.program_id(0)
    sp, tp, sib, across, beside = here()
    par = sp & 1
    up, down = lax.rem(sp + 1, n), lax.rem(sp + n - 1, n)
    left = lax.rem(tp + 3, 4)

    def own():
        todo = []
        for b in range(2):
            todo += [
                (wi_ref.at[b], nb.at[0, pl.ds(4 * b, 3)]), (bi_ref.at[b], nb.at[0, 4 * b + 3]),
                (we_ref.at[b], wb.at[0, pl.ds(9 * b, 4)]), (ws_ref.at[b], wb.at[0, pl.ds(9 * b + 4, 4)]),
                (wo_ref.at[b], wb.at[0, pl.ds(9 * b + 8, 1)]),
            ]
        todo.append((sm_ref, smb.at[0]))
        return [pltpu.make_async_copy(s, d, lsem.at[i]) for i, (s, d) in enumerate(todo)]

    def to_sib(b):
        parts = [(nb, pl.ds(4 * b, 4)), (wb, pl.ds(9 * b + 8, 1)), (wb, pl.ds(9 * b, 8))]
        return [
            push(buf.at[0, d], buf.at[1, d], ss.at[b, k], sr.at[b, k], sib) for k, (buf, d) in enumerate(parts)
        ]

    def narrow(c):
        b, r = c // NCH, c % NCH
        return r < 4, 4 * b + r, 9 * b + jnp.where(r == 4, 8, r - 5)

    def each(c, act):
        small, kn, kw = narrow(c)

        @pl.when(small)
        def _():
            act(nb, kn, 256)

        @pl.when(jnp.logical_not(small))
        def _():
            act(wb, kw, 64)

    def half(size, h):
        return pl.ds(pl.multiple_of(h * size, size), size)

    def x_copy(c, buf, k, size):
        return push(buf.at[0, k, half(size, par)], buf.at[2, k, half(size, par)], xs.at[c], xr.at[c], across)

    def y_copy(c, buf, k, size):
        return push(buf.at[2, k, half(size, par)], buf.at[2, k, half(size, par)], ys.at[c], yr.at[c], beside)

    def s2_copy(c, buf, k, size):
        return push(buf.at[2, k, half(size, par)], buf.at[3, k, half(size, par)], s2s.at[c], s2r.at[c], sib)

    def s3_copy(c, buf, k, size):
        return push(
            buf.at[2, k, half(size, 1 - par)], buf.at[3, k, half(size, 1 - par)], s3s.at[c], s3r.at[c], sib
        )

    def rs_copies(k):
        if k < 2:
            i = 1 + 2 * k
            return [
                push(pb.at[i], pr.at[k], rss.at[0, k], rsr.at[0, k], sib),
                push(stb.at[i], str_.at[k], rss.at[1, k], rsr.at[1, k], sib),
            ]
        return [
            push(pb.at[2], px, rss.at[0, 2], rsr.at[0, 2], across),
            push(stb.at[2], stx, rss.at[1, 2], rsr.at[1, 2], across),
        ]

    def vec_copies():
        return [push(vp.at[0], vp.at[i], vps.at[i - 1], vpr.at[i - 1], (sp, tp ^ i)) for i in (1, 2, 3)]

    def sm_copy(k):
        src, dst, peer = ((0, 1, sib), (0, 2, across), (2, 3, sib))[k]
        return push(smb.at[src], smb.at[dst], sms.at[k], smr.at[k], peer)

    def valid_copy():
        return push(vs_ref, vr, vvs.at[0], vvr.at[0], (down, tp))

    def moves():
        todo = [(at(0, 1, 0), at(2, 0, 1), (sp, left)), (at(0, 0, 0), at(2, 1, 1), (down, left))]
        for w0, s0, w1, s1 in COLS:
            todo.append((at(w1, 0, s1), at(w0, 1, s0), (down, tp)))
        return [push(field.at[s], moved.at[d], mvs.at[i], mvr.at[i], peer) for i, (s, d, peer) in enumerate(todo)]

    def cot_copy(k, i):
        t = tp ^ i
        src = cot_ref.at[1 - k, pl.ds(6 * t, 6)]
        return push(src, cb.at[tp, k], cbs.at[k, i], cbr.at[k, i], ((sp, t), (down, t))[k])

    def cot_in(k, i):
        src = cot_ref.at[1 - k, pl.ds(0, 6)]
        return push(src, cb.at[tp ^ i, k], cbs.at[k, i], cbr.at[k, i], (sp, tp ^ 1))

    def cot_own():
        return pltpu.make_async_copy(cot_ref.at[1, pl.ds(6 * tp, 6)], cb.at[tp, 0], cbl.at[0])

    @pl.when(step == 0)
    def _():
        for copy in own():
            copy.start()
        barrier = pltpu.get_barrier_semaphore()
        near = [beside] + [(sp, tp ^ i) for i in (1, 2, 3)]
        near += [(up, tp ^ i) for i in range(4)] + [(down, tp ^ i) for i in range(4)]
        for peer in near:
            pl.semaphore_signal(barrier, inc=1, device_id=peer, device_id_type=MESH)
        pl.semaphore_wait(barrier, len(near))
        gain, offset = mg_ref[0:1, :], mg_ref[1:2, :]
        wpair = split(mw_ref[...])
        rows8 = lax.broadcasted_iota(jnp.int32, (8, 256), 0)
        pick = jnp.where(rows8 == 0, gain, jnp.where(rows8 == 1, offset, 0.0))
        vp[0] = jnp.dot(pick, mw_ref[...], precision=lax.Precision.HIGHEST, preferred_element_type=f32)
        for copy in vec_copies():
            copy.start()
        valid_copy().start()
        lane = lax.broadcasted_iota(jnp.int32, (TOK, 128), 1)
        for i in (3, 1, 2, 0):
            quad = q_ref[tp ^ i]
            pb[i] = mm3(split(quad * gain), wpair, NN)
            s1 = jnp.sum(quad, axis=-1, keepdims=True)
            s2 = jnp.sum(quad * quad, axis=-1, keepdims=True)
            stb[i] = jnp.where(lane == 0, s1, jnp.where(lane == 1, s2, 0.0)).T[0:8, :]
            if i % 2 == 1:
                for copy in rs_copies((i - 1) // 2):
                    copy.start()
            if i == 1:
                for copy in own():
                    copy.wait()
                sm_copy(0).start()
                sm_copy(1).start()
                for c in (0, 1):
                    x_copy(c, nb, c, 256).start()
        for copy in rs_copies(1):
            copy.wait_recv()
        pb[2] = pb[2] + pr[1]
        stb[2] = stb[2] + str_[1]
        for copy in rs_copies(2):
            copy.start()
        for copy in to_sib(0):
            copy.start()
        for copy in rs_copies(0):
            copy.wait_recv()
        pb[0] = pb[0] + pr[0]
        stb[0] = stb[0] + str_[0]
        x_copy(2, nb, 2, 256).start()
        sq_ref[...] = jnp.zeros_like(sq_ref)
        os_ref[...] = jnp.zeros_like(os_ref)
        vec_ref[...] = jnp.zeros_like(vec_ref)

    @pl.when(step == 1)
    def _():
        sm_copy(1).wait_recv()
        sm_copy(2).start()
        for copy in vec_copies():
            copy.wait()
        vec_ref[...] = (vp[0] + vp[1]) + (vp[2] + vp[3])
        valid_copy().wait()
        for b in range(2):
            line = v0_ref[...] if b == 0 else v1_ref[...] + vr[...]
            tall = jnp.concatenate([line, jnp.zeros((120, 128), f32)], axis=0).T
            vc[b] = jnp.concatenate([tall[:, w : w + 1] for w in range(NW)], axis=0)
            if b == 1:
                vr[...] = line
        sq_ref[5:6, 0:128] = colsum(v0_ref[...])
        for k in range(2):
            for copy in rs_copies(k):
                copy.wait_send()
        for copy in rs_copies(2):
            copy.wait()
        sums = jnp.concatenate([stb[0] + stx[...], jnp.zeros((120, TOK), f32)], axis=0).T
        mean = sums[:, 0:1] / (4.0 * C2)
        inverse = lax.rsqrt(sums[:, 1:2] / (4.0 * C2) - mean * mean + epsilon)
        lane = lax.broadcasted_iota(jnp.int32, (TOK, 128), 1)
        stat_ref[...] = jnp.where(lane == 0, mean, jnp.where(lane == 1, inverse, 0.0))
        field[...] = inverse * (pb[0] + px[...] - mean * vec_ref[0:1, :]) + vec_ref[1:2, :]

    att, mlp = fwd_order(step)

    @pl.when(among(step, (2, 3, 7, 8, 17, 18, 20, 21)))
    def _():
        b, i = att // 4, att % 4

        @pl.when(i == 0)
        def _():
            @pl.when(b == 1)
            def _():
                for copy in moves():
                    copy.wait()
                field[...] = moved[...]

            field_out[0] = field[...]
            xhat, _ = normalized(field[...])
            nh[...], nl[...] = split(xhat * g1_ref[b] + b1_ref[b])
            mixed[...] = jnp.broadcast_to(bo_ref[b], mixed.shape)

        for k in range(2):

            @pl.when((i == 1) & (b == k))
            def _(k=k):
                for copy in to_sib(k)[:2]:
                    copy.wait_recv()
                if k == 0:
                    sm_copy(0).wait()
                    sm_copy(1).wait_send()
                    sm_copy(2).wait()

        @pl.when(i == 3)
        def _():
            for r in range(5):
                c = b * NCH + r
                buf, k, size = (nb, 4 * b + r, 256) if r < 4 else (wb, 9 * b + 8, 64)
                s2_copy(c, buf, k, size).wait_recv()
                s3_copy(c, buf, k, size).wait_recv()

        pltpu.make_async_copy(nb.at[i, pl.ds(4 * b, 4)], nall.at[i, b], hn.at[b, i]).start()
        w = jnp.concatenate([nb[i, 4 * b + j] for j in range(3)], axis=1)
        lane = lax.broadcasted_iota(jnp.int32, (1, 384), 1)
        qkv = mm3((nh[...], nl[...]), split(w), NN) + smb[i, pl.ds(2 + b, 1), 0:384]
        qkv_ref[0] = qkv * jnp.where(lane < 128, HD ** (-0.5), 1.0)
        masks = head_masks(bf16)
        bias = nb[i, 4 * b + 3]
        eye = lax.broadcasted_iota(jnp.int32, (WT, WT), 0) == lax.broadcasted_iota(jnp.int32, (WT, WT), 1)
        for j in range(NW):
            rows = pl.ds(j * WT, WT)
            seen = qkv_ref[0, rows, :]
            q4 = stacked(split(seen[:, :128]), masks)
            k = split(seen[:, 128:256])
            v4 = stacked(split(seen[:, 256:]), masks)
            flags = jnp.where(b == 0, v0_ref[j : j + 1, :], vr[j : j + 1, :])
            allowed = (regc_ref[b, rows, :] == regr_ref[b, j : j + 1, :]) & (flags > 0) | eye
            allowed = jnp.concatenate([allowed.astype(f32)] * GROUP, axis=0) > 0
            s = jnp.where(allowed, mm3(q4, k, NT) + bias, masked)
            e = jnp.exp(s - jnp.max(s, axis=-1, keepdims=True))
            p = e / jnp.sum(e, axis=-1, keepdims=True)
            p_ref[0, j] = p
            att_ref[0, rows, :] = mm3(side_by_side(split(p)), v4, NN)
        mixed[...] += mm3(split(att_ref[0]), split(wb[i, 9 * b + 8]), NN)

        @pl.when(i == 3)
        def _():
            middle = field[...] + mixed[...]
            mid_out[0] = middle
            sq_ref[pl.ds(2 * b, 1), :] = colsum(mixed[...] * mixed[...] * vc[b])

    @pl.when(among(step, (9, 10, 15, 16, 22, 23, 28, 29)))
    def _():
        b, i = mlp // 4, mlp % 4

        @pl.when(i == 0)
        def _():
            xhat, _ = normalized(mid_out[0])
            nh[...], nl[...] = split(xhat * g2_ref[b] + b2_ref[b])
            mixed[...] = jnp.broadcast_to(bs_ref[b], mixed.shape)

            @pl.when(b == 0)
            def _():
                for copy in to_sib(1):
                    copy.start()

        for k in range(2):

            @pl.when((i == 1) & (b == k))
            def _(k=k):
                to_sib(k)[2].wait_recv()

        @pl.when(i == 3)
        def _():
            for r in range(8):
                c = b * NCH + 5 + r
                s2_copy(c, wb, 9 * b + r, 64).wait_recv()
                s3_copy(c, wb, 9 * b + r, 64).wait_recv()

        pltpu.make_async_copy(wb.at[i, pl.ds(9 * b, 9)], wall.at[i, b], hw.at[b, i]).start()
        we = wb[i, pl.ds(9 * b, 4)].reshape(512, 512)
        ws = wb[i, pl.ds(9 * b + 4, 4)].reshape(512, 512)
        pre = mm3((nh[...], nl[...]), split(we), NN) + smb[i, pl.ds(b, 1), :]
        phi = 0.5 * (1.0 + lax.erf(pre * (2 ** -0.5)))
        hidden = pre * phi
        hid_ref[0] = hidden
        slope_ref[0] = phi + pre * (jnp.exp(-0.5 * pre * pre) * ((2 * np.pi) ** -0.5))
        mixed[...] += mm3(split(hidden), split(ws), NN)

        @pl.when(i == 3)
        def _():
            out = mid_out[0] + mixed[...]
            field[...] = out
            sq_ref[pl.ds(2 * b + 1, 1), :] = colsum(mixed[...] * mixed[...] * vc[b])

            @pl.when(b == 0)
            def _():
                for copy in moves():
                    copy.start()
                for w0, s0, w1, s1 in COLS:
                    moved[at(w0, 0, s0), :] = field[at(w1, 1, s1), :]

            @pl.when(b == 1)
            def _():
                sq_ref[4:5, :] = colsum(out * out * vc[1])
                for t in range(4):
                    for w in range(NW):
                        for r in range(2):
                            os_ref[t, r, w * 64 : w * 64 + 64, :] = out[
                                w * WT + r * 64 : w * WT + r * 64 + 64, t * 128 : (t + 1) * 128
                            ]

    p = step - 1

    @pl.when((p >= 1) & (p + 2 < GCH))
    def _():
        each(p + 2, lambda buf, k, size: x_copy(p + 2, buf, k, size).start())

    @pl.when(step == GCH - 1)
    def _():
        cot_own().start()
        for k in range(2):
            for i in range(4):
                if k + i > 0:
                    cot_copy(k, i).start()

    @pl.when((p >= 0) & (p < GCH))
    def _():
        def act(buf, k, size):
            x_copy(p, buf, k, size).wait_recv()
            y_copy(p, buf, k, size).start()
            s2_copy(p, buf, k, size).start()

        each(p, act)

    @pl.when((p >= 1) & (p <= GCH))
    def _():
        def act(buf, k, size):
            y_copy(p - 1, buf, k, size).wait_recv()
            s3_copy(p - 1, buf, k, size).start()

        each(p - 1, act)

    @pl.when(step == F_STEPS - 1)
    def _():
        cot_own().wait()
        for k in range(2):
            for i in range(4):
                if k + i > 0:
                    cot_copy(k, i).wait_send()
                    cot_in(k, i).wait_recv()
        for b in range(2):
            for copy in to_sib(b):
                copy.wait_send()
            for i in range(4):
                pltpu.make_async_copy(nb.at[i, pl.ds(4 * b, 4)], nall.at[i, b], hn.at[b, i]).wait()
                pltpu.make_async_copy(wb.at[i, pl.ds(9 * b, 9)], wall.at[i, b], hw.at[b, i]).wait()

        @pl.loop(0, GCH)
        def _(c):
            def act(buf, k, size):
                x_copy(c, buf, k, size).wait_send()
                y_copy(c, buf, k, size).wait_send()
                s2_copy(c, buf, k, size).wait_send()
                s3_copy(c, buf, k, size).wait_send()

            each(c, act)


def forward(n, args, ident):
    dma = pltpu.SemaphoreType.DMA

    def fixed(shape):
        return pl.BlockSpec(shape, lambda s: (0,) * len(shape), pipeline_mode=pl.Buffered(1))

    def by(index, shape):
        zeros = (0,) * len(shape)
        return pl.BlockSpec((1,) + shape, lambda s: (index(s),) + zeros)

    att_at = lambda s: fwd_order(s)[0]
    mlp_at = lambda s: fwd_order(s)[1]
    second = lambda s: jnp.where(s < 17, 0, 1)
    vm = lambda *shape: pltpu.VMEM(shape, f32)
    two = fixed((2, 1, C))
    return pl.pallas_call(
        functools.partial(fwd_kernel, n),
        grid=(F_STEPS,),
        in_specs=[
            fixed((4, TOK, 256)), fixed((256, C)), fixed((8, 256)), ANY, ANY, ANY, ANY, ANY, ANY,
            two, two, two, two, two, two, fixed((2, TOK, 1)), fixed((2, 8, 128)), fixed((8, 128)),
            fixed((8, 128)), fixed((8, 128)), ANY,
        ],
        out_specs=[
            ANY, ANY, ANY, by(second, (TOK, C)), by(second, (TOK, C)), by(att_at, (TOK, 384)),
            by(att_at, (NW, GROUP * WT, WT)), by(att_at, (TOK, 128)), by(mlp_at, (TOK, 512)),
            by(mlp_at, (TOK, 512)), fixed((TOK, 128)), fixed((8, C)), fixed((8, C)), fixed((4, 2, 192, 128)),
        ],
        out_shape=[
            sds(4, 2, 4, 512, 128), sds(4, 2, 9, 128, 512), sds(4, 2, 6, SUB, 128), sds(2, TOK, C), sds(2, TOK, C),
            sds(8, TOK, 384), sds(8, NW, GROUP * WT, WT), sds(8, TOK, 128), sds(8, TOK, 512), sds(8, TOK, 512),
            sds(TOK, 128), sds(8, C), sds(8, C), sds(4, 2, 192, 128),
        ],
        scratch_shapes=[
            vm(4, 8, 512, 128), vm(4, 18, 128, 512), vm(4, 8, C), vm(4, TOK, C), vm(2, TOK, C), vm(TOK, C),
            vm(4, 8, TOK), vm(2, 8, TOK), vm(8, TOK), vm(4, 8, C), vm(8, 128), vm(2, TOK, 1), vm(TOK, C),
            pltpu.VMEM((TOK, C), bf16), pltpu.VMEM((TOK, C), bf16), vm(TOK, C), vm(TOK, C),
            dma((11,)), dma((2, 3)), dma((2, 3)), dma((GCH,)), dma((GCH,)), dma((GCH,)), dma((GCH,)),
            dma((GCH,)), dma((GCH,)), dma((GCH,)), dma((GCH,)), dma((3,)), dma((3,)), dma((2, 3)), dma((2, 3)),
            dma((3,)), dma((3,)), dma((1,)), dma((1,)), dma((7,)), dma((7,)), dma((2, 4)), dma((2, 4)),
            dma((1,)), dma((2, 4)), dma((2, 4)),
        ],
        compiler_params=pltpu.CompilerParams(
            collective_id=ident, has_side_effects=True, vmem_limit_bytes=60 << 20,
            dimension_semantics=("arbitrary",),
        ),
        name="forward",
    )(*args)


def bwd_kernel(n, *refs):
    (
        cot_ref, mid_ref, field_ref, g1_ref, b1_ref, g2_ref, b2_ref, we_ref, ws_ref, wqkv_ref, wo_ref,
        hid_ref, slope_ref, qkv_ref, p_ref, att_ref, sq_ref, q_ref, mw_ref, vec_ref, mg_ref, stat_ref, os_ref,
    ) = refs[:23]
    pack, gall, exall, ob, out_ref, gq_ref, tout_ref = refs[23:30]
    (
        nth, ntl, gh, gl, acc, dqkv, gf, gbuf, moved, ext, extin, qbuf,
        loc, pair, yr, zr, fin, ta, tx, tz,
        gsem, mvs, mvr, ags, agr, agl, msem, ss, rs, zs, zq, fs, fq, ls, os, ts, tq, tzs, tzq, obs, obr, obl,
    ) = refs[30:]
    step = pl.program_id(0)
    dmw, gqbuf = moved.at[pl.ds(0, 256)], dqkv.at[:, pl.ds(0, 256)]
    sp, tp, sib, across, beside = here()
    par, mine = sp & 1, sp // 2
    m = n // 2
    piece = HALF // m
    up, down, right = lax.rem(sp + 1, n), lax.rem(sp + n - 1, n), lax.rem(tp + 1, 4)

    def member(j):
        return lax.rem(mine + j, m)

    def device(q):
        return (q * 2 + par, tp)

    def out_copy(k, i):
        t = tp ^ i
        return push(
            os_ref.at[t, k], ob.at[1 - k, pl.ds(6 * tp, 6)], obs.at[k, i], obr.at[k, i], ((sp, t), (up, t))[k]
        )

    def out_in(k, i):
        return push(
            os_ref.at[0, k], ob.at[1 - k, pl.ds(6 * (tp ^ i), 6)], obs.at[k, i], obr.at[k, i], (sp, tp ^ 1)
        )

    def out_own():
        return pltpu.make_async_copy(os_ref.at[tp, 0], ob.at[1, pl.ds(6 * tp, 6)], obl.at[0])

    @pl.when(step == 0)
    def _():
        barrier = pltpu.get_barrier_semaphore()
        near = [beside] + [(sp, tp ^ i) for i in (1, 2, 3)]
        near += [(up, tp ^ i) for i in range(4)] + [(down, tp ^ i) for i in range(4)]
        for peer in near:
            pl.semaphore_signal(barrier, inc=1, device_id=peer, device_id_type=MESH)

        @pl.loop(1, m)
        def _(j):
            pl.semaphore_signal(barrier, inc=1, device_id=device(member(j)), device_id_type=MESH)

        ta[...] = jnp.zeros_like(ta)
        ta[0, 28:36, :] = sq_ref[...]
        for t in range(4):
            for w in range(NW):
                for r in range(2):
                    gf[w * WT + r * 64 : w * WT + r * 64 + 64, t * 128 : (t + 1) * 128] = cot_ref[
                        t, r, w * 64 : w * 64 + 64, :
                    ]
        pl.semaphore_wait(barrier, len(near) + m - 1)
        out_own().start()
        for k in range(2):
            for i in range(4):
                if k + i > 0:
                    out_copy(k, i).start()

    def packed(b, i, late):
        size = ATT_ROWS if late else MLP_ROWS
        base = pl.multiple_of((1 - b) * (MLP_ROWS + ATT_ROWS) + (MLP_ROWS if late else 0), ROWS)
        slot = i % 2
        return pltpu.make_async_copy(
            gbuf.at[slot, pl.ds(0, size)], pack.at[tp ^ i, pl.ds(base, size)], gsem.at[slot]
        )

    def moves():
        todo = [
            (at(2, 0, 1), at(0, 1, 0), (sp, right)),
            (at(2, 1, 1), at(0, 0, 0), (up, right)),
        ]
        for w0, s0, w1, s1 in COLS:
            todo.append((at(w0, 1, s0), at(w1, 0, s1), (up, tp)))
        return [push(acc.at[src], moved.at[dst], mvs.at[i], mvr.at[i], peer) for i, (src, dst, peer) in enumerate(todo)]

    def kept():
        for w0, s0, w1, s1 in COLS:
            moved[at(w1, 1, s1), :] = acc[at(w0, 0, s0), :]

    phase = step // 4

    @pl.when((phase == 0) | (phase == 2))
    def _():
        b = 1 - phase // 2
        i = step % 4

        @pl.when(i == 0)
        def _():
            @pl.when(b == 0)
            def _():
                for copy in moves():
                    copy.wait()
                gf[...] = moved[...]

            xhat, _ = normalized(mid_ref[0])
            nth[...], ntl[...] = split((xhat * g2_ref[b] + b2_ref[b]).T)
            gh[...], gl[...] = split(gf[...])
            acc[...] = jnp.zeros_like(acc)

        slot = i % 2
        grad = (gh[...], gl[...])
        dws = mm3(split(hid_ref[0].T), grad, NN)
        for j in range(4):
            gbuf[slot, 2048 + j * 512 : 2560 + j * 512, :] = dws[:, j * 128 : (j + 1) * 128]
        dpre = mm3(grad, split(ws_ref[0, 0].reshape(512, C)), NT) * slope_ref[0]
        ta[0, pl.ds(12 + b * 4 + (tp ^ i), 1), :] = colsum(dpre)
        pair_ = split(dpre)
        dwe = mm3((nth[...], ntl[...]), pair_, NN)
        for j in range(4):
            gbuf[slot, j * 512 : (j + 1) * 512, :] = dwe[:, j * 128 : (j + 1) * 128]
        acc[...] += mm3(pair_, split(we_ref[0, 0].reshape(C, 512)), NT)

        @pl.when(i > 0)
        def _():
            packed(b, i - 1, False).wait()

        packed(b, i, False).start()

        @pl.when(i == 3)
        def _():
            grad_x, dgain, dshift = norm_back(mid_ref[0], g2_ref[b], acc[...])
            ta[0, pl.ds(6 + 3 * b, 1), :] = dgain
            ta[0, pl.ds(7 + 3 * b, 1), :] = dshift
            ta[0, pl.ds(8 + 3 * b, 1), :] = colsum(gf[...])
            gf[...] = gf[...] + grad_x
            packed(b, 3, False).wait()

    @pl.when((phase == 1) | (phase == 3))
    def _():
        b = 1 - phase // 2
        i = step % 4

        @pl.when(i == 0)
        def _():
            xhat, _ = normalized(field_ref[0])
            nth[...], ntl[...] = split((xhat * g1_ref[b] + b1_ref[b]).T)
            gh[...], gl[...] = split(gf[...])
            acc[...] = jnp.zeros_like(acc)

        slot = i % 2
        grad = (gh[...], gl[...])
        dwo = mm3(split(att_ref[0].T), grad, NN)
        for j in range(4):
            gbuf[slot, 1536 + j * 128 : 1664 + j * 128, :] = dwo[:, j * 128 : (j + 1) * 128]
        dout = mm3(grad, split(wo_ref[0, 0, 0]), NT)
        masks = head_masks(bf16)
        dbias = jnp.zeros((GROUP * WT, WT), f32)
        for w in range(NW):
            rows = slice(w * WT, (w + 1) * WT)
            seen = qkv_ref[0, pl.ds(w * WT, WT), :]
            q4 = stacked(split(seen[:, :128]), masks)
            k4 = stacked(split(seen[:, 128:256]), masks)
            v = split(seen[:, 256:])
            p = p_ref[0, w]
            do4 = stacked(split(dout[rows]), masks)
            dp = mm3(do4, v, NT)
            ds = p * (dp - jnp.sum(p * dp, axis=-1, keepdims=True))
            dbias = dbias + ds
            dpair = split(ds)
            dqkv[pl.ds(w * WT, WT), 0:128] = mm3(side_by_side(dpair), k4, NN) * HD ** (-0.5)
            dqkv[pl.ds(w * WT, WT), 128:256] = mm3(dpair, q4, TN)
            dqkv[pl.ds(w * WT, WT), 256:384] = mm3(split(p), do4, TN)
        gbuf[slot, 2048:2560, :] = dbias
        grads = dqkv[...]
        ta[0, pl.ds(20 + b * 4 + (tp ^ i), 1), 0:384] = colsum(grads)
        pair_ = split(grads)
        dw = mm3((nth[...], ntl[...]), pair_, NN)
        for j in range(3):
            gbuf[slot, j * 512 : (j + 1) * 512, :] = dw[:, j * 128 : (j + 1) * 128]
        w = jnp.concatenate([wqkv_ref[0, 0, j] for j in range(3)], axis=1)
        acc[...] += mm3(pair_, split(w), NT)

        @pl.when(i > 0)
        def _():
            packed(b, i - 1, True).wait()

        packed(b, i, True).start()

        @pl.when(i == 3)
        def _():
            grad_x, dgain, dshift = norm_back(field_ref[0], g1_ref[b], acc[...])
            ta[0, pl.ds(3 * b, 1), :] = dgain
            ta[0, pl.ds(1 + 3 * b, 1), :] = dshift
            ta[0, pl.ds(2 + 3 * b, 1), :] = colsum(gf[...])
            acc[...] = gf[...] + grad_x

            @pl.when(b == 1)
            def _():
                for copy in moves():
                    copy.start()
                kept()

            packed(b, 3, True).wait()

    def ag(k, src, dst, peer, which):
        return push(src, dst, ags.at[which, k], agr.at[which, k], peer)

    def ag_copies(k):
        own = (acc, ext)
        whole_ = (gall, exall)
        return [
            ag(k, own[w], whole_[w].at[tp], (sib, across)[k], w) if k < 2
            else ag(k, whole_[w].at[tp ^ 2], whole_[w].at[tp ^ 2], sib, w)
            for w in range(2)
        ]

    @pl.when(step == AG_STEP)
    def _():
        m2 = jnp.sum(acc[...] * (field_ref[0] - vec_ref[1:2, :]), axis=-1, keepdims=True)
        lane = lax.broadcasted_iota(jnp.int32, (TOK, 128), 1)
        tall = jnp.where(lane == 2, m2, stat_ref[...])
        ext[...] = tall.T[0:8, :]
        for k in range(2):
            for copy in ag_copies(k):
                copy.start()

    @pl.when(step == MERGE_STEP - 1)
    def _():
        for copy in ag_copies(1):
            copy.wait()
        for copy in ag_copies(2):
            copy.start()
        for copy in ag_copies(0):
            copy.wait()

    @pl.when((step >= MERGE_STEP) & (step < MERGE_STEP + 4))
    def _():
        i = step - MERGE_STEP
        t = tp ^ i

        @pl.when(i == 2)
        def _():
            for copy in ag_copies(2):
                copy.wait()

        fetch = [pltpu.make_async_copy(q_ref.at[t], qbuf, msem.at[0])]
        fetch[0].start()

        @pl.when(i == 0)
        def _():
            dmw[...] = jnp.zeros((256, C), f32)
            gf[...] = acc[...]
            extin[...] = ext[...]

        @pl.when(i > 0)
        def _():
            two = [
                pltpu.make_async_copy(gall.at[t], gf, msem.at[1]),
                pltpu.make_async_copy(exall.at[t], extin, msem.at[2]),
            ]
            for copy in two:
                copy.start()
            for copy in two:
                copy.wait()

        fetch[0].wait()
        wide = jnp.concatenate([extin[...], jnp.zeros((120, TOK), f32)], axis=0).T
        mean, inv, m2 = wide[:, 0:1], wide[:, 1:2], wide[:, 2:3]
        full = gf[...]
        m1 = jnp.sum(full * vec_ref[0:1, :], axis=-1, keepdims=True) / (4.0 * C2)
        m2 = m2 / (4.0 * C2)
        fpair = split(full)
        xhat = (qbuf[...] - mean) * inv
        gmerged = mm3(fpair, split(mw_ref[...]), NT)
        dmw[...] += mm3(split((xhat * mg_ref[0:1, :] + mg_ref[1:2, :]).T), fpair, NN)
        row = pl.ds(36 + tp, 1)
        ta[0, row, 0:256] += colsum(gmerged * xhat)
        ta[0, row, 256:512] += colsum(gmerged)

        @pl.when(i > 0)
        def _():
            pltpu.make_async_copy(gqbuf, gq_ref.at[t], msem.at[3]).wait()

        gqbuf[...] = inv * (gmerged * mg_ref[0:1, :] - m1 - xhat * m2)
        pltpu.make_async_copy(gqbuf, gq_ref.at[t], msem.at[3]).start()

        @pl.when(i == 3)
        def _():
            pltpu.make_async_copy(gqbuf, gq_ref.at[t], msem.at[3]).wait()
            for k in range(2):
                for j in range(2):
                    low = (2 * k + j) * 128
                    pair[FULL_CH + k, 0, j * 256 : (j + 1) * 256, :] = dmw[:, low : low + 128]

    def rows(c):
        return pl.ds(pl.multiple_of(c * ROWS, ROWS), ROWS)

    def load(c, k):
        return pltpu.make_async_copy(pack.at[tp ^ (2 * k), rows(c)], loc.at[c % 2, k], ls.at[c % 2, k])

    def swap(c, k):
        return push(pack.at[tp ^ 1 ^ (2 * k), rows(c)], pair.at[c, k], ss.at[k, c], rs.at[k, c], sib)

    def cross(c):
        return push(pair.at[c, 1], fin.at[c], ss.at[2, c], rs.at[2, c], across)

    def halves(h):
        return pl.ds(pl.multiple_of(h * HALF, HALF), HALF)

    def side(c):
        return push(pair.at[c, 0, halves(1 - par)], yr.at[c], ss.at[3, c], rs.at[3, c], beside)

    def bit(q):
        return pl.ds(pl.multiple_of(q * piece, piece), piece)

    def spread(c, q, slot):
        return push(yr.at[c, bit(q)], zr.at[c, slot], zs.at[c % 4, q], zq.at[c, slot], device(q))

    def place(q):
        return pl.ds(pl.multiple_of(par * HALF + q * piece, piece), piece)

    def share(c, q, slot):
        return push(fin.at[c, place(slot)], fin.at[c, place(slot)], fs.at[c % 4, q], fq.at[c, slot], device(q))

    def back(c):
        return push(fin.at[c, halves(par)], fin.at[c, halves(par)], ss.at[4, c], rs.at[4, c], beside)

    def write(c):
        return pltpu.make_async_copy(fin.at[c], out_ref.at[rows(c)], os.at[c])

    def tiny(k, peer):
        return push(ta.at[k], tx.at[k], ts.at[k], tq.at[k], peer)

    def tiny_z(q, slot):
        return push(ta.at[3], tz.at[slot], tzs.at[q], tzq.at[slot], device(q))

    def stage(lag, first, last):
        c = step - FIRST - lag
        return c, (c >= first) & (c < last)

    peers = (sib, across, beside)
    for k in range(4):

        @pl.when(step == TINY_STEP + 2 * k)
        def _(k=k):
            if k > 0:
                tiny(k - 1, peers[k - 1]).wait()
                ta[k] = ta[k - 1] + tx[k - 1]
            if k < 3:
                tiny(k, peers[k]).start()
            else:
                tz[mine] = ta[3]

                @pl.loop(1, m)
                def _(j):
                    tiny_z(member(j), mine).start()

    c0, on0 = stage(0, 0, FULL_CH)

    @pl.when(on0)
    def _():
        for k in (1, 0):
            swap(c0, k).start()
            load(c0, k).start()

    c1, on1 = stage(1, 0, FULL_CH)

    @pl.when(on1)
    def _():
        for k in (1, 0):
            load(c1, k).wait()
            swap(c1, k).wait_recv()
            pair[c1, k] = pair[c1, k] + loc[c1 % 2, k]
            if k == 1:
                cross(c1).start()

    c2, on2 = stage(2, 0, CHUNKS)

    @pl.when(on2)
    def _():
        @pl.when(c2 < FULL_CH)
        def _():
            cross(c2).wait_recv()
            pair[c2, 0] = pair[c2, 0] + fin[c2]

        side(c2).start()

    c3, on3 = stage(3, 0, CHUNKS)

    @pl.when(on3)
    def _():
        side(c3).wait_recv()
        yr[c3] = yr[c3] + pair[c3, 0, halves(par)]

        @pl.loop(1, m)
        def _(j):
            spread(c3, member(j), mine).start()

    c4, on4 = stage(4, 0, CHUNKS)

    @pl.when(on4)
    def _():
        fin[c4, place(mine)] = yr[c4, bit(mine)]

        @pl.loop(1, m)
        def _(j):
            spread(c4, member(j), member(j)).wait_recv()
            fin[c4, place(mine)] = fin[c4, place(mine)] + zr[c4, member(j)]

        @pl.loop(1, m)
        def _(j):
            share(c4, member(j), mine).start()

    c5, on5 = stage(5, 0, CHUNKS)

    @pl.when(on5)
    def _():
        @pl.loop(1, m)
        def _(j):
            share(c5, member(j), member(j)).wait_recv()
            spread(c5, member(j), mine).wait_send()

        back(c5).start()

    c6, on6 = stage(6, 0, CHUNKS)

    @pl.when(on6)
    def _():
        back(c6).wait_recv()
        write(c6).start()

        @pl.loop(1, m)
        def _(j):
            share(c6, member(j), mine).wait_send()

    @pl.when(step == STEPS - 1)
    def _():
        @pl.loop(1, m)
        def _(j):
            tiny_z(member(j), member(j)).wait_recv()
            tiny_z(member(j), mine).wait_send()

        out_own().wait()
        for k in range(2):
            for i in range(4):
                if k + i > 0:
                    out_copy(k, i).wait_send()
                    out_in(k, i).wait_recv()
        total = tz[0]
        for q in range(1, m):
            total = total + tz[q]
        tout_ref[...] = total

        @pl.loop(0, CHUNKS)
        def _(c):
            @pl.when(c < FULL_CH)
            def _():
                for k in range(2):
                    swap(c, k).wait_send()
                cross(c).wait_send()

            side(c).wait_send()
            back(c).wait_send()
            write(c).wait()


def backward(n, args, ident):
    m = n // 2
    dma = pltpu.SemaphoreType.DMA

    def fixed(shape):
        return pl.BlockSpec(shape, lambda s: (0,) * len(shape), pipeline_mode=pl.Buffered(1))

    def mlp_at(s):
        return jnp.where(s < 4, 4 + s, jnp.where(s < 8, 0, jnp.where(s < 12, s - 8, 3)))

    def att_at(s):
        return jnp.where(s < 4, 4, jnp.where(s < 8, s, jnp.where(s < 12, 0, jnp.where(s < 16, s - 12, 3))))

    def by(index, shape, mode=None):
        zeros = (0,) * len(shape)
        return pl.BlockSpec((1,) + shape, lambda s: (index(s),) + zeros, pipeline_mode=mode)

    def spot(index, shape, k):
        return pl.BlockSpec((1, 1) + shape, lambda s: (index(s) % 4, index(s) // 4, k, 0, 0))

    one = pl.Buffered(1)
    lanes = (CHUNKS, ROWS, 128)
    in_specs = [
        fixed((4, 2, 192, 128)), by(lambda s: jnp.where(s < 4, 1, 0), (TOK, C), one),
        by(lambda s: jnp.where(s < 8, 1, 0), (TOK, C), one),
        fixed((2, 1, C)), fixed((2, 1, C)), fixed((2, 1, C)), fixed((2, 1, C)),
        spot(mlp_at, (4, 128, 512), 0), spot(mlp_at, (4, 128, 512), 1), spot(att_at, (3, C, 128), 0),
        spot(att_at, (1, 128, C), 8),
        by(mlp_at, (TOK, 512)), by(mlp_at, (TOK, 512)), by(att_at, (TOK, 384)),
        by(att_at, (NW, GROUP * WT, WT)), by(att_at, (TOK, 128)),
        fixed((8, C)), ANY, fixed((256, C)), fixed((8, C)), fixed((8, 256)), fixed((TOK, 128)), ANY,
    ]
    return pl.pallas_call(
        functools.partial(bwd_kernel, n),
        grid=(STEPS,),
        in_specs=in_specs,
        out_specs=[ANY, ANY, ANY, ANY, ANY, ANY, fixed((TINY, C))],
        out_shape=[
            sds(4, FULL_CH * ROWS, 128), sds(4, TOK, C), sds(4, 8, TOK), sds(2, 24, SUB, 128), sds(CHUNKS * ROWS, 128),
            sds(4, TOK, 256), sds(TINY, C),
        ],
        scratch_shapes=[
            pltpu.VMEM((C, TOK), bf16), pltpu.VMEM((C, TOK), bf16), pltpu.VMEM((TOK, C), bf16),
            pltpu.VMEM((TOK, C), bf16), pltpu.VMEM((TOK, C), f32), pltpu.VMEM((TOK, 384), f32),
            pltpu.VMEM((TOK, C), f32), pltpu.VMEM((2, MLP_ROWS, 128), f32), pltpu.VMEM((TOK, C), f32),
            pltpu.VMEM((8, TOK), f32), pltpu.VMEM((8, TOK), f32), pltpu.VMEM((TOK, 256), f32),
            pltpu.VMEM((2, 2, ROWS, 128), f32), pltpu.VMEM((CHUNKS, 2, ROWS, 128), f32),
            pltpu.VMEM((CHUNKS, HALF, 128), f32), pltpu.VMEM((CHUNKS, m, HALF // m, 128), f32),
            pltpu.VMEM(lanes, f32), pltpu.VMEM((4, TINY, C), f32), pltpu.VMEM((3, TINY, C), f32),
            pltpu.VMEM((m, TINY, C), f32),
            dma((2,)), dma((7,)), dma((7,)), dma((2, 3)), dma((2, 3)), dma((2,)), dma((4,)),
            dma((5, CHUNKS)), dma((5, CHUNKS)), dma((4, m)), dma((CHUNKS, m)), dma((4, m)),
            dma((CHUNKS, m)), dma((2, 2)), dma((CHUNKS,)), dma((3,)), dma((3,)), dma((m,)), dma((m,)),
            dma((2, 4)), dma((2, 4)), dma((1,)),
        ],
        compiler_params=pltpu.CompilerParams(
            collective_id=ident, has_side_effects=True, vmem_limit_bytes=60 << 20,
            dimension_semantics=("arbitrary",),
        ),
        name="backward",
    )(*args)


def column_pick():
    pick = np.zeros((19, WIN, WIN), np.float32)
    for a in range(WIN):
        for b in range(WIN):
            pick[a - b + WIN - 1, a, b] = 1.0
    return pick


def row_pick():
    pick = np.zeros((19, WIN, WIN, WIN, 2, 2, SUB), np.float32)
    for pr in range(WIN):
        for qr in range(WIN):
            for qc in range(WIN):
                pick[pr - qr + WIN - 1, qc, pr, 0, qr // 5, qc // 5, (qr % 5) * 5 + qc % 5] = 1.0
    return pick[:, :, :, 0].reshape(190, WIN * WT)


def bias_of(table):
    heads = table.shape[0]
    grid = table.reshape(heads, 19, 19)
    columns = jnp.einsum("hrd,dab->harb", grid, jnp.asarray(column_pick()), precision="highest")
    rows = jnp.dot(columns.reshape(heads * WIN, 190), jnp.asarray(row_pick()), precision="highest")
    rows = rows.reshape(heads, 2, 5, 2, 5, WT).transpose(0, 3, 1, 4, 2, 5)
    rows = rows.reshape(heads, 4, REAL, WT)
    return jnp.pad(rows, ((0, 0), (0, 0), (0, SUB - REAL), (0, 0))).reshape(heads, WT, WT)


def table_of(dbias):
    heads = dbias.shape[0]
    rows = dbias.reshape(heads, 4, SUB, WT)[:, :, :REAL].reshape(heads, 2, 2, 5, 5, WT)
    rows = rows.transpose(0, 2, 4, 1, 3, 5).reshape(heads * WIN, WIN * WT)
    columns = lax.dot_general(rows, jnp.asarray(row_pick()), NT, precision="highest")
    columns = columns.reshape(heads, WIN, 19, WIN)
    return jnp.einsum("harb,dab->hrd", columns, jnp.asarray(column_pick()), precision="highest")


def shards(
    patches, merge_gain, merge_shift, merge_weight, first_gain, first_shift, input_weight,
    input_bias, position_table, output_weight, output_bias, second_gain, second_shift,
    expand_weight, expand_bias, shrink_weight, shrink_bias, page_map, valid_flags, cotangent,
):
    sp_count = lax.axis_size("sp")
    tp = lax.axis_index("tp")
    sp = lax.axis_index("sp")

    tables = position_table.transpose(0, 2, 1).reshape(8, 361)
    bias = bias_of(tables).reshape(2, 512, 128)
    pairs = jnp.concatenate([input_bias, jnp.zeros_like(input_bias)], axis=2).reshape(2, 512)
    small = jnp.concatenate([expand_bias, pairs, jnp.zeros((4, 512), f32)], axis=0)
    three = lambda x: x.reshape(2, 1, C)

    valid = valid_flags.astype(f32).reshape(2, 5, 24, 5).transpose(0, 2, 1, 3).reshape(2, 24, REAL)
    valid = jnp.pad(valid, ((0, 0), (0, 0), (0, SUB - REAL)))
    own = lambda grid: lax.dynamic_slice_in_dim(grid, 6 * tp, 6, 1).reshape(2, NW, 2 * SUB)
    here_ = own(valid)
    next_ = own(jnp.roll(valid, -1, axis=1))
    blank = jnp.zeros((NW, 2 * SUB), f32)
    line = lambda a, c: jnp.pad(jnp.concatenate([a, c], axis=1), ((0, 5), (0, 0)))
    valid0, valid1, valids = line(here_[0], here_[1]), line(next_[1], blank), line(blank, next_[0])
    pages = jnp.concatenate([page_map, page_map[:1]], axis=0)
    pages = jnp.concatenate([pages, pages[:, :1]], axis=1)
    pages = lax.dynamic_slice(pages, (sp, 3 * tp), (2, 4))
    page = jnp.stack([pages[:, :3], pages[:, 1:]], axis=2).transpose(1, 0, 2)
    wrap_row = (jnp.arange(2) == 1) & (sp == sp_count - 1)
    wrap_col = (jnp.arange(2) == 1)[None, :] & (jnp.arange(NW) == NW - 1)[:, None] & (tp == 3)
    region = page * 4 + 2 * wrap_row[None, :, None].astype(jnp.int32) + wrap_col[:, None, :].astype(jnp.int32)
    region = jnp.broadcast_to(region[..., None], (NW, 2, 2, SUB)).reshape(NW, WT)
    region = jnp.stack([jnp.zeros_like(region), region])
    regc, regr = region.reshape(2, TOK, 1), jnp.pad(region, ((0, 0), (0, 5), (0, 0)))

    gain = merge_gain.reshape(2, 2, 64).transpose(1, 0, 2).reshape(1, 256)
    offset = merge_shift.reshape(2, 2, 64).transpose(1, 0, 2).reshape(1, 256)
    mgain = jnp.concatenate([gain, offset, jnp.zeros((6, 256), f32)], axis=0)
    weight = merge_weight.reshape(2, 2, 64, C).transpose(1, 0, 2, 3).reshape(256, C)
    quads = patches.reshape(2, 5, 2, 4, NW, 2, 5, 128).transpose(3, 4, 0, 5, 1, 6, 2, 7).reshape(4, NW, 4, REAL, 256)
    quads = jnp.pad(quads, ((0, 0), (0, 0), (0, 0), (0, SUB - REAL), (0, 0))).reshape(4, TOK, 256)
    cot = jnp.roll(cotangent.reshape(2, 5, 24, 5, 128), -1, axis=2).transpose(0, 2, 1, 3, 4).reshape(2, 24, REAL, 128)
    cot = jnp.pad(cot, ((0, 0), (0, 0), (0, SUB - REAL), (0, 0)))

    nall, wall, cot, fields, middles, qkv, p, att, hid, slope, stat, vecs, squares, out = forward(
        sp_count,
        (
            quads, weight, mgain, input_weight.transpose(0, 2, 1, 3), bias, output_weight.reshape(2, 1, 128, C),
            expand_weight.reshape(2, 4, 128, 512), shrink_weight.reshape(2, 4, 128, C), small,
            three(first_gain), three(first_shift), three(output_bias), three(second_gain), three(second_shift),
            three(shrink_bias), regc, regr, valid0, valid1, valids, cot,
        ),
        1,
    )
    _, _, _, output, packed, gquads, tiny = backward(
        sp_count,
        (
            cot.reshape(4, 2, 192, 128), middles, fields, three(first_gain), three(first_shift),
            three(second_gain), three(second_shift), wall, wall, nall, wall, hid, slope, qkv, p, att,
            squares, quads, weight, vecs, mgain, stat, out.reshape(4, 2, 6, SUB, 128),
        ),
        2,
    )
    output = jnp.roll(output[:, :, :REAL], 1, axis=1).reshape(2, 24, 5, 5, 128)
    output = output.transpose(0, 2, 1, 3, 4).reshape(10, 120, 128)
    gquads = gquads.reshape(4, NW, 4, SUB, 256)[:, :, :, :REAL].reshape(4, NW, 2, 2, 5, 5, 2, 128)
    patches_grad = gquads.transpose(2, 4, 6, 0, 1, 3, 5, 7).reshape(20, 240, 64)
    small1, small2 = tiny[0:6].reshape(2, 3, C), tiny[6:12].reshape(2, 3, C)
    dbe, dbqkv = tiny[12:20].reshape(2, 4, 512), tiny[20:28, :384].reshape(2, 4, 384)
    sums = jnp.sum(tiny[28:34], axis=1)
    sums, count = sums[:5], sums[5]
    dmgs = lax.dynamic_index_in_dim(tiny[36:40], tp, 0, keepdims=False)
    dmg, dms = dmgs[:256], dmgs[256:]
    blocks = packed.reshape(CHUNKS, ROWS, 128)
    cut = lambda lo, hi: jnp.stack([blocks[13 + lo : 13 + hi], blocks[lo:hi]])
    lanes = lambda x: x.transpose(0, 2, 1, 3).reshape(2, x.shape[2], C)
    g_we, g_ws = lanes(cut(0, 4)), lanes(cut(4, 8))
    g_qkv = cut(8, 11).transpose(0, 2, 1, 3)
    g_wo = lanes(cut(11, 12).reshape(2, 4, 128, 128))
    dbias = cut(12, 13).reshape(8, WT, WT)
    g_tab = table_of(dbias).reshape(2, 4, 361).transpose(0, 2, 1)
    dmw = blocks[26:28].reshape(4, 256, 128).transpose(1, 0, 2).reshape(256, C)
    own4 = lambda x, axis: lax.dynamic_index_in_dim(x, tp, axis, keepdims=False)
    dbqkv = own4(dbqkv, 1).reshape(2, 3, 128)
    g_bias = jnp.stack([dbqkv[:, 0], dbqkv[:, 2]], axis=1)
    g_be = own4(dbe, 1).reshape(2, 512)
    back = lambda x: x.reshape((2, 2, 64) + x.shape[1:]).swapaxes(0, 1).reshape((4, 64) + x.shape[1:])
    rms = jnp.sqrt(sums / (count * C))
    return (
        output, patches_grad, back(dmg), back(dms), back(dmw), small1[:, 0], small1[:, 1], g_qkv, g_bias,
        g_tab, g_wo, small1[:, 2], small2[:, 0], small2[:, 1], g_we, g_be, g_ws, small2[:, 2], rms,
    )


def solution(mesh):
    placed = (
        P("sp", None, "tp"), P(None, "tp"), P(None, "tp"), P(None, "tp", None), P(), P(),
        P(None, None, None, "tp"), P(None, None, "tp"), P(None, None, "tp"), P(None, "tp", None),
        P(), P(), P(), P(None, None, "tp"), P(None, "tp"), P(None, "tp", None), P(), P(),
        P("sp", None), P("sp", None, "tp"),
    )
    results = (
        P("sp", None, "tp"), P("sp", None, "tp"), P(None, "tp"), P(None, "tp"), P(None, "tp", None),
        P(), P(), P(None, None, None, "tp"), P(None, None, "tp"), P(None, None, "tp"),
        P(None, "tp", None), P(), P(), P(), P(None, None, "tp"), P(None, "tp"), P(None, "tp", None),
        P(), P(),
    )
    return jax.shard_map(shards, mesh=mesh, in_specs=placed, out_specs=results, check_vma=False)
```

time: 739 us -> 483 us (0.65)
  Pallas kernels: 510 us -> 416 us
  other arithmetic: 55.8 us -> 11.4 us
  local copies, waits for them, and re-layouts: 88.4 us -> 46.2 us
  starting transfers between devices: 19.5 us -> 0 us
  waiting for transfers between devices: 18.4 us -> 0 us
  between operations: 15.9 us -> 1.81 us
  blocking collectives: 10.4 us -> 0 us
    pallas_call x5 -> x1, Pallas kernels: 246 us -> 151 us  [forward(): pl.pallas_call(functools.partial(fwd_kernel, n), grid=(F_STEPS,), in_spec...]
    concatenate x18 -> x5, other arithmetic: 37.2 us -> 2.23 us  [the longest x1 0.68 us: shards(): jnp.concatenate([a, c], axis=1)]
    ppermute x7 -> x0, starting transfers between devices: 11.3 us -> none  [shift_along(): lax.ppermute(x, axis, [((i - distance) % count, i) for i in range(count)])]
    ppermute x7 -> x0, waiting for transfers between devices: 10.9 us -> none  [shift_along(): lax.ppermute(x, axis, [((i - distance) % count, i) for i in range(count)])]
    psum x1 -> x0, blocking collectives: 10.4 us -> none  [shards(): lax.psum((jnp.dot(gain, weight, precision='highest'), jnp.dot(offset, wei...]
    all_to_all x2 -> x0, starting transfers between devices: 8.13 us -> none  [the longest x1 4.48 us: shards(): lax.all_to_all(cotangent.reshape(10, 120, 1, 128), 'tp', 1, 2, tiled=True)]
    all_to_all x2 -> x0, waiting for transfers between devices: 7.53 us -> none  [the longest x1 7.53 us: shards(): lax.all_to_all(out_nat.reshape(10, 30, 4, 128), 'tp', 2, 1, tiled=True)]
    unnamed x127 -> x49, local copies, waits for them, and re-layouts: 16.3 us -> 10.4 us
  transfers between devices with their start and end apart: 10 -> 0, of which waited for: 4 -> 0; matrix products, arithmetic and copies ran while one was open for 14% -> 0% of each run, Pallas kernels for 30% -> 0%
where the time goes in v3:
time: 483 us; the launch traced here: 482 us
  Pallas kernels  416 us (86%)
  local copies, waits for them, and re-layouts  46.2 us (10%)
  other arithmetic  11.4 us (2%)
  matrix products  6.48 us (1%)
    pallas_call x1, Pallas kernels, backward(): pl.pallas_call(functools.partial(bwd_kernel, n), grid=(STEPS,), in_specs=...  264 us
    pallas_call x1, Pallas kernels, forward(): pl.pallas_call(functools.partial(fwd_kernel, n), grid=(F_STEPS,), in_spec...  151 us
    unnamed x49, local copies, waits for them, and re-layouts  10.4 us

profile of v3, /device:TPU:0, one launch (start us, length us, event | category | flops | bytes accessed | tf_op | source)
XLA Modules:
  0.0 481.5 jit_solution(15312342310455413910)
XLA Ops:
  0.7 0.7 slice.161
  1.4 0.7 pad_add_fusion
  2.0 0.8 fusion.7
  3.3 1.0 reshape.340.refs_15_
  4.4 0.6 pad.36.refs_16_
  5.0 0.7 convert_element_type.25
  6.4 0.7 select_maximum_fusion.refs_17_
  7.5 0.6 pad.79.refs_18_
  8.3 0.7 pad.80.refs_19_
  8.9 1.2 reshape.306
  10.6 0.9 pad.41.refs_20_
  11.5 1.9 copy.95
  13.4 1.5 reshape.283
  14.9 2.5 copy.146
  17.4 1.0 reshape.341
  18.5 1.3 pad.34.clone
  19.8 0.8 copy.98
  20.9 0.7 maximum_maximum_fusion.1.refs_2_.refs_20_
  24.1 0.7 convolution_bitcast_fusion
  24.8 0.6 copy.101
  25.7 0.7 convolution_bitcast_fusion.1
  26.5 0.8 pad.35.clone
  27.5 0.7 maximum_maximum_fusion.refs_8_
  29.3 151.4 %forward.1 = (f32[4,2,4,512,128]{4,3,2,1,0:T(8,128)}, f32[4,2,9,128,512]{4,3,2,1,0:T(8,128)}, f32[4,2,6,32,128]{4,3,2,1,0:T(8,128)}, f32[2,384,512]{2,1,0:T(8,12...) custom-call(f32[4,384,256]{2,1,0:T(8,128)} %bitcast.140, ...), custom_call_target="tpu_custom_call" | custom-call | tf_op jit(solution)/shard_map/forward/pallas_call | solution.py:536
  180.7 264.3 %backward.1 = (f32[4,13312,128]{2,1,0:T(8,128)}, f32[4,384,512]{2,1,0:T(8,128)}, f32[4,8,384]{2,1,0:T(8,128)}, f32[2,24,32,128]{3,2,1,0:T(8,128)}, f32[14336,128...) custom-call(f32[4,2,192,128]{3,2,1,0:T(8,128)} %bitcast.168, f32[2,384,512]{2,1,0:T(8,128)} %get-tuple-element.38.refs_1_, ...), custom_call_target="tpu_custom_call" | custom-call | tf_op jit(solution)/shard_map/backward/pallas_call | solution.py:1067
  445.0 0.9 slice_reduce_fusion
  447.7 2.5 fusion.8
  450.2 2.6 copy_bitcast_fusion
  452.8 0.6 copy_bitcast_fusion.4
  453.4 0.8 slice.199
  454.2 0.6 copy_bitcast_fusion.5
  454.8 1.3 fusion.9
  456.1 0.9 copy_bitcast_fusion.2
  457.5 3.9 fusion.15
  461.5 1.2 convolution_bitcast_fusion.2
  462.6 0.7 reshape.325
  463.4 0.7 slice.185
  464.7 1.5 fusion.10
  466.2 1.3 maximum_bitcast_fusion.2
  467.5 0.6 copy_bitcast_fusion.8
  468.2 0.7 reshape.342
  468.9 1.6 copy.116
  470.4 2.5 reshape.314
  472.9 1.8 copy.128
  475.4 0.9 reshape.311
  476.3 1.1 slice.179
  478.0 0.8 copy.120
  479.4 0.7 slice.176
  (116 shorter events, 12.4 us)
Async XLA Ops:
  18.4 1.4 copy-start.4
  18.4 2.2 copy-start.16
  18.4 2.3 copy-start.17
  18.5 3.1 copy-start.9
  18.5 3.7 copy-start.10
  18.5 4.3 copy-start.11
  18.5 4.9 %copy-start.12 = (f32[2,512]{1,0:T(2,128)S(1)}, f32[2,512]{1,0:T(2,128)}, u32[]{:S(2)}) copy-start(f32[2,512]{1,0:T(2,128)} %param.36) | copy-start | bytes 12292
  18.5 5.5 %copy-start.7 = (f32[2,361,4]{1,2,0:T(4,128)S(1)}, f32[2,361,4]{1,2,0:T(4,128)}, u32[]{:S(2)}) copy-start(f32[2,361,4]{1,2,0:T(4,128)} %param.32) | copy-start | bytes 34660
  18.5 5.5 %copy-start.6 = (f32[19,10,10,1]{0,2,3,1:T(8,128)S(1)}, f32[19,10,10,1]{0,2,3,1:T(8,128)}, u32[]{:S(2)}) copy-start(f32[19,10,10,1]{0,2,3,1:T(8,128)} %constant.90) | copy-start | bytes 22804
  20.6 5.0 %copy-start.2 = (f32[2,5,128,190,1,1]{2,3,1,0,5,4:T(8,128)S(1)}, f32[2,5,128,190,1,1]{2,3,1,0,5,4:T(8,128)}, u32[]{:S(2)}) copy-start(f32[2,5,128,190,1,1]{2,3,1,0,5,4:T(8,128)} %constant.91) | copy-start | bytes 2918404
  25.6 1.7 copy-start.15
  25.7 1.8 copy-start.8
  25.7 2.5 copy-start.13
  25.7 3.1 copy-start.14
  456.1 1.5 copy-start.1
  457.0 4.5 copy-start.5
  466.2 2.0 copy-start
  472.9 1.8 copy-start.3

commit v4 on v3

--- a/solution.py
+++ b/solution.py
@@ -105,17 +105,19 @@
     )
 
 
-ROWS = 512
-HALF = ROWS // 2
-MLP_ROWS, ATT_ROWS = 4096, 2560
-MLP_CH, ATT_CH = MLP_ROWS // ROWS, ATT_ROWS // ROWS
-FULL_CH = 2 * (MLP_CH + ATT_CH)
-CHUNKS = FULL_CH + 2
-FIRST = 4
+MLP_ROWS, ATT_ROWS = 4096, 2048
+BLOCK_ROWS = MLP_ROWS + ATT_ROWS
+FIRST = 2
 AG_STEP = 15
-MERGE_STEP = 20
-TINY_STEP = 25
-STEPS = FIRST + CHUNKS + 6
+STEPS = 17
+
+
+def chunk_plan(n):
+    rows = 256 if n <= 16 else 512
+    every = 2 * BLOCK_ROWS // rows
+    return rows, every, every + 1024 // rows, 3 if rows == 256 else 1
+
+
 TINY = 40
 COLS = [(0, 0, 0, 1), (0, 1, 1, 0), (1, 0, 1, 1), (1, 1, 2, 0), (2, 0, 2, 1)]
 
@@ -126,21 +128,24 @@
 
 NCH = 13
 GCH = 2 * NCH
-F_STEPS = 31
+F_STEPS = 19
+
+
+GATHERED = (0, 0, 0, 3, 9, 10, 11, 13, 17, 18, 19, 20, 22, 24, 26, 28, 30, 30, 30, 30)
+AHEAD = 6
 
 
 def fwd_order(s):
-    att = jnp.where(s < 3, 0, jnp.where(s < 7, 1, jnp.where(s < 8, 2, jnp.where(s < 17, 3, jnp.where(
-        s < 18, 4, jnp.where(s < 20, 5, jnp.where(s < 21, 6, 7)))))))
-    mlp = jnp.where(s < 10, 0, jnp.where(s < 15, 1, jnp.where(s < 16, 2, jnp.where(s < 22, 3, jnp.where(
-        s < 23, 4, jnp.where(s < 28, 5, jnp.where(s < 29, 6, 7)))))))
+    att = jnp.where(s < 2, 0, jnp.where(s < 6, s - 2, jnp.where(s < 10, 3, jnp.where(s < 14, s - 6, 7))))
+    mlp = jnp.where(s < 6, 0, jnp.where(s < 10, s - 6, jnp.where(s < 14, 3, jnp.where(s < 18, s - 10, 7))))
     return att, mlp
 
 
-def among(step, steps):
-    found = step == steps[0]
-    for s in steps[1:]:
-        found = found | (step == s)
+def gathered(s):
+    found = jnp.int32(GATHERED[0])
+    for k in range(1, len(GATHERED)):
+        if GATHERED[k] != GATHERED[k - 1]:
+            found = jnp.where(s >= k, GATHERED[k], found)
     return found
 
 
@@ -155,7 +160,7 @@
     ) = refs[21:35]
     (
         nb, wb, smb, pb, pr, px, stb, str_, stx, vp, vr, vc, field, nh, nl, mixed, moved,
-        lsem, ss, sr, xs, xr, ys, yr, s2s, s2r, s3s, s3r, sms, smr, rss, rsr, vps, vpr, vvs, vvr,
+        lsem, ss, sr, xs, xr, ys, yr, zs, zr, s2s, s2r, sms, smr, rss, rsr, vps, vpr, vvs, vvr,
         mvs, mvr, cbs, cbr, cbl, hn, hw,
     ) = refs[35:]
     step = pl.program_id(0)
@@ -190,28 +195,51 @@
 
         @pl.when(small)
         def _():
-            act(nb, kn, 256)
+            act(nb, kn, 512)
 
         @pl.when(jnp.logical_not(small))
         def _():
-            act(wb, kw, 64)
-
-    def half(size, h):
-        return pl.ds(pl.multiple_of(h * size, size), size)
-
-    def x_copy(c, buf, k, size):
-        return push(buf.at[0, k, half(size, par)], buf.at[2, k, half(size, par)], xs.at[c], xr.at[c], across)
-
-    def y_copy(c, buf, k, size):
-        return push(buf.at[2, k, half(size, par)], buf.at[2, k, half(size, par)], ys.at[c], yr.at[c], beside)
-
-    def s2_copy(c, buf, k, size):
-        return push(buf.at[2, k, half(size, par)], buf.at[3, k, half(size, par)], s2s.at[c], s2r.at[c], sib)
-
-    def s3_copy(c, buf, k, size):
-        return push(
-            buf.at[2, k, half(size, 1 - par)], buf.at[3, k, half(size, 1 - par)], s3s.at[c], s3r.at[c], sib
-        )
+            act(wb, kw, 128)
+
+    zpar = lax.rem(sp // 2, 2)
+    far = (sp ^ 2, tp)
+
+    def deep(c):
+        return c % 3 != 0
+
+    def cut(size, k):
+        return pl.ds(pl.multiple_of(k * size, size), size)
+
+    def x_copy(c, buf, k, size, low):
+        d = cut(size // 4, 2 * zpar + par) if low else cut(size // 2, par)
+        return push(buf.at[0, k, d], buf.at[2, k, d], xs.at[c], xr.at[c], across)
+
+    def y_copy(c, buf, k, size, low):
+        d = cut(size // 4, 2 * zpar + par) if low else cut(size // 2, par)
+        return push(buf.at[2, k, d], buf.at[2, k, d], ys.at[c], yr.at[c], beside)
+
+    def z_copy(c, buf, k, size):
+        d = cut(size // 2, zpar)
+        return push(buf.at[2, k, d], buf.at[2, k, d], zs.at[c], zr.at[c], far)
+
+    def s_copy(which, c, buf, k, size):
+        d = cut(size // 2, which)
+        send, recv = (s2s, s2r)
+        return push(buf.at[2, k, d], buf.at[3, k, d], send.at[which, c], recv.at[which, c], sib)
+
+    def x_start(c):
+        def act(buf, k, size):
+            for low in (False, True):
+
+                @pl.when(deep(c) == low)
+                def _(low=low):
+                    x_copy(c, buf, k, size, low).start()
+
+        each(c, act)
+
+    def s_in(c, buf, k, size):
+        for h in range(2):
+            s_copy(h, c, buf, k, size).wait_recv()
 
     def rs_copies(k):
         if k < 2:
@@ -258,7 +286,7 @@
         for copy in own():
             copy.start()
         barrier = pltpu.get_barrier_semaphore()
-        near = [beside] + [(sp, tp ^ i) for i in (1, 2, 3)]
+        near = [beside, far] + [(sp, tp ^ i) for i in (1, 2, 3)]
         near += [(up, tp ^ i) for i in range(4)] + [(down, tp ^ i) for i in range(4)]
         for peer in near:
             pl.semaphore_signal(barrier, inc=1, device_id=peer, device_id_type=MESH)
@@ -287,7 +315,7 @@
                 sm_copy(0).start()
                 sm_copy(1).start()
                 for c in (0, 1):
-                    x_copy(c, nb, c, 256).start()
+                    x_copy(c, nb, c, 512, c % 3 != 0).start()
         for copy in rs_copies(1):
             copy.wait_recv()
         pb[2] = pb[2] + pr[1]
@@ -300,7 +328,8 @@
             copy.wait_recv()
         pb[0] = pb[0] + pr[0]
         stb[0] = stb[0] + str_[0]
-        x_copy(2, nb, 2, 256).start()
+        for c in range(2, AHEAD):
+            x_copy(c, nb if c < 4 else wb, c if c < 4 else (8 if c == 4 else c - 5), 512 if c < 4 else 128, c % 3 != 0).start()
         sq_ref[...] = jnp.zeros_like(sq_ref)
         os_ref[...] = jnp.zeros_like(os_ref)
         vec_ref[...] = jnp.zeros_like(vec_ref)
@@ -334,7 +363,7 @@
 
     att, mlp = fwd_order(step)
 
-    @pl.when(among(step, (2, 3, 7, 8, 17, 18, 20, 21)))
+    @pl.when(((step >= 2) & (step < 6)) | ((step >= 10) & (step < 14)))
     def _():
         b, i = att // 4, att % 4
 
@@ -366,9 +395,8 @@
         def _():
             for r in range(5):
                 c = b * NCH + r
-                buf, k, size = (nb, 4 * b + r, 256) if r < 4 else (wb, 9 * b + 8, 64)
-                s2_copy(c, buf, k, size).wait_recv()
-                s3_copy(c, buf, k, size).wait_recv()
+                buf, k, size = (nb, 4 * b + r, 512) if r < 4 else (wb, 9 * b + 8, 128)
+                s_in(c, buf, k, size)
 
         pltpu.make_async_copy(nb.at[i, pl.ds(4 * b, 4)], nall.at[i, b], hn.at[b, i]).start()
         w = jnp.concatenate([nb[i, 4 * b + j] for j in range(3)], axis=1)
@@ -400,7 +428,7 @@
             mid_out[0] = middle
             sq_ref[pl.ds(2 * b, 1), :] = colsum(mixed[...] * mixed[...] * vc[b])
 
-    @pl.when(among(step, (9, 10, 15, 16, 22, 23, 28, 29)))
+    @pl.when(((step >= 6) & (step < 10)) | ((step >= 14) & (step < 18)))
     def _():
         b, i = mlp // 4, mlp % 4
 
@@ -425,8 +453,7 @@
         def _():
             for r in range(8):
                 c = b * NCH + 5 + r
-                s2_copy(c, wb, 9 * b + r, 64).wait_recv()
-                s3_copy(c, wb, 9 * b + r, 64).wait_recv()
+                s_in(c, wb, 9 * b + r, 128)
 
         pltpu.make_async_copy(wb.at[i, pl.ds(9 * b, 9)], wall.at[i, b], hw.at[b, i]).start()
         we = wb[i, pl.ds(9 * b, 4)].reshape(512, 512)
@@ -461,13 +488,7 @@
                                 w * WT + r * 64 : w * WT + r * 64 + 64, t * 128 : (t + 1) * 128
                             ]
 
-    p = step - 1
-
-    @pl.when((p >= 1) & (p + 2 < GCH))
-    def _():
-        each(p + 2, lambda buf, k, size: x_copy(p + 2, buf, k, size).start())
-
-    @pl.when(step == GCH - 1)
+    @pl.when(step == 15)
     def _():
         cot_own().start()
         for k in range(2):
@@ -475,22 +496,63 @@
                 if k + i > 0:
                     cot_copy(k, i).start()
 
-    @pl.when((p >= 0) & (p < GCH))
-    def _():
-        def act(buf, k, size):
-            x_copy(p, buf, k, size).wait_recv()
-            y_copy(p, buf, k, size).start()
-            s2_copy(p, buf, k, size).start()
-
-        each(p, act)
-
-    @pl.when((p >= 1) & (p <= GCH))
-    def _():
-        def act(buf, k, size):
-            y_copy(p - 1, buf, k, size).wait_recv()
-            s3_copy(p - 1, buf, k, size).start()
-
-        each(p - 1, act)
+    def both(c, act):
+        def run(buf, k, size):
+            for low in (False, True):
+
+                @pl.when(deep(c) == low)
+                def _(low=low):
+                    act(buf, k, size, low)
+
+        each(c, run)
+
+    @pl.loop(gathered(step), gathered(step + 1))
+    def _(p):
+        @pl.when(p + AHEAD < GCH)
+        def _():
+            x_start(p + AHEAD)
+
+        @pl.when(p < GCH)
+        def _():
+            def act(buf, k, size, low):
+                x_copy(p, buf, k, size, low).wait_recv()
+                y_copy(p, buf, k, size, low).start()
+                if not low:
+                    for h in range(2):
+
+                        @pl.when(par == h)
+                        def _(h=h):
+                            s_copy(h, p, buf, k, size).start()
+
+            both(p, act)
+
+        @pl.when((p >= 2) & (p - 2 < GCH))
+        def _():
+            def act(buf, k, size, low):
+                y_copy(p - 2, buf, k, size, low).wait_recv()
+                half_here = zpar if low else 1 - par
+                if low:
+                    z_copy(p - 2, buf, k, size).start()
+                for h in range(2):
+
+                    @pl.when(half_here == h)
+                    def _(h=h):
+                        s_copy(h, p - 2, buf, k, size).start()
+
+            both(p - 2, act)
+
+        @pl.when((p >= 4) & (p - 4 < GCH))
+        def _():
+            def act(buf, k, size, low):
+                if low:
+                    z_copy(p - 4, buf, k, size).wait_recv()
+                    for h in range(2):
+
+                        @pl.when(1 - zpar == h)
+                        def _(h=h):
+                            s_copy(h, p - 4, buf, k, size).start()
+
+            both(p - 4, act)
 
     @pl.when(step == F_STEPS - 1)
     def _():
@@ -509,13 +571,15 @@
 
         @pl.loop(0, GCH)
         def _(c):
-            def act(buf, k, size):
-                x_copy(c, buf, k, size).wait_send()
-                y_copy(c, buf, k, size).wait_send()
-                s2_copy(c, buf, k, size).wait_send()
-                s3_copy(c, buf, k, size).wait_send()
-
-            each(c, act)
+            def act(buf, k, size, low):
+                x_copy(c, buf, k, size, low).wait_send()
+                y_copy(c, buf, k, size, low).wait_send()
+                if low:
+                    z_copy(c, buf, k, size).wait_send()
+                for h in range(2):
+                    s_copy(h, c, buf, k, size).wait_send()
+
+            both(c, act)
 
 
 def forward(n, args, ident):
@@ -530,7 +594,7 @@
 
     att_at = lambda s: fwd_order(s)[0]
     mlp_at = lambda s: fwd_order(s)[1]
-    second = lambda s: jnp.where(s < 17, 0, 1)
+    second = lambda s: jnp.where(s < 10, 0, 1)
     vm = lambda *shape: pltpu.VMEM(shape, f32)
     two = fixed((2, 1, C))
     return pl.pallas_call(
@@ -556,7 +620,7 @@
             vm(4, 8, TOK), vm(2, 8, TOK), vm(8, TOK), vm(4, 8, C), vm(8, 128), vm(2, TOK, 1), vm(TOK, C),
             pltpu.VMEM((TOK, C), bf16), pltpu.VMEM((TOK, C), bf16), vm(TOK, C), vm(TOK, C),
             dma((11,)), dma((2, 3)), dma((2, 3)), dma((GCH,)), dma((GCH,)), dma((GCH,)), dma((GCH,)),
-            dma((GCH,)), dma((GCH,)), dma((GCH,)), dma((GCH,)), dma((3,)), dma((3,)), dma((2, 3)), dma((2, 3)),
+            dma((GCH,)), dma((GCH,)), dma((2, GCH)), dma((2, GCH)), dma((3,)), dma((3,)), dma((2, 3)), dma((2, 3)),
             dma((3,)), dma((3,)), dma((1,)), dma((1,)), dma((7,)), dma((7,)), dma((2, 4)), dma((2, 4)),
             dma((1,)), dma((2, 4)), dma((2, 4)),
         ],
@@ -568,22 +632,52 @@
     )(*args)
 
 
+def table_line(dbias, pick, pile):
+    high, low = split(dbias)
+    spread = mm(high, pick, NN) + mm(low, pick, NN)
+    spread = jnp.concatenate([spread[h * WT : (h + 1) * WT] for h in range(GROUP)], axis=1)
+    high, low = split(spread)
+    piled = mm(pile, high, NN) + mm(pile, low, NN)
+    total = piled[0:16]
+    for pc in range(1, WIN):
+        total = total + pltpu.roll(piled[pc * 16 : pc * 16 + 16], pc, 1)
+    row = lax.broadcasted_iota(jnp.int32, total.shape, 0)
+    line = jnp.where(row == 0, total, 0.0)
+    for pr in range(1, WIN):
+        line = line + jnp.where(row == pr, pltpu.roll(total, 19 * pr, 1), 0.0)
+    return colsum(line)
+
+
+def table_picks():
+    pick = np.zeros((WT, 384), np.float32)
+    pile = np.zeros((WIN, 16, WT), np.float32)
+    for r in range(WIN):
+        for c in range(WIN):
+            place = (r // 5) * 64 + (c // 5) * SUB + (r % 5) * 5 + c % 5
+            pick[place, (9 - r) * 19 + 9 - c] = 1.0
+            pile[c, r, place] = 1.0
+    return jnp.asarray(pick, bf16), jnp.asarray(pile.reshape(160, WT), bf16)
+
+
 def bwd_kernel(n, *refs):
     (
         cot_ref, mid_ref, field_ref, g1_ref, b1_ref, g2_ref, b2_ref, we_ref, ws_ref, wqkv_ref, wo_ref,
         hid_ref, slope_ref, qkv_ref, p_ref, att_ref, sq_ref, q_ref, mw_ref, vec_ref, mg_ref, stat_ref, os_ref,
-    ) = refs[:23]
-    pack, gall, exall, ob, out_ref, gq_ref, tout_ref = refs[23:30]
+        pick_ref, pile_ref,
+    ) = refs[:25]
+    pack, gall, exall, ob, out_ref, gq_ref, tout_ref = refs[25:32]
     (
         nth, ntl, gh, gl, acc, dqkv, gf, gbuf, moved, ext, extin, qbuf,
-        loc, pair, yr, zr, fin, ta, tx, tz,
-        gsem, mvs, mvr, ags, agr, agl, msem, ss, rs, zs, zq, fs, fq, ls, os, ts, tq, tzs, tzq, obs, obr, obl,
-    ) = refs[30:]
+        loc, pair, yr, zr, fin, ta, tx, tz, tsh, tr,
+        gsem, mvs, mvr, ags, agr, agl, msem, ss, rs, zs, zq, fs, fq, ls, os, tzs, tzq, obs, obr, obl, tss, tsq,
+    ) = refs[32:]
     step = pl.program_id(0)
     dmw, gqbuf = moved.at[pl.ds(0, 256)], dqkv.at[:, pl.ds(0, 256)]
     sp, tp, sib, across, beside = here()
     par, mine = sp & 1, sp // 2
     m = n // 2
+    ROWS, FULL_CH, CHUNKS, RATE = chunk_plan(n)
+    HALF = ROWS // 2
     piece = HALF // m
     up, down, right = lax.rem(sp + 1, n), lax.rem(sp + n - 1, n), lax.rem(tp + 1, 4)
 
@@ -620,6 +714,7 @@
             pl.semaphore_signal(barrier, inc=1, device_id=device(member(j)), device_id_type=MESH)
 
         ta[...] = jnp.zeros_like(ta)
+        tsh[...] = jnp.zeros_like(tsh)
         ta[0, 28:36, :] = sq_ref[...]
         for t in range(4):
             for w in range(NW):
@@ -634,12 +729,12 @@
                 if k + i > 0:
                     out_copy(k, i).start()
 
-    def packed(b, i, late):
+    def packed(b, j, late):
         size = ATT_ROWS if late else MLP_ROWS
-        base = pl.multiple_of((1 - b) * (MLP_ROWS + ATT_ROWS) + (MLP_ROWS if late else 0), ROWS)
-        slot = i % 2
+        base = pl.multiple_of((1 - b) * BLOCK_ROWS + (MLP_ROWS if late else 0), 512)
+        slot = j % 2
         return pltpu.make_async_copy(
-            gbuf.at[slot, pl.ds(0, size)], pack.at[tp ^ i, pl.ds(base, size)], gsem.at[slot]
+            gbuf.at[slot, pl.ds(0, size)], pack.at[tp ^ j ^ 2, pl.ds(base, size)], gsem.at[slot]
         )
 
     def moves():
@@ -660,9 +755,10 @@
     @pl.when((phase == 0) | (phase == 2))
     def _():
         b = 1 - phase // 2
-        i = step % 4
-
-        @pl.when(i == 0)
+        j = step % 4
+        i = j ^ 2
+
+        @pl.when(j == 0)
         def _():
             @pl.when(b == 0)
             def _():
@@ -675,51 +771,52 @@
             gh[...], gl[...] = split(gf[...])
             acc[...] = jnp.zeros_like(acc)
 
-        slot = i % 2
+        slot = j % 2
         grad = (gh[...], gl[...])
         dws = mm3(split(hid_ref[0].T), grad, NN)
-        for j in range(4):
-            gbuf[slot, 2048 + j * 512 : 2560 + j * 512, :] = dws[:, j * 128 : (j + 1) * 128]
+        for q in range(4):
+            gbuf[slot, 2048 + q * 512 : 2560 + q * 512, :] = dws[:, q * 128 : (q + 1) * 128]
         dpre = mm3(grad, split(ws_ref[0, 0].reshape(512, C)), NT) * slope_ref[0]
-        ta[0, pl.ds(12 + b * 4 + (tp ^ i), 1), :] = colsum(dpre)
+        tsh[i, pl.ds(b, 1), :] = colsum(dpre)
         pair_ = split(dpre)
         dwe = mm3((nth[...], ntl[...]), pair_, NN)
-        for j in range(4):
-            gbuf[slot, j * 512 : (j + 1) * 512, :] = dwe[:, j * 128 : (j + 1) * 128]
+        for q in range(4):
+            gbuf[slot, q * 512 : (q + 1) * 512, :] = dwe[:, q * 128 : (q + 1) * 128]
         acc[...] += mm3(pair_, split(we_ref[0, 0].reshape(C, 512)), NT)
 
-        @pl.when(i > 0)
-        def _():
-            packed(b, i - 1, False).wait()
-
-        packed(b, i, False).start()
-
-        @pl.when(i == 3)
+        @pl.when(j > 0)
+        def _():
+            packed(b, j - 1, False).wait()
+
+        packed(b, j, False).start()
+
+        @pl.when(j == 3)
         def _():
             grad_x, dgain, dshift = norm_back(mid_ref[0], g2_ref[b], acc[...])
-            ta[0, pl.ds(6 + 3 * b, 1), :] = dgain
-            ta[0, pl.ds(7 + 3 * b, 1), :] = dshift
-            ta[0, pl.ds(8 + 3 * b, 1), :] = colsum(gf[...])
+            ta[0, pl.ds(22 + 3 * b, 1), :] = dgain
+            ta[0, pl.ds(23 + 3 * b, 1), :] = dshift
+            ta[0, pl.ds(24 + 3 * b, 1), :] = colsum(gf[...])
             gf[...] = gf[...] + grad_x
             packed(b, 3, False).wait()
 
     @pl.when((phase == 1) | (phase == 3))
     def _():
         b = 1 - phase // 2
-        i = step % 4
-
-        @pl.when(i == 0)
+        j = step % 4
+        i = j ^ 2
+
+        @pl.when(j == 0)
         def _():
             xhat, _ = normalized(field_ref[0])
             nth[...], ntl[...] = split((xhat * g1_ref[b] + b1_ref[b]).T)
             gh[...], gl[...] = split(gf[...])
             acc[...] = jnp.zeros_like(acc)
 
-        slot = i % 2
+        slot = j % 2
         grad = (gh[...], gl[...])
         dwo = mm3(split(att_ref[0].T), grad, NN)
-        for j in range(4):
-            gbuf[slot, 1536 + j * 128 : 1664 + j * 128, :] = dwo[:, j * 128 : (j + 1) * 128]
+        for q in range(4):
+            gbuf[slot, 1536 + q * 128 : 1664 + q * 128, :] = dwo[:, q * 128 : (q + 1) * 128]
         dout = mm3(grad, split(wo_ref[0, 0, 0]), NT)
         masks = head_masks(bf16)
         dbias = jnp.zeros((GROUP * WT, WT), f32)
@@ -738,28 +835,30 @@
             dqkv[pl.ds(w * WT, WT), 0:128] = mm3(side_by_side(dpair), k4, NN) * HD ** (-0.5)
             dqkv[pl.ds(w * WT, WT), 128:256] = mm3(dpair, q4, TN)
             dqkv[pl.ds(w * WT, WT), 256:384] = mm3(split(p), do4, TN)
-        gbuf[slot, 2048:2560, :] = dbias
+        line = table_line(dbias, pick_ref[...], pile_ref[...])
+        for q in range(3):
+            tsh[i, pl.ds(4 + 3 * b + q, 1), :] = line[:, q * 512 : (q + 1) * 512]
         grads = dqkv[...]
-        ta[0, pl.ds(20 + b * 4 + (tp ^ i), 1), 0:384] = colsum(grads)
+        tsh[i, pl.ds(2 + b, 1), 0:384] = colsum(grads)
         pair_ = split(grads)
         dw = mm3((nth[...], ntl[...]), pair_, NN)
-        for j in range(3):
-            gbuf[slot, j * 512 : (j + 1) * 512, :] = dw[:, j * 128 : (j + 1) * 128]
-        w = jnp.concatenate([wqkv_ref[0, 0, j] for j in range(3)], axis=1)
+        for q in range(3):
+            gbuf[slot, q * 512 : (q + 1) * 512, :] = dw[:, q * 128 : (q + 1) * 128]
+        w = jnp.concatenate([wqkv_ref[0, 0, q] for q in range(3)], axis=1)
         acc[...] += mm3(pair_, split(w), NT)
 
-        @pl.when(i > 0)
-        def _():
-            packed(b, i - 1, True).wait()
-
-        packed(b, i, True).start()
-
-        @pl.when(i == 3)
+        @pl.when(j > 0)
+        def _():
+            packed(b, j - 1, True).wait()
+
+        packed(b, j, True).start()
+
+        @pl.when(j == 3)
         def _():
             grad_x, dgain, dshift = norm_back(field_ref[0], g1_ref[b], acc[...])
-            ta[0, pl.ds(3 * b, 1), :] = dgain
-            ta[0, pl.ds(1 + 3 * b, 1), :] = dshift
-            ta[0, pl.ds(2 + 3 * b, 1), :] = colsum(gf[...])
+            ta[0, pl.ds(16 + 3 * b, 1), :] = dgain
+            ta[0, pl.ds(17 + 3 * b, 1), :] = dshift
+            ta[0, pl.ds(18 + 3 * b, 1), :] = colsum(gf[...])
             acc[...] = gf[...] + grad_x
 
             @pl.when(b == 1)
@@ -792,24 +891,21 @@
             for copy in ag_copies(k):
                 copy.start()
 
-    @pl.when(step == MERGE_STEP - 1)
-    def _():
+    def ag_pass():
         for copy in ag_copies(1):
             copy.wait()
         for copy in ag_copies(2):
             copy.start()
-        for copy in ag_copies(0):
-            copy.wait()
-
-    @pl.when((step >= MERGE_STEP) & (step < MERGE_STEP + 4))
-    def _():
-        i = step - MERGE_STEP
+
+    def merge(i):
         t = tp ^ i
 
-        @pl.when(i == 2)
-        def _():
-            for copy in ag_copies(2):
-                copy.wait()
+        for k in (0, 2):
+
+            @pl.when(i == (1 if k == 0 else 2))
+            def _(k=k):
+                for copy in ag_copies(k):
+                    copy.wait()
 
         fetch = [pltpu.make_async_copy(q_ref.at[t], qbuf, msem.at[0])]
         fetch[0].start()
@@ -841,9 +937,8 @@
         xhat = (qbuf[...] - mean) * inv
         gmerged = mm3(fpair, split(mw_ref[...]), NT)
         dmw[...] += mm3(split((xhat * mg_ref[0:1, :] + mg_ref[1:2, :]).T), fpair, NN)
-        row = pl.ds(36 + tp, 1)
-        ta[0, row, 0:256] += colsum(gmerged * xhat)
-        ta[0, row, 256:512] += colsum(gmerged)
+        tsh[0, 10:11, 0:256] += colsum(gmerged * xhat)
+        tsh[0, 10:11, 256:512] += colsum(gmerged)
 
         @pl.when(i > 0)
         def _():
@@ -855,16 +950,15 @@
         @pl.when(i == 3)
         def _():
             pltpu.make_async_copy(gqbuf, gq_ref.at[t], msem.at[3]).wait()
-            for k in range(2):
-                for j in range(2):
-                    low = (2 * k + j) * 128
-                    pair[FULL_CH + k, 0, j * 256 : (j + 1) * 256, :] = dmw[:, low : low + 128]
+            for k in range(4):
+                row = k * 256
+                pair[FULL_CH + row // ROWS, 0, row % ROWS : row % ROWS + 256, :] = dmw[:, k * 128 : (k + 1) * 128]
 
     def rows(c):
         return pl.ds(pl.multiple_of(c * ROWS, ROWS), ROWS)
 
     def load(c, k):
-        return pltpu.make_async_copy(pack.at[tp ^ (2 * k), rows(c)], loc.at[c % 2, k], ls.at[c % 2, k])
+        return pltpu.make_async_copy(pack.at[tp ^ (2 * k), rows(c)], loc.at[c % 4, k], ls.at[c % 4, k])
 
     def swap(c, k):
         return push(pack.at[tp ^ 1 ^ (2 * k), rows(c)], pair.at[c, k], ss.at[k, c], rs.at[k, c], sib)
@@ -896,110 +990,152 @@
     def write(c):
         return pltpu.make_async_copy(fin.at[c], out_ref.at[rows(c)], os.at[c])
 
-    def tiny(k, peer):
-        return push(ta.at[k], tx.at[k], ts.at[k], tq.at[k], peer)
+    low, high = pl.ds(0, 16), pl.ds(16, 24)
+
+    def tiny(k):
+        if k == 0:
+            todo = [(tsh.at[1], tr.at[0]), (tsh.at[3], tr.at[1]), (ta.at[0, high], tx.at[0, high])]
+        elif k == 1:
+            todo = [(tsh.at[2], tx.at[1, low]), (ta.at[1, high], tx.at[1, high])]
+        else:
+            todo = [(ta.at[2], tx.at[2])]
+        peer = (sib, across, beside)[k]
+        return [push(a, b, tss.at[k, i], tsq.at[k, i], peer) for i, (a, b) in enumerate(todo)]
+
+    def tiny_sum(k):
+        if k == 0:
+            ta[1, low] = tsh[0] + tr[0]
+            ta[1, high] = ta[0, high] + tx[0, high]
+            tsh[2] = tsh[2] + tr[1]
+        else:
+            ta[k + 1] = ta[k] + tx[k]
 
     def tiny_z(q, slot):
         return push(ta.at[3], tz.at[slot], tzs.at[q], tzq.at[slot], device(q))
 
-    def stage(lag, first, last):
-        c = step - FIRST - lag
-        return c, (c >= first) & (c < last)
-
-    peers = (sib, across, beside)
-    for k in range(4):
-
-        @pl.when(step == TINY_STEP + 2 * k)
-        def _(k=k):
-            if k > 0:
-                tiny(k - 1, peers[k - 1]).wait()
-                ta[k] = ta[k - 1] + tx[k - 1]
-            if k < 3:
-                tiny(k, peers[k]).start()
-            else:
-                tz[mine] = ta[3]
-
-                @pl.loop(1, m)
-                def _(j):
-                    tiny_z(member(j), mine).start()
-
-    c0, on0 = stage(0, 0, FULL_CH)
-
-    @pl.when(on0)
-    def _():
-        for k in (1, 0):
-            swap(c0, k).start()
-            load(c0, k).start()
-
-    c1, on1 = stage(1, 0, FULL_CH)
-
-    @pl.when(on1)
-    def _():
-        for k in (1, 0):
-            load(c1, k).wait()
-            swap(c1, k).wait_recv()
-            pair[c1, k] = pair[c1, k] + loc[c1 % 2, k]
-            if k == 1:
-                cross(c1).start()
-
-    c2, on2 = stage(2, 0, CHUNKS)
-
-    @pl.when(on2)
-    def _():
-        @pl.when(c2 < FULL_CH)
-        def _():
-            cross(c2).wait_recv()
-            pair[c2, 0] = pair[c2, 0] + fin[c2]
-
-        side(c2).start()
-
-    c3, on3 = stage(3, 0, CHUNKS)
-
-    @pl.when(on3)
-    def _():
-        side(c3).wait_recv()
-        yr[c3] = yr[c3] + pair[c3, 0, halves(par)]
-
-        @pl.loop(1, m)
-        def _(j):
-            spread(c3, member(j), mine).start()
-
-    c4, on4 = stage(4, 0, CHUNKS)
-
-    @pl.when(on4)
-    def _():
-        fin[c4, place(mine)] = yr[c4, bit(mine)]
-
-        @pl.loop(1, m)
-        def _(j):
-            spread(c4, member(j), member(j)).wait_recv()
-            fin[c4, place(mine)] = fin[c4, place(mine)] + zr[c4, member(j)]
-
-        @pl.loop(1, m)
-        def _(j):
-            share(c4, member(j), mine).start()
-
-    c5, on5 = stage(5, 0, CHUNKS)
-
-    @pl.when(on5)
-    def _():
-        @pl.loop(1, m)
-        def _(j):
-            share(c5, member(j), member(j)).wait_recv()
-            spread(c5, member(j), mine).wait_send()
-
-        back(c5).start()
-
-    c6, on6 = stage(6, 0, CHUNKS)
-
-    @pl.when(on6)
-    def _():
-        back(c6).wait_recv()
-        write(c6).start()
-
-        @pl.loop(1, m)
-        def _(j):
-            share(c6, member(j), mine).wait_send()
+    late = RATE * (16 - FIRST)
+    tiny_turn = late + 10
+
+    def begun(s):
+        return jnp.where(s < FIRST, 0, jnp.where(s < STEPS, RATE * (s - FIRST), CHUNKS + 18))
+
+    def turn(p):
+        @pl.when(p == late + 5)
+        def _():
+            ag_pass()
+
+        due = p - late
+
+        @pl.when((due >= 0) & (due < 12) & (due % 3 == 0))
+        def _():
+            merge(due // 3)
+
+        def stage(lag, end):
+            c = p - lag
+            return c, (c >= 0) & (c < end)
+
+        for k in range(4):
+
+            @pl.when(p == tiny_turn + 4 * k)
+            def _(k=k):
+                if k > 0:
+                    for copy in tiny(k - 1):
+                        copy.wait()
+                    tiny_sum(k - 1)
+                if k < 3:
+                    for copy in tiny(k):
+                        copy.start()
+                else:
+                    tz[mine] = ta[3]
+
+                    @pl.loop(1, m)
+                    def _(j):
+                        tiny_z(member(j), mine).start()
+
+        c0, on0 = stage(0, FULL_CH)
+
+        @pl.when(on0)
+        def _():
+            swap(c0, 1).start()
+            load(c0, 1).start()
+
+        c1, on1 = stage(2, FULL_CH)
+
+        @pl.when(on1)
+        def _():
+            load(c1, 1).wait()
+            swap(c1, 1).wait_recv()
+            pair[c1, 1] = pair[c1, 1] + loc[c1 % 4, 1]
+            cross(c1).start()
+
+        c2, on2 = stage(3, FULL_CH)
+
+        @pl.when(on2)
+        def _():
+            swap(c2, 0).start()
+            load(c2, 0).start()
+
+        c3, on3 = stage(6, CHUNKS)
+
+        @pl.when(on3)
+        def _():
+            @pl.when(c3 < FULL_CH)
+            def _():
+                load(c3, 0).wait()
+                swap(c3, 0).wait_recv()
+                cross(c3).wait_recv()
+                pair[c3, 0] = (pair[c3, 0] + loc[c3 % 4, 0]) + fin[c3]
+
+            side(c3).start()
+
+        c4, on4 = stage(9, CHUNKS)
+
+        @pl.when(on4)
+        def _():
+            side(c4).wait_recv()
+            yr[c4] = yr[c4] + pair[c4, 0, halves(par)]
+
+            @pl.loop(1, m)
+            def _(j):
+                spread(c4, member(j), mine).start()
+
+        c5, on5 = stage(12, CHUNKS)
+
+        @pl.when(on5)
+        def _():
+            fin[c5, place(mine)] = yr[c5, bit(mine)]
+
+            @pl.loop(1, m)
+            def _(j):
+                spread(c5, member(j), member(j)).wait_recv()
+                fin[c5, place(mine)] = fin[c5, place(mine)] + zr[c5, member(j)]
+
+            @pl.loop(1, m)
+            def _(j):
+                share(c5, member(j), mine).start()
+                spread(c5, member(j), mine).wait_send()
+
+        c6, on6 = stage(15, CHUNKS)
+
+        @pl.when(on6)
+        def _():
+            @pl.loop(1, m)
+            def _(j):
+                share(c6, member(j), member(j)).wait_recv()
+                share(c6, member(j), mine).wait_send()
+
+            back(c6).start()
+
+        c7, on7 = stage(18, CHUNKS)
+
+        @pl.when(on7)
+        def _():
+            back(c7).wait_recv()
+            write(c7).start()
+
+    @pl.loop(begun(step), begun(step + 1))
+    def _(p):
+        turn(p)
 
     @pl.when(step == STEPS - 1)
     def _():
@@ -1034,16 +1170,19 @@
 
 def backward(n, args, ident):
     m = n // 2
+    ROWS, FULL_CH, CHUNKS, _ = chunk_plan(n)
+    HALF = ROWS // 2
     dma = pltpu.SemaphoreType.DMA
 
     def fixed(shape):
         return pl.BlockSpec(shape, lambda s: (0,) * len(shape), pipeline_mode=pl.Buffered(1))
 
     def mlp_at(s):
-        return jnp.where(s < 4, 4 + s, jnp.where(s < 8, 0, jnp.where(s < 12, s - 8, 3)))
+        return jnp.where(s < 4, 4 + (s ^ 2), jnp.where(s < 8, 2, jnp.where(s < 12, (s - 8) ^ 2, 1)))
 
     def att_at(s):
-        return jnp.where(s < 4, 4, jnp.where(s < 8, s, jnp.where(s < 12, 0, jnp.where(s < 16, s - 12, 3))))
+        return jnp.where(s < 4, 6, jnp.where(s < 8, 4 + ((s - 4) ^ 2), jnp.where(
+            s < 12, 2, jnp.where(s < 16, (s - 12) ^ 2, 1))))
 
     def by(index, shape, mode=None):
         zeros = (0,) * len(shape)
@@ -1063,6 +1202,7 @@
         by(mlp_at, (TOK, 512)), by(mlp_at, (TOK, 512)), by(att_at, (TOK, 384)),
         by(att_at, (NW, GROUP * WT, WT)), by(att_at, (TOK, 128)),
         fixed((8, C)), ANY, fixed((256, C)), fixed((8, C)), fixed((8, 256)), fixed((TOK, 128)), ANY,
+        fixed((WT, 384)), fixed((160, WT)),
     ]
     return pl.pallas_call(
         functools.partial(bwd_kernel, n),
@@ -1078,14 +1218,14 @@
             pltpu.VMEM((TOK, C), bf16), pltpu.VMEM((TOK, C), f32), pltpu.VMEM((TOK, 384), f32),
             pltpu.VMEM((TOK, C), f32), pltpu.VMEM((2, MLP_ROWS, 128), f32), pltpu.VMEM((TOK, C), f32),
             pltpu.VMEM((8, TOK), f32), pltpu.VMEM((8, TOK), f32), pltpu.VMEM((TOK, 256), f32),
-            pltpu.VMEM((2, 2, ROWS, 128), f32), pltpu.VMEM((CHUNKS, 2, ROWS, 128), f32),
+            pltpu.VMEM((4, 2, ROWS, 128), f32), pltpu.VMEM((CHUNKS, 2, ROWS, 128), f32),
             pltpu.VMEM((CHUNKS, HALF, 128), f32), pltpu.VMEM((CHUNKS, m, HALF // m, 128), f32),
             pltpu.VMEM(lanes, f32), pltpu.VMEM((4, TINY, C), f32), pltpu.VMEM((3, TINY, C), f32),
-            pltpu.VMEM((m, TINY, C), f32),
+            pltpu.VMEM((m, TINY, C), f32), pltpu.VMEM((4, 16, C), f32), pltpu.VMEM((2, 16, C), f32),
             dma((2,)), dma((7,)), dma((7,)), dma((2, 3)), dma((2, 3)), dma((2,)), dma((4,)),
             dma((5, CHUNKS)), dma((5, CHUNKS)), dma((4, m)), dma((CHUNKS, m)), dma((4, m)),
-            dma((CHUNKS, m)), dma((2, 2)), dma((CHUNKS,)), dma((3,)), dma((3,)), dma((m,)), dma((m,)),
-            dma((2, 4)), dma((2, 4)), dma((1,)),
+            dma((CHUNKS, m)), dma((4, 2)), dma((CHUNKS,)), dma((m,)), dma((m,)),
+            dma((2, 4)), dma((2, 4)), dma((1,)), dma((3, 3)), dma((3, 3)),
         ],
         compiler_params=pltpu.CompilerParams(
             collective_id=ident, has_side_effects=True, vmem_limit_bytes=60 << 20,
@@ -1120,15 +1260,6 @@
     rows = rows.reshape(heads, 2, 5, 2, 5, WT).transpose(0, 3, 1, 4, 2, 5)
     rows = rows.reshape(heads, 4, REAL, WT)
     return jnp.pad(rows, ((0, 0), (0, 0), (0, SUB - REAL), (0, 0))).reshape(heads, WT, WT)
-
-
-def table_of(dbias):
-    heads = dbias.shape[0]
-    rows = dbias.reshape(heads, 4, SUB, WT)[:, :, :REAL].reshape(heads, 2, 2, 5, 5, WT)
-    rows = rows.transpose(0, 2, 4, 1, 3, 5).reshape(heads * WIN, WIN * WT)
-    columns = lax.dot_general(rows, jnp.asarray(row_pick()), NT, precision="highest")
-    columns = columns.reshape(heads, WIN, 19, WIN)
-    return jnp.einsum("harb,dab->hrd", columns, jnp.asarray(column_pick()), precision="highest")
 
 
 def shards(
@@ -1190,6 +1321,7 @@
             cot.reshape(4, 2, 192, 128), middles, fields, three(first_gain), three(first_shift),
             three(second_gain), three(second_shift), wall, wall, nall, wall, hid, slope, qkv, p, att,
             squares, quads, weight, vecs, mgain, stat, out.reshape(4, 2, 6, SUB, 128),
+            *table_picks(),
         ),
         2,
     )
@@ -1197,25 +1329,19 @@
     output = output.transpose(0, 2, 1, 3, 4).reshape(10, 120, 128)
     gquads = gquads.reshape(4, NW, 4, SUB, 256)[:, :, :, :REAL].reshape(4, NW, 2, 2, 5, 5, 2, 128)
     patches_grad = gquads.transpose(2, 4, 6, 0, 1, 3, 5, 7).reshape(20, 240, 64)
-    small1, small2 = tiny[0:6].reshape(2, 3, C), tiny[6:12].reshape(2, 3, C)
-    dbe, dbqkv = tiny[12:20].reshape(2, 4, 512), tiny[20:28, :384].reshape(2, 4, 384)
+    small1, small2 = tiny[16:22].reshape(2, 3, C), tiny[22:28].reshape(2, 3, C)
     sums = jnp.sum(tiny[28:34], axis=1)
     sums, count = sums[:5], sums[5]
-    dmgs = lax.dynamic_index_in_dim(tiny[36:40], tp, 0, keepdims=False)
-    dmg, dms = dmgs[:256], dmgs[256:]
-    blocks = packed.reshape(CHUNKS, ROWS, 128)
-    cut = lambda lo, hi: jnp.stack([blocks[13 + lo : 13 + hi], blocks[lo:hi]])
+    g_be, dbqkv, dmg, dms = tiny[0:2], tiny[2:4, :384].reshape(2, 3, 128), tiny[10, :256], tiny[10, 256:]
+    g_bias = jnp.stack([dbqkv[:, 0], dbqkv[:, 2]], axis=1)
+    g_tab = tiny[4:10].reshape(2, 4, 384)[:, :, :361].transpose(0, 2, 1)
+    blocks = packed.reshape(26, 512, 128)
+    cut = lambda lo, hi: jnp.stack([blocks[12 + lo : 12 + hi], blocks[lo:hi]])
     lanes = lambda x: x.transpose(0, 2, 1, 3).reshape(2, x.shape[2], C)
     g_we, g_ws = lanes(cut(0, 4)), lanes(cut(4, 8))
     g_qkv = cut(8, 11).transpose(0, 2, 1, 3)
     g_wo = lanes(cut(11, 12).reshape(2, 4, 128, 128))
-    dbias = cut(12, 13).reshape(8, WT, WT)
-    g_tab = table_of(dbias).reshape(2, 4, 361).transpose(0, 2, 1)
-    dmw = blocks[26:28].reshape(4, 256, 128).transpose(1, 0, 2).reshape(256, C)
-    own4 = lambda x, axis: lax.dynamic_index_in_dim(x, tp, axis, keepdims=False)
-    dbqkv = own4(dbqkv, 1).reshape(2, 3, 128)
-    g_bias = jnp.stack([dbqkv[:, 0], dbqkv[:, 2]], axis=1)
-    g_be = own4(dbe, 1).reshape(2, 512)
+    dmw = blocks[24:26].reshape(4, 256, 128).transpose(1, 0, 2).reshape(256, C)
     back = lambda x: x.reshape((2, 2, 64) + x.shape[1:]).swapaxes(0, 1).reshape((4, 64) + x.shape[1:])
     rms = jnp.sqrt(sums / (count * C))
     return (

time: 483 us -> 427 us (0.88)
  Pallas kernels: 416 us -> 360 us
  matrix products: 6.48 us -> 1.38 us
  local copies, waits for them, and re-layouts: 46.2 us -> 51.1 us
    pallas_call x1, Pallas kernels: 264 us -> 234 us  [backward(): pl.pallas_call(functools.partial(bwd_kernel, n), grid=(STEPS,), in_specs=...]
    pallas_call x1, Pallas kernels: 151 us -> 126 us  [forward(): pl.pallas_call(functools.partial(fwd_kernel, n), grid=(F_STEPS,), in_spec...]
    dot_general x2 -> x0, matrix products: 5.1 us -> none  [the longest x1 3.92 us: table_of(): lax.dot_general(rows, jnp.asarray(row_pick()), NT, precision='highest')]
    unnamed x49 -> x20, local copies, waits for them, and re-layouts: 10.4 us -> 9.79 us
where the time goes in v4:
time: 427 us; the launch traced here: 426 us
  Pallas kernels  360 us (84%)
  local copies, waits for them, and re-layouts  51.1 us (12%)
  other arithmetic  11.3 us (3%)
    pallas_call x1, Pallas kernels, backward(): pl.pallas_call(functools.partial(bwd_kernel, n), grid=(STEPS,), in_specs=...  234 us
    pallas_call x1, Pallas kernels, forward(): pl.pallas_call(functools.partial(fwd_kernel, n), grid=(F_STEPS,), in_spec...  126 us
    unnamed x20, local copies, waits for them, and re-layouts  9.79 us

profile of v4, /device:TPU:0, one launch (start us, length us, event | category | flops | bytes accessed | tf_op | source)
XLA Modules:
  0.0 425.7 jit_solution(2739916035766854700)
XLA Ops:
  0.7 0.7 slice.151
  1.7 0.7 copy.156
  2.4 0.7 copy.155
  3.2 1.3 reshape.268.refs_9_.refs_3_
  4.5 1.3 reshape.269.refs_10_.refs_4_
  5.8 1.3 reshape.271.refs_12_.refs_5_
  7.0 1.3 reshape.272.refs_13_.refs_6_
  8.3 0.7 pad_bitcast_fusion
  9.0 1.3 reshape.270.refs_11_
  10.3 1.3 reshape.273.refs_14_
  11.6 0.7 maximum_maximum_fusion.1.refs_2_.refs_20_
  12.2 0.7 pad_add_fusion
  12.9 0.8 fusion.5
  14.1 0.6 pad.36.refs_16_
  14.7 0.7 convert_element_type.25
  15.4 1.4 maximum_maximum_fusion.refs_8_
  16.8 0.8 reshape.298
  18.3 0.7 select_maximum_fusion.refs_17_
  19.4 0.7 pad.78.refs_19_
  20.3 0.6 pad.77.refs_18_
  20.9 1.0 reshape.303.refs_15_
  21.9 2.0 copy.95
  23.8 0.7 convolution_bitcast_fusion
  24.5 0.6 copy.98
  25.4 0.7 convolution_bitcast_fusion.1
  26.3 0.8 pad.35.clone
  27.7 0.9 pad.41.refs_20_
  28.6 1.9 copy.92
  30.5 1.5 reshape.254
  32.0 2.5 copy.134
  34.5 1.0 reshape.304
  35.5 1.3 pad.34.clone
  36.8 126.5 %forward.1 = (f32[4,2,4,512,128]{4,3,2,1,0:T(8,128)}, f32[4,2,9,128,512]{4,3,2,1,0:T(8,128)}, f32[4,2,6,32,128]{4,3,2,1,0:T(8,128)}, f32[2,384,512]{2,1,0:T(8,12...) custom-call(f32[4,384,256]{2,1,0:T(8,128)} %bitcast.115, ...), custom_call_target="tpu_custom_call" | custom-call | tf_op jit(solution)/shard_map/forward/pallas_call | solution.py:600
  163.3 233.7 %backward.1 = (f32[4,12288,128]{2,1,0:T(8,128)}, f32[4,384,512]{2,1,0:T(8,128)}, f32[4,8,384]{2,1,0:T(8,128)}, f32[2,24,32,128]{3,2,1,0:T(8,128)}, f32[13312,128...) custom-call(f32[4,2,192,128]{3,2,1,0:T(8,128)} %bitcast.140, f32[2,384,512]{2,1,0:T(8,128)} %get-tuple-element.38.refs_1_, ...), custom_call_target="tpu_custom_call" | custom-call | tf_op jit(solution)/shard_map/backward/pallas_call | solution.py:1207
  397.1 2.1 reshape.305
  404.2 0.6 slice_bitcast_fusion
  406.7 0.9 reshape.282
  407.7 1.1 slice.168
  409.3 0.8 copy.117
  410.1 1.1 fusion.7
  411.2 0.9 copy_bitcast_fusion.2
  412.1 1.5 copy.113
  413.6 2.5 reshape.285
  416.0 1.8 copy.121
  417.9 1.5 fusion.8
  419.3 2.5 fusion.6
  421.8 1.3 maximum_bitcast_fusion.2
  423.1 2.6 copy_bitcast_fusion
  (79 shorter events, 9.9 us)
Async XLA Ops:
  0.7 23.2 %copy-start.3 = (f32[19,10,10,1]{0,2,3,1:T(8,128)S(1)}, f32[19,10,10,1]{0,2,3,1:T(8,128)}, u32[]{:S(2)}) copy-start(f32[19,10,10,1]{0,2,3,1:T(8,128)} %constant.83) | copy-start | bytes 22804
  21.9 3.5 copy-start
  25.4 1.7 copy-start.2
  397.0 2.1 copy-start.4
  397.0 9.0 %copy-start.1 = (f32[2,24,32,128]{3,2,1,0:T(8,128)S(1)}, f32[2,24,32,128]{3,2,1,0:T(8,128)}, u32[]{:S(2)}) copy-start(f32[2,24,32,128]{3,2,1,0:T(8,128)} %get-tuple-element.51) | copy-start | bytes 2359300

commit v5 on v4

--- a/solution.py
+++ b/solution.py
@@ -131,7 +131,8 @@
 F_STEPS = 19
 
 
-GATHERED = (0, 0, 0, 3, 9, 10, 11, 13, 17, 18, 19, 20, 22, 24, 26, 28, 30, 30, 30, 30)
+TURNS = (0, 0, 0, 5, 11, 13, 15, 18, 21, 23, 25, 27, 28, 29, 30, 30, 30, 30, 30, 30)
+LAG = 2
 AHEAD = 6
 
 
@@ -141,28 +142,28 @@
     return att, mlp
 
 
-def gathered(s):
-    found = jnp.int32(GATHERED[0])
-    for k in range(1, len(GATHERED)):
-        if GATHERED[k] != GATHERED[k - 1]:
-            found = jnp.where(s >= k, GATHERED[k], found)
+def so_far(table, s):
+    found = jnp.int32(table[0])
+    for k in range(1, len(table)):
+        if table[k] != table[k - 1]:
+            found = jnp.where(s >= k, table[k], found)
     return found
 
 
 def fwd_kernel(n, *refs):
     (
         q_ref, mw_ref, mg_ref, wi_ref, bi_ref, wo_ref, we_ref, ws_ref, sm_ref, g1_ref, b1_ref, bo_ref,
-        g2_ref, b2_ref, bs_ref, regc_ref, regr_ref, v0_ref, v1_ref, vs_ref, cot_ref,
-    ) = refs[:21]
+        g2_ref, b2_ref, bs_ref, page_ref, grid_ref, cot_ref,
+    ) = refs[:18]
     (
         nall, wall, cb, field_out, mid_out, qkv_ref, p_ref, att_ref, hid_ref, slope_ref, stat_ref, vec_ref,
         sq_ref, os_ref,
-    ) = refs[21:35]
+    ) = refs[18:32]
     (
-        nb, wb, smb, pb, pr, px, stb, str_, stx, vp, vr, vc, field, nh, nl, mixed, moved,
+        nb, wb, smb, pb, pr, px, stb, str_, stx, vp, v0_ref, v1_ref, vs_ref, vr, vc, regr_ref, regc_ref, field, nh, nl, mixed, moved,
         lsem, ss, sr, xs, xr, ys, yr, zs, zr, s2s, s2r, sms, smr, rss, rsr, vps, vpr, vvs, vvr,
         mvs, mvr, cbs, cbr, cbl, hn, hw,
-    ) = refs[35:]
+    ) = refs[32:]
     step = pl.program_id(0)
     sp, tp, sib, across, beside = here()
     par = sp & 1
@@ -298,24 +299,55 @@
         vp[0] = jnp.dot(pick, mw_ref[...], precision=lax.Precision.HIGHEST, preferred_element_type=f32)
         for copy in vec_copies():
             copy.start()
+        lane1 = lax.broadcasted_iota(jnp.int32, (1, 128), 1) // SUB
+        for buf in (v0_ref, v1_ref, vs_ref, regr_ref):
+            buf[...] = jnp.zeros_like(buf)
+        for w in range(NW):
+            here_, next_, sent, region = [jnp.zeros((1, 128), f32) for _ in range(4)]
+            for k in range(4):
+                sr, sc = k // 2, k % 2
+                column = 6 * tp + 2 * w + sc
+                after = lax.rem(column + 1, 24)
+                bring = lambda r, c: pltpu.roll(grid_ref[r, pl.ds(c, 1), :], SUB * k, 1)
+                here_ = here_ + bring(sr, column)
+                if sr == 0:
+                    next_ = next_ + bring(1, after)
+                else:
+                    sent = sent + bring(0, after)
+                page = page_ref[lax.rem(sp + sr, n), lax.rem(3 * tp + w + sc, 12)] * 4
+                if sr == 1:
+                    page = page + 2 * (sp == n - 1).astype(jnp.int32)
+                if sc == 1 and w == NW - 1:
+                    page = page + (tp == 3).astype(jnp.int32)
+                region = region + jnp.where(lane1 == k, page, 0).astype(f32)
+            v0_ref[w : w + 1, :] = here_
+            v1_ref[w : w + 1, :] = next_
+            vs_ref[w : w + 1, :] = sent
+            regr_ref[1, w : w + 1, :] = region
         valid_copy().start()
         lane = lax.broadcasted_iota(jnp.int32, (TOK, 128), 1)
-        for i in (3, 1, 2, 0):
+
+        def project(i):
             quad = q_ref[tp ^ i]
             pb[i] = mm3(split(quad * gain), wpair, NN)
             s1 = jnp.sum(quad, axis=-1, keepdims=True)
             s2 = jnp.sum(quad * quad, axis=-1, keepdims=True)
             stb[i] = jnp.where(lane == 0, s1, jnp.where(lane == 1, s2, 0.0)).T[0:8, :]
-            if i % 2 == 1:
-                for copy in rs_copies((i - 1) // 2):
-                    copy.start()
-            if i == 1:
-                for copy in own():
-                    copy.wait()
-                sm_copy(0).start()
-                sm_copy(1).start()
-                for c in (0, 1):
-                    x_copy(c, nb, c, 512, c % 3 != 0).start()
+
+        project(3)
+        for copy in rs_copies(1):
+            copy.start()
+        project(1)
+        for copy in rs_copies(0):
+            copy.start()
+        for copy in own():
+            copy.wait()
+        sm_copy(0).start()
+        sm_copy(1).start()
+        for c in range(2):
+            x_copy(c, nb, c, 512, c % 3 != 0).start()
+        project(2)
+        project(0)
         for copy in rs_copies(1):
             copy.wait_recv()
         pb[2] = pb[2] + pr[1]
@@ -324,12 +356,9 @@
             copy.start()
         for copy in to_sib(0):
             copy.start()
-        for copy in rs_copies(0):
-            copy.wait_recv()
-        pb[0] = pb[0] + pr[0]
-        stb[0] = stb[0] + str_[0]
         for c in range(2, AHEAD):
-            x_copy(c, nb if c < 4 else wb, c if c < 4 else (8 if c == 4 else c - 5), 512 if c < 4 else 128, c % 3 != 0).start()
+            buf, k, size = (nb, c, 512) if c < 4 else (wb, 8 if c == 4 else c - 5, 128)
+            x_copy(c, buf, k, size, c % 3 != 0).start()
         sq_ref[...] = jnp.zeros_like(sq_ref)
         os_ref[...] = jnp.zeros_like(os_ref)
         vec_ref[...] = jnp.zeros_like(vec_ref)
@@ -348,7 +377,13 @@
             vc[b] = jnp.concatenate([tall[:, w : w + 1] for w in range(NW)], axis=0)
             if b == 1:
                 vr[...] = line
+            tall = jnp.concatenate([regr_ref[b], jnp.zeros((120, 128), f32)], axis=0).T
+            regc_ref[b] = jnp.concatenate([tall[:, w : w + 1] for w in range(NW)], axis=0)
         sq_ref[5:6, 0:128] = colsum(v0_ref[...])
+        for copy in rs_copies(0):
+            copy.wait_recv()
+        pb[0] = pb[0] + pr[0]
+        stb[0] = stb[0] + str_[0]
         for k in range(2):
             for copy in rs_copies(k):
                 copy.wait_send()
@@ -377,8 +412,8 @@
 
             field_out[0] = field[...]
             xhat, _ = normalized(field[...])
-            nh[...], nl[...] = split(xhat * g1_ref[b] + b1_ref[b])
-            mixed[...] = jnp.broadcast_to(bo_ref[b], mixed.shape)
+            nh[...], nl[...] = split(xhat * g1_ref[pl.ds(b, 1), :] + b1_ref[pl.ds(b, 1), :])
+            mixed[...] = jnp.broadcast_to(bo_ref[pl.ds(b, 1), :], mixed.shape)
 
         for k in range(2):
 
@@ -435,8 +470,8 @@
         @pl.when(i == 0)
         def _():
             xhat, _ = normalized(mid_out[0])
-            nh[...], nl[...] = split(xhat * g2_ref[b] + b2_ref[b])
-            mixed[...] = jnp.broadcast_to(bs_ref[b], mixed.shape)
+            nh[...], nl[...] = split(xhat * g2_ref[pl.ds(b, 1), :] + b2_ref[pl.ds(b, 1), :])
+            mixed[...] = jnp.broadcast_to(bs_ref[pl.ds(b, 1), :], mixed.shape)
 
             @pl.when(b == 0)
             def _():
@@ -506,7 +541,7 @@
 
         each(c, run)
 
-    @pl.loop(gathered(step), gathered(step + 1))
+    @pl.loop(so_far(TURNS, step), so_far(TURNS, step + 1))
     def _(p):
         @pl.when(p + AHEAD < GCH)
         def _():
@@ -526,33 +561,39 @@
 
             both(p, act)
 
-        @pl.when((p >= 2) & (p - 2 < GCH))
+        y = p - LAG
+
+        @pl.when((y >= 0) & (y < GCH))
         def _():
             def act(buf, k, size, low):
-                y_copy(p - 2, buf, k, size, low).wait_recv()
+                y_copy(y, buf, k, size, low).wait_recv()
+                x_copy(y, buf, k, size, low).wait_send()
                 half_here = zpar if low else 1 - par
                 if low:
-                    z_copy(p - 2, buf, k, size).start()
+                    z_copy(y, buf, k, size).start()
                 for h in range(2):
 
                     @pl.when(half_here == h)
                     def _(h=h):
-                        s_copy(h, p - 2, buf, k, size).start()
-
-            both(p - 2, act)
-
-        @pl.when((p >= 4) & (p - 4 < GCH))
+                        s_copy(h, y, buf, k, size).start()
+
+            both(y, act)
+
+        z = p - 2 * LAG
+
+        @pl.when((z >= 0) & (z < GCH))
         def _():
             def act(buf, k, size, low):
+                y_copy(z, buf, k, size, low).wait_send()
                 if low:
-                    z_copy(p - 4, buf, k, size).wait_recv()
+                    z_copy(z, buf, k, size).wait_recv()
                     for h in range(2):
 
                         @pl.when(1 - zpar == h)
                         def _(h=h):
-                            s_copy(h, p - 4, buf, k, size).start()
-
-            both(p - 4, act)
+                            s_copy(h, z, buf, k, size).start()
+
+            both(z, act)
 
     @pl.when(step == F_STEPS - 1)
     def _():
@@ -572,8 +613,6 @@
         @pl.loop(0, GCH)
         def _(c):
             def act(buf, k, size, low):
-                x_copy(c, buf, k, size, low).wait_send()
-                y_copy(c, buf, k, size, low).wait_send()
                 if low:
                     z_copy(c, buf, k, size).wait_send()
                 for h in range(2):
@@ -596,14 +635,13 @@
     mlp_at = lambda s: fwd_order(s)[1]
     second = lambda s: jnp.where(s < 10, 0, 1)
     vm = lambda *shape: pltpu.VMEM(shape, f32)
-    two = fixed((2, 1, C))
+    two = fixed((2, C))
     return pl.pallas_call(
         functools.partial(fwd_kernel, n),
         grid=(F_STEPS,),
         in_specs=[
             fixed((4, TOK, 256)), fixed((256, C)), fixed((8, 256)), ANY, ANY, ANY, ANY, ANY, ANY,
-            two, two, two, two, two, two, fixed((2, TOK, 1)), fixed((2, 8, 128)), fixed((8, 128)),
-            fixed((8, 128)), fixed((8, 128)), ANY,
+            two, two, two, two, two, two, pl.BlockSpec(memory_space=pltpu.SMEM), fixed((2, 24, 128)), ANY,
         ],
         out_specs=[
             ANY, ANY, ANY, by(second, (TOK, C)), by(second, (TOK, C)), by(att_at, (TOK, 384)),
@@ -617,7 +655,8 @@
         ],
         scratch_shapes=[
             vm(4, 8, 512, 128), vm(4, 18, 128, 512), vm(4, 8, C), vm(4, TOK, C), vm(2, TOK, C), vm(TOK, C),
-            vm(4, 8, TOK), vm(2, 8, TOK), vm(8, TOK), vm(4, 8, C), vm(8, 128), vm(2, TOK, 1), vm(TOK, C),
+            vm(4, 8, TOK), vm(2, 8, TOK), vm(8, TOK), vm(4, 8, C), vm(8, 128), vm(8, 128), vm(8, 128), vm(8, 128), vm(2, TOK, 1), vm(2, 8, 128), vm(2, TOK, 1),
+            vm(TOK, C),
             pltpu.VMEM((TOK, C), bf16), pltpu.VMEM((TOK, C), bf16), vm(TOK, C), vm(TOK, C),
             dma((11,)), dma((2, 3)), dma((2, 3)), dma((GCH,)), dma((GCH,)), dma((GCH,)), dma((GCH,)),
             dma((GCH,)), dma((GCH,)), dma((2, GCH)), dma((2, GCH)), dma((3,)), dma((3,)), dma((2, 3)), dma((2, 3)),
@@ -767,7 +806,7 @@
                 gf[...] = moved[...]
 
             xhat, _ = normalized(mid_ref[0])
-            nth[...], ntl[...] = split((xhat * g2_ref[b] + b2_ref[b]).T)
+            nth[...], ntl[...] = split((xhat * g2_ref[pl.ds(b, 1), :] + b2_ref[pl.ds(b, 1), :]).T)
             gh[...], gl[...] = split(gf[...])
             acc[...] = jnp.zeros_like(acc)
 
@@ -792,7 +831,7 @@
 
         @pl.when(j == 3)
         def _():
-            grad_x, dgain, dshift = norm_back(mid_ref[0], g2_ref[b], acc[...])
+            grad_x, dgain, dshift = norm_back(mid_ref[0], g2_ref[pl.ds(b, 1), :], acc[...])
             ta[0, pl.ds(22 + 3 * b, 1), :] = dgain
             ta[0, pl.ds(23 + 3 * b, 1), :] = dshift
             ta[0, pl.ds(24 + 3 * b, 1), :] = colsum(gf[...])
@@ -808,7 +847,7 @@
         @pl.when(j == 0)
         def _():
             xhat, _ = normalized(field_ref[0])
-            nth[...], ntl[...] = split((xhat * g1_ref[b] + b1_ref[b]).T)
+            nth[...], ntl[...] = split((xhat * g1_ref[pl.ds(b, 1), :] + b1_ref[pl.ds(b, 1), :]).T)
             gh[...], gl[...] = split(gf[...])
             acc[...] = jnp.zeros_like(acc)
 
@@ -855,7 +894,7 @@
 
         @pl.when(j == 3)
         def _():
-            grad_x, dgain, dshift = norm_back(field_ref[0], g1_ref[b], acc[...])
+            grad_x, dgain, dshift = norm_back(field_ref[0], g1_ref[pl.ds(b, 1), :], acc[...])
             ta[0, pl.ds(16 + 3 * b, 1), :] = dgain
             ta[0, pl.ds(17 + 3 * b, 1), :] = dshift
             ta[0, pl.ds(18 + 3 * b, 1), :] = colsum(gf[...])
@@ -1017,7 +1056,7 @@
     tiny_turn = late + 10
 
     def begun(s):
-        return jnp.where(s < FIRST, 0, jnp.where(s < STEPS, RATE * (s - FIRST), CHUNKS + 18))
+        return jnp.where(s < FIRST, 0, jnp.where(s < STEPS, RATE * (s - FIRST), CHUNKS + 21))
 
     def turn(p):
         @pl.when(p == late + 5)
@@ -1085,6 +1124,7 @@
                 swap(c3, 0).wait_recv()
                 cross(c3).wait_recv()
                 pair[c3, 0] = (pair[c3, 0] + loc[c3 % 4, 0]) + fin[c3]
+                swap(c3, 1).wait_send()
 
             side(c3).start()
 
@@ -1092,6 +1132,11 @@
 
         @pl.when(on4)
         def _():
+            @pl.when(c4 < FULL_CH)
+            def _():
+                swap(c4, 0).wait_send()
+                cross(c4).wait_send()
+
             side(c4).wait_recv()
             yr[c4] = yr[c4] + pair[c4, 0, halves(par)]
 
@@ -1103,6 +1148,7 @@
 
         @pl.when(on5)
         def _():
+            side(c5).wait_send()
             fin[c5, place(mine)] = yr[c5, bit(mine)]
 
             @pl.loop(1, m)
@@ -1130,8 +1176,14 @@
 
         @pl.when(on7)
         def _():
-            back(c7).wait_recv()
+            back(c7).wait()
             write(c7).start()
+
+        c8, on8 = stage(21, CHUNKS)
+
+        @pl.when(on8)
+        def _():
+            write(c8).wait()
 
     @pl.loop(begun(step), begun(step + 1))
     def _(p):
@@ -1155,18 +1207,6 @@
             total = total + tz[q]
         tout_ref[...] = total
 
-        @pl.loop(0, CHUNKS)
-        def _(c):
-            @pl.when(c < FULL_CH)
-            def _():
-                for k in range(2):
-                    swap(c, k).wait_send()
-                cross(c).wait_send()
-
-            side(c).wait_send()
-            back(c).wait_send()
-            write(c).wait()
-
 
 def backward(n, args, ident):
     m = n // 2
@@ -1196,7 +1236,7 @@
     in_specs = [
         fixed((4, 2, 192, 128)), by(lambda s: jnp.where(s < 4, 1, 0), (TOK, C), one),
         by(lambda s: jnp.where(s < 8, 1, 0), (TOK, C), one),
-        fixed((2, 1, C)), fixed((2, 1, C)), fixed((2, 1, C)), fixed((2, 1, C)),
+        fixed((2, C)), fixed((2, C)), fixed((2, C)), fixed((2, C)),
         spot(mlp_at, (4, 128, 512), 0), spot(mlp_at, (4, 128, 512), 1), spot(att_at, (3, C, 128), 0),
         spot(att_at, (1, 128, C), 8),
         by(mlp_at, (TOK, 512)), by(mlp_at, (TOK, 512)), by(att_at, (TOK, 384)),
@@ -1235,6 +1275,72 @@
     )(*args)
 
 
+def unpack_kernel(
+    pack_ref, merge_ref, tiny_ref,
+    we_ref, ws_ref, qkv_ref, wo_ref, mw_ref, mg_ref, ms_ref, g1_ref, b1_ref, bias_ref, tab_ref, bo_ref, g2_ref,
+    b2_ref, be_ref, bs_ref, rms_ref,
+):
+    for q in range(4):
+        lanes = slice(q * 128, (q + 1) * 128)
+        we_ref[0, :, lanes] = pack_ref[q]
+        ws_ref[0, :, lanes] = pack_ref[4 + q]
+        wo_ref[0, :, lanes] = pack_ref[11, q * 128 : (q + 1) * 128, :]
+    for j in range(3):
+        qkv_ref[0, j] = pack_ref[8 + j]
+
+    @pl.when(pl.program_id(0) == 0)
+    def _():
+        for i in range(2):
+            for j in range(2):
+                k, low = 2 * j + i, (2 * i + j) * 64
+                for q in range(4):
+                    mw_ref[k, :, q * 128 : (q + 1) * 128] = merge_ref[q, low : low + 64, :]
+                mg_ref[k : k + 1, :] = tiny_ref[10:11, low : low + 64]
+                ms_ref[k : k + 1, :] = tiny_ref[10:11, 256 + low : 320 + low]
+        be_ref[...] = tiny_ref[0:2, :]
+        for b in range(2):
+            bias_ref[b, 0:1, :] = tiny_ref[2 + b : 3 + b, 0:128]
+            bias_ref[b, 1:2, :] = tiny_ref[2 + b : 3 + b, 256:384]
+            line = jnp.concatenate([tiny_ref[4 + 3 * b + q : 5 + 3 * b + q, :] for q in range(3)], axis=1)
+            for h in range(4):
+                tab_ref[b, h : h + 1, :] = line[:, h * 384 : h * 384 + 361]
+            for k, ref in enumerate((g1_ref, b1_ref, bo_ref)):
+                ref[b : b + 1, :] = tiny_ref[16 + 3 * b + k : 17 + 3 * b + k, :]
+            for k, ref in enumerate((g2_ref, b2_ref, bs_ref)):
+                ref[b : b + 1, :] = tiny_ref[22 + 3 * b + k : 23 + 3 * b + k, :]
+        sums = jnp.sum(tiny_ref[28:36, :], axis=1, keepdims=True)
+        rms_ref[...] = jnp.broadcast_to(jnp.sqrt(sums / (sums[5:6] * C)), (8, 128))
+
+
+def unpack(packed, tiny):
+    blocks = packed.reshape(-1, 512, 128)
+    merged = packed.reshape(-1, 256, 128)
+    whole = lambda *shape: pl.BlockSpec(shape, lambda b: (0,) * len(shape))
+    layer = lambda *shape: pl.BlockSpec((1,) + shape, lambda b: (b,) + (0,) * len(shape))
+    row = (2, C)
+    return pl.pallas_call(
+        unpack_kernel,
+        grid=(2,),
+        in_specs=[
+            pl.BlockSpec((12, 512, 128), lambda b: (1 - b, 0, 0)),
+            pl.BlockSpec((4, 256, 128), lambda b: (12, 0, 0)),
+            whole(TINY, C),
+        ],
+        out_specs=[
+            layer(512, 512), layer(512, 512), layer(3, 512, 128), layer(128, 512), whole(4, 64, C), whole(4, 64),
+            whole(4, 64), whole(*row), whole(*row), whole(2, 2, 128), whole(2, 4, 361), whole(*row), whole(*row),
+            whole(*row), whole(*row), whole(*row), whole(8, 128),
+        ],
+        out_shape=[
+            sds(2, 512, 512), sds(2, 512, 512), sds(2, 3, 512, 128), sds(2, 128, 512), sds(4, 64, C), sds(4, 64),
+            sds(4, 64), sds(*row), sds(*row), sds(2, 2, 128), sds(2, 4, 361), sds(*row), sds(*row), sds(*row),
+            sds(*row), sds(*row), sds(8, 128),
+        ],
+        compiler_params=pltpu.CompilerParams(vmem_limit_bytes=48 << 20),
+        name="unpack",
+    )(blocks, merged, tiny)
+
+
 def column_pick():
     pick = np.zeros((19, WIN, WIN), np.float32)
     for a in range(WIN):
@@ -1269,32 +1375,14 @@
 ):
     sp_count = lax.axis_size("sp")
     tp = lax.axis_index("tp")
-    sp = lax.axis_index("sp")
 
     tables = position_table.transpose(0, 2, 1).reshape(8, 361)
     bias = bias_of(tables).reshape(2, 512, 128)
     pairs = jnp.concatenate([input_bias, jnp.zeros_like(input_bias)], axis=2).reshape(2, 512)
     small = jnp.concatenate([expand_bias, pairs, jnp.zeros((4, 512), f32)], axis=0)
-    three = lambda x: x.reshape(2, 1, C)
 
     valid = valid_flags.astype(f32).reshape(2, 5, 24, 5).transpose(0, 2, 1, 3).reshape(2, 24, REAL)
-    valid = jnp.pad(valid, ((0, 0), (0, 0), (0, SUB - REAL)))
-    own = lambda grid: lax.dynamic_slice_in_dim(grid, 6 * tp, 6, 1).reshape(2, NW, 2 * SUB)
-    here_ = own(valid)
-    next_ = own(jnp.roll(valid, -1, axis=1))
-    blank = jnp.zeros((NW, 2 * SUB), f32)
-    line = lambda a, c: jnp.pad(jnp.concatenate([a, c], axis=1), ((0, 5), (0, 0)))
-    valid0, valid1, valids = line(here_[0], here_[1]), line(next_[1], blank), line(blank, next_[0])
-    pages = jnp.concatenate([page_map, page_map[:1]], axis=0)
-    pages = jnp.concatenate([pages, pages[:, :1]], axis=1)
-    pages = lax.dynamic_slice(pages, (sp, 3 * tp), (2, 4))
-    page = jnp.stack([pages[:, :3], pages[:, 1:]], axis=2).transpose(1, 0, 2)
-    wrap_row = (jnp.arange(2) == 1) & (sp == sp_count - 1)
-    wrap_col = (jnp.arange(2) == 1)[None, :] & (jnp.arange(NW) == NW - 1)[:, None] & (tp == 3)
-    region = page * 4 + 2 * wrap_row[None, :, None].astype(jnp.int32) + wrap_col[:, None, :].astype(jnp.int32)
-    region = jnp.broadcast_to(region[..., None], (NW, 2, 2, SUB)).reshape(NW, WT)
-    region = jnp.stack([jnp.zeros_like(region), region])
-    regc, regr = region.reshape(2, TOK, 1), jnp.pad(region, ((0, 0), (0, 5), (0, 0)))
+    valid = jnp.pad(valid, ((0, 0), (0, 0), (0, 128 - REAL)))
 
     gain = merge_gain.reshape(2, 2, 64).transpose(1, 0, 2).reshape(1, 256)
     offset = merge_shift.reshape(2, 2, 64).transpose(1, 0, 2).reshape(1, 256)
@@ -1310,16 +1398,16 @@
         (
             quads, weight, mgain, input_weight.transpose(0, 2, 1, 3), bias, output_weight.reshape(2, 1, 128, C),
             expand_weight.reshape(2, 4, 128, 512), shrink_weight.reshape(2, 4, 128, C), small,
-            three(first_gain), three(first_shift), three(output_bias), three(second_gain), three(second_shift),
-            three(shrink_bias), regc, regr, valid0, valid1, valids, cot,
+            first_gain, first_shift, output_bias, second_gain, second_shift,
+            shrink_bias, page_map, valid, cot,
         ),
         1,
     )
     _, _, _, output, packed, gquads, tiny = backward(
         sp_count,
         (
-            cot.reshape(4, 2, 192, 128), middles, fields, three(first_gain), three(first_shift),
-            three(second_gain), three(second_shift), wall, wall, nall, wall, hid, slope, qkv, p, att,
+            cot.reshape(4, 2, 192, 128), middles, fields, first_gain, first_shift,
+            second_gain, second_shift, wall, wall, nall, wall, hid, slope, qkv, p, att,
             squares, quads, weight, vecs, mgain, stat, out.reshape(4, 2, 6, SUB, 128),
             *table_picks(),
         ),
@@ -1329,24 +1417,10 @@
     output = output.transpose(0, 2, 1, 3, 4).reshape(10, 120, 128)
     gquads = gquads.reshape(4, NW, 4, SUB, 256)[:, :, :, :REAL].reshape(4, NW, 2, 2, 5, 5, 2, 128)
     patches_grad = gquads.transpose(2, 4, 6, 0, 1, 3, 5, 7).reshape(20, 240, 64)
-    small1, small2 = tiny[16:22].reshape(2, 3, C), tiny[22:28].reshape(2, 3, C)
-    sums = jnp.sum(tiny[28:34], axis=1)
-    sums, count = sums[:5], sums[5]
-    g_be, dbqkv, dmg, dms = tiny[0:2], tiny[2:4, :384].reshape(2, 3, 128), tiny[10, :256], tiny[10, 256:]
-    g_bias = jnp.stack([dbqkv[:, 0], dbqkv[:, 2]], axis=1)
-    g_tab = tiny[4:10].reshape(2, 4, 384)[:, :, :361].transpose(0, 2, 1)
-    blocks = packed.reshape(26, 512, 128)
-    cut = lambda lo, hi: jnp.stack([blocks[12 + lo : 12 + hi], blocks[lo:hi]])
-    lanes = lambda x: x.transpose(0, 2, 1, 3).reshape(2, x.shape[2], C)
-    g_we, g_ws = lanes(cut(0, 4)), lanes(cut(4, 8))
-    g_qkv = cut(8, 11).transpose(0, 2, 1, 3)
-    g_wo = lanes(cut(11, 12).reshape(2, 4, 128, 128))
-    dmw = blocks[24:26].reshape(4, 256, 128).transpose(1, 0, 2).reshape(256, C)
-    back = lambda x: x.reshape((2, 2, 64) + x.shape[1:]).swapaxes(0, 1).reshape((4, 64) + x.shape[1:])
-    rms = jnp.sqrt(sums / (count * C))
+    we, ws, qkv, wo, dmw, dmg, dms, dg1, db1, dbias, table, dbo, dg2, db2, dbe, dbs, rms = unpack(packed, tiny)
     return (
-        output, patches_grad, back(dmg), back(dms), back(dmw), small1[:, 0], small1[:, 1], g_qkv, g_bias,
-        g_tab, g_wo, small1[:, 2], small2[:, 0], small2[:, 1], g_we, g_be, g_ws, small2[:, 2], rms,
+        output, patches_grad, dmg, dms, dmw, dg1, db1, qkv.transpose(0, 2, 1, 3), dbias, table.transpose(0, 2, 1),
+        wo, dbo, dg2, db2, we, dbe, ws, dbs, rms[:5, 0],
     )
 
 

time: 427 us -> 398 us (0.932)
  local copies, waits for them, and re-layouts: 51.1 us -> 27.4 us
  other arithmetic: 11.3 us -> 2.89 us
    reshape x12 -> x0, local copies, waits for them, and re-layouts: 9.1 us -> none  [the longest x6 7.69 us: shards(): three = lambda x: x.reshape(2, 1, C)]
    slice x20 -> x1, local copies, waits for them, and re-layouts: 8.62 us -> 0.63 us  [shards(): rms[:5, 0]]
    pallas_call x0 -> x1, Pallas kernels: none -> 5.38 us  [unpack(): pl.pallas_call(unpack_kernel, grid=(2,), in_specs=[pl.BlockSpec((12, 512,...]
    unnamed x20 -> x15, local copies, waits for them, and re-layouts: 9.79 us -> 7.98 us
where the time goes in v5:
time: 398 us; the launch traced here: 397 us
  Pallas kernels  364 us (91%)
  local copies, waits for them, and re-layouts  27.4 us (7%)
    pallas_call x1, Pallas kernels, backward(): pl.pallas_call(functools.partial(bwd_kernel, n), grid=(STEPS,), in_specs=...  232 us
    pallas_call x1, Pallas kernels, forward(): pl.pallas_call(functools.partial(fwd_kernel, n), grid=(F_STEPS,), in_spec...  126 us
    unnamed x15, local copies, waits for them, and re-layouts  7.98 us

profile of v5, /device:TPU:0, one launch (start us, length us, event | category | flops | bytes accessed | tf_op | source)
XLA Modules:
  0.0 397.1 jit_solution(6619086468047501715)
XLA Ops:
  0.7 0.1 pad.27.clone
  0.7 0.1 pad.30.clone
  0.8 0.7 copy.82
  1.5 0.1 reshape.130
  1.6 0.7 copy.81
  2.3 0.1 reshape.132
  2.4 0.7 pad_bitcast_fusion
  3.0 0.7 maximum_maximum_fusion.1.refs_2_.refs_20_
  3.7 0.7 convert_element_type.11
  4.4 1.4 maximum_maximum_fusion.refs_8_
  5.8 0.8 reshape.152
  6.6 0.1 reshape.138
  6.7 0.1 copy.59
  6.8 0.1 copy.60
  6.9 0.6 pad.19.refs_16_
  7.5 2.0 copy.53
  9.5 1.6 convolution_bitcast_fusion
  11.1 0.6 copy.56
  11.7 0.3 reshape.153
  11.9 0.0 copy-done.1
  11.9 0.0 copy-start.3
  12.0 0.7 convolution_bitcast_fusion.1
  12.7 0.1 copy.73
  12.8 0.8 pad.18.clone
  13.6 0.1 reshape.140
  13.7 0.1 slice.31
  13.8 0.1 maximum_bitcast_fusion
  13.9 0.1 copy.61
  14.1 0.1 copy.62
  14.2 0.9 pad.20.refs_17_
  15.1 1.9 copy.50
  17.0 1.5 reshape.124
  18.6 2.5 copy.74
  21.1 1.0 reshape.157
  22.1 1.3 pad.17.clone
  23.3 126.4 %forward.1 = (f32[4,2,4,512,128]{4,3,2,1,0:T(8,128)}, f32[4,2,9,128,512]{4,3,2,1,0:T(8,128)}, f32[4,2,6,32,128]{4,3,2,1,0:T(8,128)}, f32[2,384,512]{2,1,0:T(8,12...) custom-call(f32[4,384,256]{2,1,0:T(8,128)} %bitcast.62, ...), custom_call_target="tpu_custom_call" | custom-call | tf_op jit(solution)/shard_map/forward/pallas_call | solution.py:639
  149.8 231.8 %backward.1 = (f32[4,12288,128]{2,1,0:T(8,128)}, f32[4,384,512]{2,1,0:T(8,128)}, f32[4,8,384]{2,1,0:T(8,128)}, f32[2,24,32,128]{3,2,1,0:T(8,128)}, f32[13312,128...) custom-call(f32[4,2,192,128]{3,2,1,0:T(8,128)} %bitcast.76, f32[2,384,512]{2,1,0:T(8,128)} %get-tuple-element.55.refs_1_, ...), custom_call_target="tpu_custom_call" | custom-call | tf_op jit(solution)/shard_map/backward/pallas_call | solution.py:1247
  381.6 2.1 reshape.158
  383.7 0.1 slice.28
  383.7 0.1 pad_maximum_fusion
  383.8 0.4 copy.63
  384.2 0.2 copy.64
  384.4 0.9 reshape.145
  385.3 1.5 copy.66
  386.8 2.5 reshape.148
  389.3 1.8 copy.67
  391.1 5.4 %unpack.1 = (f32[2,512,512]{2,1,0:T(8,128)}, f32[2,512,512]{2,1,0:T(8,128)}, f32[2,3,512,128]{3,2,1,0:T(8,128)}, f32[2,128,512]{2,1,0:T(8,128)}, f32[4,64,512]{2...) custom-call(f32[26,512,128]{2,1,0:T(8,128)} %bitcast.60, ...), custom_call_target="tpu_custom_call" | custom-call | tf_op jit(solution)/shard_map/unpack/pallas_call | solution.py:1321
  396.5 0.6 slice_reduce_fusion
  (12 shorter events, 0.1 us)
Async XLA Ops:
  7.5 4.4 %copy-start.1 = (f32[2,5,128,190,1,1]{2,3,1,0,5,4:T(8,128)S(1)}, f32[2,5,128,190,1,1]{2,3,1,0,5,4:T(8,128)}, u32[]{:S(2)}) copy-start(f32[2,5,128,190,1,1]{2,3,1,0,5,4:T(8,128)} %constant.34) | copy-start | bytes 2918404
  11.9 1.7 copy-start.3
  381.6 2.1 copy-start.2
  389.2 1.8 copy-start

commit v6 on v5

--- a/solution.py
+++ b/solution.py
@@ -18,6 +18,7 @@
 WT = 128
 TOK = 384
 NW = 3
+DENSE = 304
 GROUP = 4
 
 bf16 = jnp.bfloat16
@@ -47,6 +48,23 @@
     center = x - jnp.mean(x, axis=-1, keepdims=True)
     rho = lax.rsqrt(jnp.mean(center * center, axis=-1, keepdims=True) + epsilon)
     return center * rho, rho
+
+
+def placing():
+    token = lax.broadcasted_iota(jnp.int32, (TOK, DENSE), 0)
+    column = lax.broadcasted_iota(jnp.int32, (TOK, DENSE), 1)
+    inner = token % SUB
+    return ((inner < REAL) & (column == (token // SUB) * REAL + inner)).astype(f32).astype(bf16)
+
+
+def selected(pick, x, dims):
+    high, rest = x.astype(bf16), x - x.astype(bf16).astype(f32)
+    mid, low = split(rest)
+    return mm(pick, high, dims) + (mm(pick, mid, dims) + mm(pick, low, dims))
+
+
+def upright(columns):
+    return jnp.concatenate([columns, jnp.zeros((TOK - DENSE, 128), f32)], axis=0).T[0:8, :]
 
 
 def head_masks(dtype):
@@ -131,7 +149,7 @@
 F_STEPS = 19
 
 
-TURNS = (0, 0, 0, 5, 11, 13, 15, 18, 21, 23, 25, 27, 28, 29, 30, 30, 30, 30, 30, 30)
+TURNS = (0, 0, 0, 2, 9, 11, 13, 15, 17, 19, 21, 23, 25, 27, 29, 30, 30, 30, 30, 30)
 LAG = 2
 AHEAD = 6
 
@@ -325,14 +343,14 @@
             vs_ref[w : w + 1, :] = sent
             regr_ref[1, w : w + 1, :] = region
         valid_copy().start()
-        lane = lax.broadcasted_iota(jnp.int32, (TOK, 128), 1)
+        lane = lax.broadcasted_iota(jnp.int32, (DENSE, 128), 1)
 
         def project(i):
             quad = q_ref[tp ^ i]
             pb[i] = mm3(split(quad * gain), wpair, NN)
             s1 = jnp.sum(quad, axis=-1, keepdims=True)
             s2 = jnp.sum(quad * quad, axis=-1, keepdims=True)
-            stb[i] = jnp.where(lane == 0, s1, jnp.where(lane == 1, s2, 0.0)).T[0:8, :]
+            stb[i] = upright(jnp.where(lane == 0, s1, jnp.where(lane == 1, s2, 0.0)))
 
         project(3)
         for copy in rs_copies(1):
@@ -389,12 +407,83 @@
                 copy.wait_send()
         for copy in rs_copies(2):
             copy.wait()
-        sums = jnp.concatenate([stb[0] + stx[...], jnp.zeros((120, TOK), f32)], axis=0).T
+        sums = jnp.concatenate([stb[0] + stx[...], jnp.zeros((120, TOK), f32)], axis=0).T[0:DENSE, :]
         mean = sums[:, 0:1] / (4.0 * C2)
         inverse = lax.rsqrt(sums[:, 1:2] / (4.0 * C2) - mean * mean + epsilon)
-        lane = lax.broadcasted_iota(jnp.int32, (TOK, 128), 1)
+        lane = lax.broadcasted_iota(jnp.int32, (DENSE, 128), 1)
         stat_ref[...] = jnp.where(lane == 0, mean, jnp.where(lane == 1, inverse, 0.0))
-        field[...] = inverse * (pb[0] + px[...] - mean * vec_ref[0:1, :]) + vec_ref[1:2, :]
+        dense = inverse * (pb[0] + px[...] - mean * vec_ref[0:1, :]) + vec_ref[1:2, :]
+        field[...] = selected(placing(), dense, NN)
+
+    def both(c, act):
+        def run(buf, k, size):
+            for low in (False, True):
+
+                @pl.when(deep(c) == low)
+                def _(low=low):
+                    act(buf, k, size, low)
+
+        each(c, run)
+
+    def gather_turn(p):
+        @pl.when(p + AHEAD < GCH)
+        def _():
+            x_start(p + AHEAD)
+
+        @pl.when(p < GCH)
+        def _():
+            def act(buf, k, size, low):
+                x_copy(p, buf, k, size, low).wait_recv()
+                y_copy(p, buf, k, size, low).start()
+                if not low:
+                    for h in range(2):
+
+                        @pl.when(par == h)
+                        def _(h=h):
+                            s_copy(h, p, buf, k, size).start()
+
+            both(p, act)
+
+        y = p - LAG
+
+        @pl.when((y >= 0) & (y < GCH))
+        def _():
+            def act(buf, k, size, low):
+                y_copy(y, buf, k, size, low).wait_recv()
+                x_copy(y, buf, k, size, low).wait_send()
+                half_here = zpar if low else 1 - par
+                if low:
+                    z_copy(y, buf, k, size).start()
+                for h in range(2):
+
+                    @pl.when(half_here == h)
+                    def _(h=h):
+                        s_copy(h, y, buf, k, size).start()
+
+            both(y, act)
+
+        z = p - 2 * LAG
+
+        @pl.when((z >= 0) & (z < GCH))
+        def _():
+            def act(buf, k, size, low):
+                y_copy(z, buf, k, size, low).wait_send()
+                if low:
+                    z_copy(z, buf, k, size).wait_recv()
+                    for h in range(2):
+
+                        @pl.when(1 - zpar == h)
+                        def _(h=h):
+                            s_copy(h, z, buf, k, size).start()
+
+            both(z, act)
+
+    def midway():
+        first = so_far(TURNS, step)
+
+        @pl.when(first < so_far(TURNS, step + 1))
+        def _():
+            gather_turn(first)
 
     att, mlp = fwd_order(step)
 
@@ -455,6 +544,8 @@
             p = e / jnp.sum(e, axis=-1, keepdims=True)
             p_ref[0, j] = p
             att_ref[0, rows, :] = mm3(side_by_side(split(p)), v4, NN)
+            if j == 1:
+                midway()
         mixed[...] += mm3(split(att_ref[0]), split(wb[i, 9 * b + 8]), NN)
 
         @pl.when(i == 3)
@@ -498,6 +589,7 @@
         hidden = pre * phi
         hid_ref[0] = hidden
         slope_ref[0] = phi + pre * (jnp.exp(-0.5 * pre * pre) * ((2 * np.pi) ** -0.5))
+        midway()
         mixed[...] += mm3(split(hidden), split(ws), NN)
 
         @pl.when(i == 3)
@@ -531,69 +623,9 @@
                 if k + i > 0:
                     cot_copy(k, i).start()
 
-    def both(c, act):
-        def run(buf, k, size):
-            for low in (False, True):
-
-                @pl.when(deep(c) == low)
-                def _(low=low):
-                    act(buf, k, size, low)
-
-        each(c, run)
-
-    @pl.loop(so_far(TURNS, step), so_far(TURNS, step + 1))
+    @pl.loop(so_far(TURNS, step) + 1, so_far(TURNS, step + 1))
     def _(p):
-        @pl.when(p + AHEAD < GCH)
-        def _():
-            x_start(p + AHEAD)
-
-        @pl.when(p < GCH)
-        def _():
-            def act(buf, k, size, low):
-                x_copy(p, buf, k, size, low).wait_recv()
-                y_copy(p, buf, k, size, low).start()
-                if not low:
-                    for h in range(2):
-
-                        @pl.when(par == h)
-                        def _(h=h):
-                            s_copy(h, p, buf, k, size).start()
-
-            both(p, act)
-
-        y = p - LAG
-
-        @pl.when((y >= 0) & (y < GCH))
-        def _():
-            def act(buf, k, size, low):
-                y_copy(y, buf, k, size, low).wait_recv()
-                x_copy(y, buf, k, size, low).wait_send()
-                half_here = zpar if low else 1 - par
-                if low:
-                    z_copy(y, buf, k, size).start()
-                for h in range(2):
-
-                    @pl.when(half_here == h)
-                    def _(h=h):
-                        s_copy(h, y, buf, k, size).start()
-
-            both(y, act)
-
-        z = p - 2 * LAG
-
-        @pl.when((z >= 0) & (z < GCH))
-        def _():
-            def act(buf, k, size, low):
-                y_copy(z, buf, k, size, low).wait_send()
-                if low:
-                    z_copy(z, buf, k, size).wait_recv()
-                    for h in range(2):
-
-                        @pl.when(1 - zpar == h)
-                        def _(h=h):
-                            s_copy(h, z, buf, k, size).start()
-
-            both(z, act)
+        gather_turn(p)
 
     @pl.when(step == F_STEPS - 1)
     def _():
@@ -640,21 +672,21 @@
         functools.partial(fwd_kernel, n),
         grid=(F_STEPS,),
         in_specs=[
-            fixed((4, TOK, 256)), fixed((256, C)), fixed((8, 256)), ANY, ANY, ANY, ANY, ANY, ANY,
+            fixed((4, DENSE, 256)), fixed((256, C)), fixed((8, 256)), ANY, ANY, ANY, ANY, ANY, ANY,
             two, two, two, two, two, two, pl.BlockSpec(memory_space=pltpu.SMEM), fixed((2, 24, 128)), ANY,
         ],
         out_specs=[
             ANY, ANY, ANY, by(second, (TOK, C)), by(second, (TOK, C)), by(att_at, (TOK, 384)),
             by(att_at, (NW, GROUP * WT, WT)), by(att_at, (TOK, 128)), by(mlp_at, (TOK, 512)),
-            by(mlp_at, (TOK, 512)), fixed((TOK, 128)), fixed((8, C)), fixed((8, C)), fixed((4, 2, 192, 128)),
+            by(mlp_at, (TOK, 512)), fixed((DENSE, 128)), fixed((8, C)), fixed((8, C)), fixed((4, 2, 192, 128)),
         ],
         out_shape=[
             sds(4, 2, 4, 512, 128), sds(4, 2, 9, 128, 512), sds(4, 2, 6, SUB, 128), sds(2, TOK, C), sds(2, TOK, C),
             sds(8, TOK, 384), sds(8, NW, GROUP * WT, WT), sds(8, TOK, 128), sds(8, TOK, 512), sds(8, TOK, 512),
-            sds(TOK, 128), sds(8, C), sds(8, C), sds(4, 2, 192, 128),
+            sds(DENSE, 128), sds(8, C), sds(8, C), sds(4, 2, 192, 128),
         ],
         scratch_shapes=[
-            vm(4, 8, 512, 128), vm(4, 18, 128, 512), vm(4, 8, C), vm(4, TOK, C), vm(2, TOK, C), vm(TOK, C),
+            vm(4, 8, 512, 128), vm(4, 18, 128, 512), vm(4, 8, C), vm(4, DENSE, C), vm(2, DENSE, C), vm(DENSE, C),
             vm(4, 8, TOK), vm(2, 8, TOK), vm(8, TOK), vm(4, 8, C), vm(8, 128), vm(8, 128), vm(8, 128), vm(8, 128), vm(2, TOK, 1), vm(2, 8, 128), vm(2, TOK, 1),
             vm(TOK, C),
             pltpu.VMEM((TOK, C), bf16), pltpu.VMEM((TOK, C), bf16), vm(TOK, C), vm(TOK, C),
@@ -706,12 +738,12 @@
     ) = refs[:25]
     pack, gall, exall, ob, out_ref, gq_ref, tout_ref = refs[25:32]
     (
-        nth, ntl, gh, gl, acc, dqkv, gf, gbuf, moved, ext, extin, qbuf,
+        nth, ntl, gh, gl, acc, dqkv, gf, gbuf, moved, ext, extin, qbuf, gdense,
         loc, pair, yr, zr, fin, ta, tx, tz, tsh, tr,
         gsem, mvs, mvr, ags, agr, agl, msem, ss, rs, zs, zq, fs, fq, ls, os, tzs, tzq, obs, obr, obl, tss, tsq,
     ) = refs[32:]
     step = pl.program_id(0)
-    dmw, gqbuf = moved.at[pl.ds(0, 256)], dqkv.at[:, pl.ds(0, 256)]
+    dmw, gqbuf = moved.at[pl.ds(0, 256)], dqkv.at[pl.ds(0, DENSE), pl.ds(0, 256)]
     sp, tp, sib, across, beside = here()
     par, mine = sp & 1, sp // 2
     m = n // 2
@@ -912,7 +944,7 @@
         return push(src, dst, ags.at[which, k], agr.at[which, k], peer)
 
     def ag_copies(k):
-        own = (acc, ext)
+        own = (gdense, ext)
         whole_ = (gall, exall)
         return [
             ag(k, own[w], whole_[w].at[tp], (sib, across)[k], w) if k < 2
@@ -923,9 +955,11 @@
     @pl.when(step == AG_STEP)
     def _():
         m2 = jnp.sum(acc[...] * (field_ref[0] - vec_ref[1:2, :]), axis=-1, keepdims=True)
-        lane = lax.broadcasted_iota(jnp.int32, (TOK, 128), 1)
-        tall = jnp.where(lane == 2, m2, stat_ref[...])
-        ext[...] = tall.T[0:8, :]
+        pick = placing()
+        gdense[...] = selected(pick, acc[...], TN)
+        lane = lax.broadcasted_iota(jnp.int32, (DENSE, 128), 1)
+        tall = selected(pick, jnp.broadcast_to(m2, (TOK, 128)), TN)
+        ext[...] = upright(jnp.where(lane == 2, tall, stat_ref[...]))
         for k in range(2):
             for copy in ag_copies(k):
                 copy.start()
@@ -952,13 +986,13 @@
         @pl.when(i == 0)
         def _():
             dmw[...] = jnp.zeros((256, C), f32)
-            gf[...] = acc[...]
+            gf[0:DENSE, :] = gdense[...]
             extin[...] = ext[...]
 
         @pl.when(i > 0)
         def _():
             two = [
-                pltpu.make_async_copy(gall.at[t], gf, msem.at[1]),
+                pltpu.make_async_copy(gall.at[t], gf.at[pl.ds(0, DENSE)], msem.at[1]),
                 pltpu.make_async_copy(exall.at[t], extin, msem.at[2]),
             ]
             for copy in two:
@@ -967,15 +1001,15 @@
                 copy.wait()
 
         fetch[0].wait()
-        wide = jnp.concatenate([extin[...], jnp.zeros((120, TOK), f32)], axis=0).T
+        wide = jnp.concatenate([extin[...], jnp.zeros((120, TOK), f32)], axis=0).T[0:DENSE, :]
         mean, inv, m2 = wide[:, 0:1], wide[:, 1:2], wide[:, 2:3]
-        full = gf[...]
+        full = gf[0:DENSE, :]
         m1 = jnp.sum(full * vec_ref[0:1, :], axis=-1, keepdims=True) / (4.0 * C2)
         m2 = m2 / (4.0 * C2)
         fpair = split(full)
         xhat = (qbuf[...] - mean) * inv
         gmerged = mm3(fpair, split(mw_ref[...]), NT)
-        dmw[...] += mm3(split((xhat * mg_ref[0:1, :] + mg_ref[1:2, :]).T), fpair, NN)
+        dmw[...] += mm3(split(xhat * mg_ref[0:1, :] + mg_ref[1:2, :]), fpair, TN)
         tsh[0, 10:11, 0:256] += colsum(gmerged * xhat)
         tsh[0, 10:11, 256:512] += colsum(gmerged)
 
@@ -1241,7 +1275,7 @@
         spot(att_at, (1, 128, C), 8),
         by(mlp_at, (TOK, 512)), by(mlp_at, (TOK, 512)), by(att_at, (TOK, 384)),
         by(att_at, (NW, GROUP * WT, WT)), by(att_at, (TOK, 128)),
-        fixed((8, C)), ANY, fixed((256, C)), fixed((8, C)), fixed((8, 256)), fixed((TOK, 128)), ANY,
+        fixed((8, C)), ANY, fixed((256, C)), fixed((8, C)), fixed((8, 256)), fixed((DENSE, 128)), ANY,
         fixed((WT, 384)), fixed((160, WT)),
     ]
     return pl.pallas_call(
@@ -1250,14 +1284,15 @@
         in_specs=in_specs,
         out_specs=[ANY, ANY, ANY, ANY, ANY, ANY, fixed((TINY, C))],
         out_shape=[
-            sds(4, FULL_CH * ROWS, 128), sds(4, TOK, C), sds(4, 8, TOK), sds(2, 24, SUB, 128), sds(CHUNKS * ROWS, 128),
-            sds(4, TOK, 256), sds(TINY, C),
+            sds(4, FULL_CH * ROWS, 128), sds(4, DENSE, C), sds(4, 8, TOK), sds(2, 24, SUB, 128), sds(CHUNKS * ROWS, 128),
+            sds(4, DENSE, 256), sds(TINY, C),
         ],
         scratch_shapes=[
             pltpu.VMEM((C, TOK), bf16), pltpu.VMEM((C, TOK), bf16), pltpu.VMEM((TOK, C), bf16),
             pltpu.VMEM((TOK, C), bf16), pltpu.VMEM((TOK, C), f32), pltpu.VMEM((TOK, 384), f32),
             pltpu.VMEM((TOK, C), f32), pltpu.VMEM((2, MLP_ROWS, 128), f32), pltpu.VMEM((TOK, C), f32),
-            pltpu.VMEM((8, TOK), f32), pltpu.VMEM((8, TOK), f32), pltpu.VMEM((TOK, 256), f32),
+            pltpu.VMEM((8, TOK), f32), pltpu.VMEM((8, TOK), f32), pltpu.VMEM((DENSE, 256), f32),
+            pltpu.VMEM((DENSE, C), f32),
             pltpu.VMEM((4, 2, ROWS, 128), f32), pltpu.VMEM((CHUNKS, 2, ROWS, 128), f32),
             pltpu.VMEM((CHUNKS, HALF, 128), f32), pltpu.VMEM((CHUNKS, m, HALF // m, 128), f32),
             pltpu.VMEM(lanes, f32), pltpu.VMEM((4, TINY, C), f32), pltpu.VMEM((3, TINY, C), f32),
@@ -1388,8 +1423,8 @@
     offset = merge_shift.reshape(2, 2, 64).transpose(1, 0, 2).reshape(1, 256)
     mgain = jnp.concatenate([gain, offset, jnp.zeros((6, 256), f32)], axis=0)
     weight = merge_weight.reshape(2, 2, 64, C).transpose(1, 0, 2, 3).reshape(256, C)
-    quads = patches.reshape(2, 5, 2, 4, NW, 2, 5, 128).transpose(3, 4, 0, 5, 1, 6, 2, 7).reshape(4, NW, 4, REAL, 256)
-    quads = jnp.pad(quads, ((0, 0), (0, 0), (0, 0), (0, SUB - REAL), (0, 0))).reshape(4, TOK, 256)
+    quads = patches.reshape(2, 5, 2, 4, NW, 2, 5, 128).transpose(3, 4, 0, 5, 1, 6, 2, 7).reshape(4, 300, 256)
+    quads = jnp.pad(quads, ((0, 0), (0, DENSE - 300), (0, 0)))
     cot = jnp.roll(cotangent.reshape(2, 5, 24, 5, 128), -1, axis=2).transpose(0, 2, 1, 3, 4).reshape(2, 24, REAL, 128)
     cot = jnp.pad(cot, ((0, 0), (0, 0), (0, SUB - REAL), (0, 0)))
 
@@ -1415,7 +1450,7 @@
     )
     output = jnp.roll(output[:, :, :REAL], 1, axis=1).reshape(2, 24, 5, 5, 128)
     output = output.transpose(0, 2, 1, 3, 4).reshape(10, 120, 128)
-    gquads = gquads.reshape(4, NW, 4, SUB, 256)[:, :, :, :REAL].reshape(4, NW, 2, 2, 5, 5, 2, 128)
+    gquads = gquads[:, :300].reshape(4, NW, 2, 2, 5, 5, 2, 128)
     patches_grad = gquads.transpose(2, 4, 6, 0, 1, 3, 5, 7).reshape(20, 240, 64)
     we, ws, qkv, wo, dmw, dmg, dms, dg1, db1, dbias, table, dbo, dg2, db2, dbe, dbs, rms = unpack(packed, tiny)
     return (

time: 398 us -> 389 us (0.977)
  Pallas kernels: 364 us -> 353 us
    pallas_call x1, Pallas kernels: 126 us -> 120 us  [forward(): pl.pallas_call(functools.partial(fwd_kernel, n), grid=(F_STEPS,), in_spec...]
    pallas_call x1, Pallas kernels: 232 us -> 228 us  [backward(): pl.pallas_call(functools.partial(bwd_kernel, n), grid=(STEPS,), in_specs=...]
    unnamed x15 -> x13, local copies, waits for them, and re-layouts: 7.98 us -> 4.5 us
where the time goes in v6:
time: 389 us; the launch traced here: 387 us
  Pallas kernels  353 us (91%)
  local copies, waits for them, and re-layouts  27.2 us (7%)
    pallas_call x1, Pallas kernels, backward(): pl.pallas_call(functools.partial(bwd_kernel, n), grid=(STEPS,), in_specs=...  228 us
    pallas_call x1, Pallas kernels, forward(): pl.pallas_call(functools.partial(fwd_kernel, n), grid=(F_STEPS,), in_spec...  120 us

profile of v6, /device:TPU:0, one launch (start us, length us, event | category | flops | bytes accessed | tf_op | source)
XLA Modules:
  0.0 386.6 jit_solution(7413148933775122582)
XLA Ops:
  0.7 0.1 pad.27.clone
  0.7 0.1 pad.30.clone
  0.8 0.7 copy.74
  1.5 0.1 reshape.123
  1.6 0.7 copy.73
  2.3 0.1 reshape.125
  2.4 0.7 pad_bitcast_fusion
  3.0 0.7 maximum_maximum_fusion.1.refs_2_.refs_20_
  3.7 0.7 convert_element_type.11
  4.4 1.4 maximum_maximum_fusion.refs_8_
  5.8 0.8 reshape.144
  6.6 0.1 reshape.131
  6.7 0.1 copy.58
  6.8 0.1 copy.59
  6.9 0.6 pad.19.refs_16_
  7.5 2.0 copy.52
  9.5 1.6 convolution_bitcast_fusion
  11.1 0.6 copy.55
  11.7 0.3 reshape.145
  11.9 0.0 copy-done.1
  11.9 0.0 copy-start.3
  12.0 0.7 convolution_bitcast_fusion.1
  12.7 0.1 copy.69
  12.8 0.8 pad.18.clone
  13.6 0.1 reshape.133
  13.7 0.1 slice.31
  13.8 0.1 maximum_bitcast_fusion
  13.9 0.1 copy.60
  14.1 0.1 copy.61
  14.2 0.9 pad.20.refs_17_
  15.1 1.9 copy.50
  17.0 1.5 reshape.118
  18.6 2.5 copy.51
  21.1 1.0 reshape.119
  22.1 1.1 pad.17.refs_0_.refs_17_
  23.2 120.3 %forward.1 = (f32[4,2,4,512,128]{4,3,2,1,0:T(8,128)}, f32[4,2,9,128,512]{4,3,2,1,0:T(8,128)}, f32[4,2,6,32,128]{4,3,2,1,0:T(8,128)}, f32[2,384,512]{2,1,0:T(8,12...) custom-call(f32[4,304,256]{2,1,0:T(8,128)} %pad.17.refs_0_.refs_17_,, ...), custom_call_target="tpu_custom_call" | custom-call | tf_op jit(solution)/shard_map/forward/pallas_call | solution.py:671
  143.5 227.7 %backward.1 = (f32[4,12288,128]{2,1,0:T(8,128)}, f32[4,304,512]{2,1,0:T(8,128)}, f32[4,8,384]{2,1,0:T(8,128)}, f32[2,24,32,128]{3,2,1,0:T(8,128)}, f32[13312,128...) custom-call(f32[4,2,192,128]{3,2,1,0:T(8,128)} %bitcast.71, f32[2,384,512]{2,1,0:T(8,128)} %get-tuple-element.55.refs_1_, ...), custom_call_target="tpu_custom_call" | custom-call | tf_op jit(solution)/shard_map/backward/pallas_call | solution.py:1281
  371.2 2.0 reshape.139
  373.2 0.1 slice.28
  373.3 0.1 pad_maximum_fusion
  373.3 0.4 copy.62
  373.7 0.2 copy.63
  373.9 0.9 reshape.138
  374.8 1.5 copy.64
  376.3 2.5 reshape.140
  378.8 1.8 copy.65
  380.6 5.4 %unpack.1 = (f32[2,512,512]{2,1,0:T(8,128)}, f32[2,512,512]{2,1,0:T(8,128)}, f32[2,3,512,128]{3,2,1,0:T(8,128)}, f32[2,128,512]{2,1,0:T(8,128)}, f32[4,64,512]{2...) custom-call(f32[26,512,128]{2,1,0:T(8,128)} %bitcast.57, ...), custom_call_target="tpu_custom_call" | custom-call | tf_op jit(solution)/shard_map/unpack/pallas_call | solution.py:1356
  386.0 0.6 slice_reduce_fusion
  (12 shorter events, 0.1 us)
Async XLA Ops:
  7.5 4.4 %copy-start.1 = (f32[2,5,128,190,1,1]{2,3,1,0,5,4:T(8,128)S(1)}, f32[2,5,128,190,1,1]{2,3,1,0,5,4:T(8,128)}, u32[]{:S(2)}) copy-start(f32[2,5,128,190,1,1]{2,3,1,0,5,4:T(8,128)} %constant.34) | copy-start | bytes 2918404
  11.9 1.7 copy-start.3
  371.2 2.0 copy-start.2
  378.8 1.8 copy-start

commit v7 on v6

--- a/solution.py
+++ b/solution.py
@@ -739,8 +739,8 @@
     pack, gall, exall, ob, out_ref, gq_ref, tout_ref = refs[25:32]
     (
         nth, ntl, gh, gl, acc, dqkv, gf, gbuf, moved, ext, extin, qbuf, gdense,
-        loc, pair, yr, zr, fin, ta, tx, tz, tsh, tr,
-        gsem, mvs, mvr, ags, agr, agl, msem, ss, rs, zs, zq, fs, fq, ls, os, tzs, tzq, obs, obr, obl, tss, tsq,
+        loc, pair, yr, zr, fin, ta, tx, tsh, tr,
+        gsem, mvs, mvr, ags, agr, agl, msem, ss, rs, zs, zq, fs, fq, ls, os, obs, obr, obl, tss, tsq,
     ) = refs[32:]
     step = pl.program_id(0)
     dmw, gqbuf = moved.at[pl.ds(0, 256)], dqkv.at[pl.ds(0, DENSE), pl.ds(0, 256)]
@@ -821,6 +821,279 @@
         for w0, s0, w1, s1 in COLS:
             moved[at(w1, 1, s1), :] = acc[at(w0, 0, s0), :]
 
+    def ag(k, src, dst, peer, which):
+        return push(src, dst, ags.at[which, k], agr.at[which, k], peer)
+
+    def ag_copies(k):
+        own = (gdense, ext)
+        whole_ = (gall, exall)
+        return [
+            ag(k, own[w], whole_[w].at[tp], (sib, across)[k], w) if k < 2
+            else ag(k, whole_[w].at[tp ^ 2], whole_[w].at[tp ^ 2], sib, w)
+            for w in range(2)
+        ]
+
+    def ag_pass():
+        for copy in ag_copies(1):
+            copy.wait()
+        for copy in ag_copies(2):
+            copy.start()
+
+    def merge(i):
+        t = tp ^ i
+
+        for k in (0, 2):
+
+            @pl.when(i == (1 if k == 0 else 2))
+            def _(k=k):
+                for copy in ag_copies(k):
+                    copy.wait()
+
+        fetch = [pltpu.make_async_copy(q_ref.at[t], qbuf, msem.at[0])]
+        fetch[0].start()
+
+        @pl.when(i == 0)
+        def _():
+            dmw[...] = jnp.zeros((256, C), f32)
+            gf[0:DENSE, :] = gdense[...]
+            extin[...] = ext[...]
+
+        @pl.when(i > 0)
+        def _():
+            two = [
+                pltpu.make_async_copy(gall.at[t], gf.at[pl.ds(0, DENSE)], msem.at[1]),
+                pltpu.make_async_copy(exall.at[t], extin, msem.at[2]),
+            ]
+            for copy in two:
+                copy.start()
+            for copy in two:
+                copy.wait()
+
+        fetch[0].wait()
+        wide = jnp.concatenate([extin[...], jnp.zeros((120, TOK), f32)], axis=0).T[0:DENSE, :]
+        mean, inv, m2 = wide[:, 0:1], wide[:, 1:2], wide[:, 2:3]
+        full = gf[0:DENSE, :]
+        m1 = jnp.sum(full * vec_ref[0:1, :], axis=-1, keepdims=True) / (4.0 * C2)
+        m2 = m2 / (4.0 * C2)
+        fpair = split(full)
+        xhat = (qbuf[...] - mean) * inv
+        gmerged = mm3(fpair, split(mw_ref[...]), NT)
+        dmw[...] += mm3(split(xhat * mg_ref[0:1, :] + mg_ref[1:2, :]), fpair, TN)
+        tsh[0, 10:11, 0:256] += colsum(gmerged * xhat)
+        tsh[0, 10:11, 256:512] += colsum(gmerged)
+
+        @pl.when(i > 0)
+        def _():
+            pltpu.make_async_copy(gqbuf, gq_ref.at[t], msem.at[3]).wait()
+
+        gqbuf[...] = inv * (gmerged * mg_ref[0:1, :] - m1 - xhat * m2)
+        pltpu.make_async_copy(gqbuf, gq_ref.at[t], msem.at[3]).start()
+
+        @pl.when(i == 3)
+        def _():
+            pltpu.make_async_copy(gqbuf, gq_ref.at[t], msem.at[3]).wait()
+            for k in range(4):
+                row = k * 256
+                pair[FULL_CH + row // ROWS, 0, row % ROWS : row % ROWS + 256, :] = dmw[:, k * 128 : (k + 1) * 128]
+
+    def rows(c):
+        return pl.ds(pl.multiple_of(c * ROWS, ROWS), ROWS)
+
+    def load(c, k):
+        return pltpu.make_async_copy(pack.at[tp ^ (2 * k), rows(c)], loc.at[c % 4, k], ls.at[c % 4, k])
+
+    def swap(c, k):
+        return push(pack.at[tp ^ 1 ^ (2 * k), rows(c)], pair.at[c, k], ss.at[k, c], rs.at[k, c], sib)
+
+    def cross(c):
+        return push(pair.at[c, 1], fin.at[c], ss.at[2, c], rs.at[2, c], across)
+
+    def halves(h):
+        return pl.ds(pl.multiple_of(h * HALF, HALF), HALF)
+
+    def side(c):
+        return push(pair.at[c, 0, halves(1 - par)], yr.at[c], ss.at[3, c], rs.at[3, c], beside)
+
+    def bit(q):
+        return pl.ds(pl.multiple_of(q * piece, piece), piece)
+
+    def spread(c, q, slot):
+        return push(yr.at[c, bit(q)], zr.at[c, slot], zs.at[c % 4, q], zq.at[c, slot], device(q))
+
+    def place(q):
+        return pl.ds(pl.multiple_of(par * HALF + q * piece, piece), piece)
+
+    def share(c, q, slot):
+        return push(fin.at[c, place(slot)], fin.at[c, place(slot)], fs.at[c % 4, q], fq.at[c, slot], device(q))
+
+    def back(c):
+        return push(fin.at[c, halves(par)], fin.at[c, halves(par)], ss.at[4, c], rs.at[4, c], beside)
+
+    def write(c):
+        return pltpu.make_async_copy(fin.at[c], out_ref.at[rows(c)], os.at[c])
+
+    low, high = pl.ds(0, 16), pl.ds(16, 24)
+
+    bits = m.bit_length() - 1
+
+    def tiny(k):
+        if k == 0:
+            todo = [(tsh.at[1], tr.at[0]), (tsh.at[3], tr.at[1]), (ta.at[0, high], tx.at[0, high])]
+        elif k == 1:
+            todo = [(tsh.at[2], tx.at[1, low]), (ta.at[1, high], tx.at[1, high])]
+        else:
+            todo = [(ta.at[k], tx.at[k])]
+        peer = (sib, across, beside)[k] if k < 3 else device(mine ^ (1 << (k - 3)))
+        return [push(a, b, tss.at[k, i], tsq.at[k, i], peer) for i, (a, b) in enumerate(todo)]
+
+    def tiny_sum(k):
+        if k == 0:
+            ta[1, low] = tsh[0] + tr[0]
+            ta[1, high] = ta[0, high] + tx[0, high]
+            tsh[2] = tsh[2] + tr[1]
+        else:
+            ta[k + 1] = ta[k] + tx[k]
+
+    late = RATE * (16 - FIRST)
+    tiny_turn = late + 10
+
+    def begun(s):
+        return jnp.where(s < FIRST, 0, jnp.where(s < STEPS, RATE * (s - FIRST), CHUNKS + 21))
+
+    def turn(p, last=False):
+        if last:
+            extra(p)
+        stages(p)
+
+    def extra(p):
+        @pl.when(p == late + 5)
+        def _():
+            ag_pass()
+
+        due = p - late
+
+        @pl.when((due >= 0) & (due < 12) & (due % 3 == 0))
+        def _():
+            merge(due // 3)
+
+        for k in range(4 + bits):
+
+            @pl.when(p == tiny_turn + 2 * k)
+            def _(k=k):
+                if k > 0:
+                    for copy in tiny(k - 1):
+                        copy.wait()
+                    tiny_sum(k - 1)
+                if k < 3 + bits:
+                    for copy in tiny(k):
+                        copy.start()
+
+    def stages(p):
+        def stage(lag, end):
+            c = p - lag
+            return c, (c >= 0) & (c < end)
+
+        c0, on0 = stage(0, FULL_CH)
+
+        @pl.when(on0)
+        def _():
+            swap(c0, 1).start()
+            load(c0, 1).start()
+
+        c1, on1 = stage(2, FULL_CH)
+
+        @pl.when(on1)
+        def _():
+            load(c1, 1).wait()
+            swap(c1, 1).wait_recv()
+            pair[c1, 1] = pair[c1, 1] + loc[c1 % 4, 1]
+            cross(c1).start()
+
+        c2, on2 = stage(4, FULL_CH)
+
+        @pl.when(on2)
+        def _():
+            swap(c2, 0).start()
+            load(c2, 0).start()
+
+        c3, on3 = stage(6, CHUNKS)
+
+        @pl.when(on3)
+        def _():
+            @pl.when(c3 < FULL_CH)
+            def _():
+                load(c3, 0).wait()
+                swap(c3, 0).wait_recv()
+                cross(c3).wait_recv()
+                pair[c3, 0] = (pair[c3, 0] + loc[c3 % 4, 0]) + fin[c3]
+                swap(c3, 1).wait_send()
+
+            side(c3).start()
+
+        c4, on4 = stage(9, CHUNKS)
+
+        @pl.when(on4)
+        def _():
+            @pl.when(c4 < FULL_CH)
+            def _():
+                swap(c4, 0).wait_send()
+                cross(c4).wait_send()
+
+            side(c4).wait_recv()
+            yr[c4] = yr[c4] + pair[c4, 0, halves(par)]
+
+            @pl.loop(1, m)
+            def _(j):
+                spread(c4, member(j), mine).start()
+
+        c5, on5 = stage(12, CHUNKS)
+
+        @pl.when(on5)
+        def _():
+            side(c5).wait_send()
+            fin[c5, place(mine)] = yr[c5, bit(mine)]
+
+            @pl.loop(1, m)
+            def _(j):
+                spread(c5, member(j), member(j)).wait_recv()
+                fin[c5, place(mine)] = fin[c5, place(mine)] + zr[c5, member(j)]
+
+            @pl.loop(1, m)
+            def _(j):
+                share(c5, member(j), mine).start()
+                spread(c5, member(j), mine).wait_send()
+
+        c6, on6 = stage(15, CHUNKS)
+
+        @pl.when(on6)
+        def _():
+            @pl.loop(1, m)
+            def _(j):
+                share(c6, member(j), member(j)).wait_recv()
+                share(c6, member(j), mine).wait_send()
+
+            back(c6).start()
+
+        c7, on7 = stage(18, CHUNKS)
+
+        @pl.when(on7)
+        def _():
+            back(c7).wait()
+            write(c7).start()
+
+        c8, on8 = stage(21, CHUNKS)
+
+        @pl.when(on8)
+        def _():
+            write(c8).wait()
+
+    def midway():
+        first = begun(step)
+
+        @pl.when(first < begun(step + 1))
+        def _():
+            turn(first)
+
     phase = step // 4
 
     @pl.when((phase == 0) | (phase == 2))
@@ -841,6 +1114,10 @@
             nth[...], ntl[...] = split((xhat * g2_ref[pl.ds(b, 1), :] + b2_ref[pl.ds(b, 1), :]).T)
             gh[...], gl[...] = split(gf[...])
             acc[...] = jnp.zeros_like(acc)
+
+        @pl.when(j > 0)
+        def _():
+            packed(b, j - 1, False).wait()
 
         slot = j % 2
         grad = (gh[...], gl[...])
@@ -849,15 +1126,12 @@
             gbuf[slot, 2048 + q * 512 : 2560 + q * 512, :] = dws[:, q * 128 : (q + 1) * 128]
         dpre = mm3(grad, split(ws_ref[0, 0].reshape(512, C)), NT) * slope_ref[0]
         tsh[i, pl.ds(b, 1), :] = colsum(dpre)
+        midway()
         pair_ = split(dpre)
         dwe = mm3((nth[...], ntl[...]), pair_, NN)
         for q in range(4):
             gbuf[slot, q * 512 : (q + 1) * 512, :] = dwe[:, q * 128 : (q + 1) * 128]
         acc[...] += mm3(pair_, split(we_ref[0, 0].reshape(C, 512)), NT)
-
-        @pl.when(j > 0)
-        def _():
-            packed(b, j - 1, False).wait()
 
         packed(b, j, False).start()
 
@@ -882,6 +1156,10 @@
             nth[...], ntl[...] = split((xhat * g1_ref[pl.ds(b, 1), :] + b1_ref[pl.ds(b, 1), :]).T)
             gh[...], gl[...] = split(gf[...])
             acc[...] = jnp.zeros_like(acc)
+
+        @pl.when(j > 0)
+        def _():
+            packed(b, j - 1, True).wait()
 
         slot = j % 2
         grad = (gh[...], gl[...])
@@ -906,6 +1184,8 @@
             dqkv[pl.ds(w * WT, WT), 0:128] = mm3(side_by_side(dpair), k4, NN) * HD ** (-0.5)
             dqkv[pl.ds(w * WT, WT), 128:256] = mm3(dpair, q4, TN)
             dqkv[pl.ds(w * WT, WT), 256:384] = mm3(split(p), do4, TN)
+            if w == 1:
+                midway()
         line = table_line(dbias, pick_ref[...], pile_ref[...])
         for q in range(3):
             tsh[i, pl.ds(4 + 3 * b + q, 1), :] = line[:, q * 512 : (q + 1) * 512]
@@ -918,10 +1198,6 @@
         w = jnp.concatenate([wqkv_ref[0, 0, q] for q in range(3)], axis=1)
         acc[...] += mm3(pair_, split(w), NT)
 
-        @pl.when(j > 0)
-        def _():
-            packed(b, j - 1, True).wait()
-
         packed(b, j, True).start()
 
         @pl.when(j == 3)
@@ -939,18 +1215,6 @@
                 kept()
 
             packed(b, 3, True).wait()
-
-    def ag(k, src, dst, peer, which):
-        return push(src, dst, ags.at[which, k], agr.at[which, k], peer)
-
-    def ag_copies(k):
-        own = (gdense, ext)
-        whole_ = (gall, exall)
-        return [
-            ag(k, own[w], whole_[w].at[tp], (sib, across)[k], w) if k < 2
-            else ag(k, whole_[w].at[tp ^ 2], whole_[w].at[tp ^ 2], sib, w)
-            for w in range(2)
-        ]
 
     @pl.when(step == AG_STEP)
     def _():
@@ -964,288 +1228,34 @@
             for copy in ag_copies(k):
                 copy.start()
 
-    def ag_pass():
-        for copy in ag_copies(1):
-            copy.wait()
-        for copy in ag_copies(2):
-            copy.start()
-
-    def merge(i):
-        t = tp ^ i
-
-        for k in (0, 2):
-
-            @pl.when(i == (1 if k == 0 else 2))
-            def _(k=k):
-                for copy in ag_copies(k):
-                    copy.wait()
-
-        fetch = [pltpu.make_async_copy(q_ref.at[t], qbuf, msem.at[0])]
-        fetch[0].start()
-
-        @pl.when(i == 0)
-        def _():
-            dmw[...] = jnp.zeros((256, C), f32)
-            gf[0:DENSE, :] = gdense[...]
-            extin[...] = ext[...]
-
-        @pl.when(i > 0)
-        def _():
-            two = [
-                pltpu.make_async_copy(gall.at[t], gf.at[pl.ds(0, DENSE)], msem.at[1]),
-                pltpu.make_async_copy(exall.at[t], extin, msem.at[2]),
-            ]
-            for copy in two:
-                copy.start()
-            for copy in two:
-                copy.wait()
-
-        fetch[0].wait()
-        wide = jnp.concatenate([extin[...], jnp.zeros((120, TOK), f32)], axis=0).T[0:DENSE, :]
-        mean, inv, m2 = wide[:, 0:1], wide[:, 1:2], wide[:, 2:3]
-        full = gf[0:DENSE, :]
-        m1 = jnp.sum(full * vec_ref[0:1, :], axis=-1, keepdims=True) / (4.0 * C2)
-        m2 = m2 / (4.0 * C2)
-        fpair = split(full)
-        xhat = (qbuf[...] - mean) * inv
-        gmerged = mm3(fpair, split(mw_ref[...]), NT)
-        dmw[...] += mm3(split(xhat * mg_ref[0:1, :] + mg_ref[1:2, :]), fpair, TN)
-        tsh[0, 10:11, 0:256] += colsum(gmerged * xhat)
-        tsh[0, 10:11, 256:512] += colsum(gmerged)
-
-        @pl.when(i > 0)
-        def _():
-            pltpu.make_async_copy(gqbuf, gq_ref.at[t], msem.at[3]).wait()
-
-        gqbuf[...] = inv * (gmerged * mg_ref[0:1, :] - m1 - xhat * m2)
-        pltpu.make_async_copy(gqbuf, gq_ref.at[t], msem.at[3]).start()
-
-        @pl.when(i == 3)
-        def _():
-            pltpu.make_async_copy(gqbuf, gq_ref.at[t], msem.at[3]).wait()
-            for k in range(4):
-                row = k * 256
-                pair[FULL_CH + row // ROWS, 0, row % ROWS : row % ROWS + 256, :] = dmw[:, k * 128 : (k + 1) * 128]
-
-    def rows(c):
-        return pl.ds(pl.multiple_of(c * ROWS, ROWS), ROWS)
-
-    def load(c, k):
-        return pltpu.make_async_copy(pack.at[tp ^ (2 * k), rows(c)], loc.at[c % 4, k], ls.at[c % 4, k])
-
-    def swap(c, k):
-        return push(pack.at[tp ^ 1 ^ (2 * k), rows(c)], pair.at[c, k], ss.at[k, c], rs.at[k, c], sib)
-
-    def cross(c):
-        return push(pair.at[c, 1], fin.at[c], ss.at[2, c], rs.at[2, c], across)
-
-    def halves(h):
-        return pl.ds(pl.multiple_of(h * HALF, HALF), HALF)
-
-    def side(c):
-        return push(pair.at[c, 0, halves(1 - par)], yr.at[c], ss.at[3, c], rs.at[3, c], beside)
-
-    def bit(q):
-        return pl.ds(pl.multiple_of(q * piece, piece), piece)
-
-    def spread(c, q, slot):
-        return push(yr.at[c, bit(q)], zr.at[c, slot], zs.at[c % 4, q], zq.at[c, slot], device(q))
-
-    def place(q):
-        return pl.ds(pl.multiple_of(par * HALF + q * piece, piece), piece)
-
-    def share(c, q, slot):
-        return push(fin.at[c, place(slot)], fin.at[c, place(slot)], fs.at[c % 4, q], fq.at[c, slot], device(q))
-
-    def back(c):
-        return push(fin.at[c, halves(par)], fin.at[c, halves(par)], ss.at[4, c], rs.at[4, c], beside)
-
-    def write(c):
-        return pltpu.make_async_copy(fin.at[c], out_ref.at[rows(c)], os.at[c])
-
-    low, high = pl.ds(0, 16), pl.ds(16, 24)
-
-    def tiny(k):
-        if k == 0:
-            todo = [(tsh.at[1], tr.at[0]), (tsh.at[3], tr.at[1]), (ta.at[0, high], tx.at[0, high])]
-        elif k == 1:
-            todo = [(tsh.at[2], tx.at[1, low]), (ta.at[1, high], tx.at[1, high])]
-        else:
-            todo = [(ta.at[2], tx.at[2])]
-        peer = (sib, across, beside)[k]
-        return [push(a, b, tss.at[k, i], tsq.at[k, i], peer) for i, (a, b) in enumerate(todo)]
-
-    def tiny_sum(k):
-        if k == 0:
-            ta[1, low] = tsh[0] + tr[0]
-            ta[1, high] = ta[0, high] + tx[0, high]
-            tsh[2] = tsh[2] + tr[1]
-        else:
-            ta[k + 1] = ta[k] + tx[k]
-
-    def tiny_z(q, slot):
-        return push(ta.at[3], tz.at[slot], tzs.at[q], tzq.at[slot], device(q))
-
-    late = RATE * (16 - FIRST)
-    tiny_turn = late + 10
-
-    def begun(s):
-        return jnp.where(s < FIRST, 0, jnp.where(s < STEPS, RATE * (s - FIRST), CHUNKS + 21))
-
-    def turn(p):
-        @pl.when(p == late + 5)
-        def _():
-            ag_pass()
-
-        due = p - late
-
-        @pl.when((due >= 0) & (due < 12) & (due % 3 == 0))
-        def _():
-            merge(due // 3)
-
-        def stage(lag, end):
-            c = p - lag
-            return c, (c >= 0) & (c < end)
-
-        for k in range(4):
-
-            @pl.when(p == tiny_turn + 4 * k)
-            def _(k=k):
-                if k > 0:
-                    for copy in tiny(k - 1):
-                        copy.wait()
-                    tiny_sum(k - 1)
-                if k < 3:
-                    for copy in tiny(k):
-                        copy.start()
-                else:
-                    tz[mine] = ta[3]
-
-                    @pl.loop(1, m)
-                    def _(j):
-                        tiny_z(member(j), mine).start()
-
-        c0, on0 = stage(0, FULL_CH)
-
-        @pl.when(on0)
-        def _():
-            swap(c0, 1).start()
-            load(c0, 1).start()
-
-        c1, on1 = stage(2, FULL_CH)
-
-        @pl.when(on1)
-        def _():
-            load(c1, 1).wait()
-            swap(c1, 1).wait_recv()
-            pair[c1, 1] = pair[c1, 1] + loc[c1 % 4, 1]
-            cross(c1).start()
-
-        c2, on2 = stage(3, FULL_CH)
-
-        @pl.when(on2)
-        def _():
-            swap(c2, 0).start()
-            load(c2, 0).start()
-
-        c3, on3 = stage(6, CHUNKS)
-
-        @pl.when(on3)
-        def _():
-            @pl.when(c3 < FULL_CH)
-            def _():
-                load(c3, 0).wait()
-                swap(c3, 0).wait_recv()
-                cross(c3).wait_recv()
-                pair[c3, 0] = (pair[c3, 0] + loc[c3 % 4, 0]) + fin[c3]
-                swap(c3, 1).wait_send()
-
-            side(c3).start()
-
-        c4, on4 = stage(9, CHUNKS)
-
-        @pl.when(on4)
-        def _():
-            @pl.when(c4 < FULL_CH)
-            def _():
-                swap(c4, 0).wait_send()
-                cross(c4).wait_send()
-
-            side(c4).wait_recv()
-            yr[c4] = yr[c4] + pair[c4, 0, halves(par)]
-
-            @pl.loop(1, m)
-            def _(j):
-                spread(c4, member(j), mine).start()
-
-        c5, on5 = stage(12, CHUNKS)
-
-        @pl.when(on5)
-        def _():
-            side(c5).wait_send()
-            fin[c5, place(mine)] = yr[c5, bit(mine)]
-
-            @pl.loop(1, m)
-            def _(j):
-                spread(c5, member(j), member(j)).wait_recv()
-                fin[c5, place(mine)] = fin[c5, place(mine)] + zr[c5, member(j)]
-
-            @pl.loop(1, m)
-            def _(j):
-                share(c5, member(j), mine).start()
-                spread(c5, member(j), mine).wait_send()
-
-        c6, on6 = stage(15, CHUNKS)
-
-        @pl.when(on6)
-        def _():
-            @pl.loop(1, m)
-            def _(j):
-                share(c6, member(j), member(j)).wait_recv()
-                share(c6, member(j), mine).wait_send()
-
-            back(c6).start()
-
-        c7, on7 = stage(18, CHUNKS)
-
-        @pl.when(on7)
-        def _():
-            back(c7).wait()
-            write(c7).start()
-
-        c8, on8 = stage(21, CHUNKS)
-
-        @pl.when(on8)
-        def _():
-            write(c8).wait()
-
-    @pl.loop(begun(step), begun(step + 1))
-    def _(p):
-        turn(p)
+    @pl.when(step < STEPS - 1)
+    def _():
+        @pl.loop(begun(step) + 1, begun(step + 1))
+        def _(p):
+            turn(p)
 
     @pl.when(step == STEPS - 1)
     def _():
-        @pl.loop(1, m)
-        def _(j):
-            tiny_z(member(j), member(j)).wait_recv()
-            tiny_z(member(j), mine).wait_send()
-
+        @pl.loop(begun(step), begun(step + 1))
+        def _(p):
+            turn(p, True)
+
+    @pl.when(step == STEPS - 1)
+    def _():
         out_own().wait()
         for k in range(2):
             for i in range(4):
                 if k + i > 0:
                     out_copy(k, i).wait_send()
                     out_in(k, i).wait_recv()
-        total = tz[0]
-        for q in range(1, m):
-            total = total + tz[q]
-        tout_ref[...] = total
+        tout_ref[...] = ta[3 + bits]
 
 
 def backward(n, args, ident):
     m = n // 2
     ROWS, FULL_CH, CHUNKS, _ = chunk_plan(n)
     HALF = ROWS // 2
+    bits = m.bit_length() - 1
     dma = pltpu.SemaphoreType.DMA
 
     def fixed(shape):
@@ -1295,12 +1305,12 @@
             pltpu.VMEM((DENSE, C), f32),
             pltpu.VMEM((4, 2, ROWS, 128), f32), pltpu.VMEM((CHUNKS, 2, ROWS, 128), f32),
             pltpu.VMEM((CHUNKS, HALF, 128), f32), pltpu.VMEM((CHUNKS, m, HALF // m, 128), f32),
-            pltpu.VMEM(lanes, f32), pltpu.VMEM((4, TINY, C), f32), pltpu.VMEM((3, TINY, C), f32),
-            pltpu.VMEM((m, TINY, C), f32), pltpu.VMEM((4, 16, C), f32), pltpu.VMEM((2, 16, C), f32),
+            pltpu.VMEM(lanes, f32), pltpu.VMEM((4 + bits, TINY, C), f32),
+            pltpu.VMEM((3 + bits, TINY, C), f32), pltpu.VMEM((4, 16, C), f32), pltpu.VMEM((2, 16, C), f32),
             dma((2,)), dma((7,)), dma((7,)), dma((2, 3)), dma((2, 3)), dma((2,)), dma((4,)),
             dma((5, CHUNKS)), dma((5, CHUNKS)), dma((4, m)), dma((CHUNKS, m)), dma((4, m)),
-            dma((CHUNKS, m)), dma((4, 2)), dma((CHUNKS,)), dma((m,)), dma((m,)),
-            dma((2, 4)), dma((2, 4)), dma((1,)), dma((3, 3)), dma((3, 3)),
+            dma((CHUNKS, m)), dma((4, 2)), dma((CHUNKS,)),
+            dma((2, 4)), dma((2, 4)), dma((1,)), dma((3 + bits, 3)), dma((3 + bits, 3)),
         ],
         compiler_params=pltpu.CompilerParams(
             collective_id=ident, has_side_effects=True, vmem_limit_bytes=60 << 20,

time: 389 us -> 384 us (0.987)
  no operation moved by 1% of the time
where the time goes in v7:
time: 384 us
  Pallas kernels  350 us (91%)
  local copies, waits for them, and re-layouts  27.2 us (7%)
    pallas_call x1, Pallas kernels, backward(): pl.pallas_call(functools.partial(bwd_kernel, n), grid=(STEPS,), in_specs=...  225 us
    pallas_call x1, Pallas kernels, forward(): pl.pallas_call(functools.partial(fwd_kernel, n), grid=(F_STEPS,), in_spec...  120 us

profile of v7, /device:TPU:0, one launch (start us, length us, event | category | flops | bytes accessed | tf_op | source)
XLA Modules:
  0.0 383.5 jit_solution(14301259666807289445)
XLA Ops:
  0.7 0.1 pad.27.clone
  0.7 0.1 pad.30.clone
  0.8 0.7 copy.74
  1.5 0.1 reshape.123
  1.6 0.7 copy.73
  2.3 0.1 reshape.125
  2.4 0.7 pad_bitcast_fusion
  3.0 0.7 maximum_maximum_fusion.1.refs_2_.refs_20_
  3.7 0.7 convert_element_type.11
  4.4 1.4 maximum_maximum_fusion.refs_8_
  5.8 0.8 reshape.144
  6.6 0.1 reshape.131
  6.7 0.1 copy.58
  6.8 0.1 copy.59
  6.9 0.6 pad.19.refs_16_
  7.5 2.0 copy.52
  9.5 1.6 convolution_bitcast_fusion
  11.1 0.6 copy.55
  11.7 0.3 reshape.145
  11.9 0.0 copy-start.3
  12.0 0.7 convolution_bitcast_fusion.1
  12.7 0.1 copy.69
  12.8 0.8 pad.18.clone
  13.6 0.0 copy-done.3
  13.6 0.1 reshape.133
  13.7 0.1 slice.31
  13.8 0.1 maximum_bitcast_fusion
  13.9 0.1 copy.60
  14.1 0.1 copy.61
  14.2 0.9 pad.20.refs_17_
  15.1 1.9 copy.50
  17.0 1.5 reshape.118
  18.6 2.5 copy.51
  21.1 1.0 reshape.119
  22.1 1.1 pad.17.refs_0_.refs_17_
  23.2 120.3 %forward.1 = (f32[4,2,4,512,128]{4,3,2,1,0:T(8,128)}, f32[4,2,9,128,512]{4,3,2,1,0:T(8,128)}, f32[4,2,6,32,128]{4,3,2,1,0:T(8,128)}, f32[2,384,512]{2,1,0:T(8,12...) custom-call(f32[4,304,256]{2,1,0:T(8,128)} %pad.17.refs_0_.refs_17_,, ...), custom_call_target="tpu_custom_call" | custom-call | tf_op jit(solution)/shard_map/forward/pallas_call | solution.py:671
  143.5 224.6 %backward.1 = (f32[4,12288,128]{2,1,0:T(8,128)}, f32[4,304,512]{2,1,0:T(8,128)}, f32[4,8,384]{2,1,0:T(8,128)}, f32[2,24,32,128]{3,2,1,0:T(8,128)}, f32[13312,128...) custom-call(f32[4,2,192,128]{3,2,1,0:T(8,128)} %bitcast.71, f32[2,384,512]{2,1,0:T(8,128)} %get-tuple-element.55.refs_1_, ...), custom_call_target="tpu_custom_call" | custom-call | tf_op jit(solution)/shard_map/backward/pallas_call | solution.py:1291
  368.1 2.0 reshape.139
  370.1 0.1 slice.28
  370.2 0.1 pad_maximum_fusion
  370.2 0.4 copy.62
  370.6 0.2 copy.63
  370.8 0.9 reshape.138
  371.7 1.5 copy.64
  373.2 2.5 reshape.140
  375.7 1.8 copy.65
  377.5 5.4 %unpack.1 = (f32[2,512,512]{2,1,0:T(8,128)}, f32[2,512,512]{2,1,0:T(8,128)}, f32[2,3,512,128]{3,2,1,0:T(8,128)}, f32[2,128,512]{2,1,0:T(8,128)}, f32[4,64,512]{2...) custom-call(f32[26,512,128]{2,1,0:T(8,128)} %bitcast.57, ...), custom_call_target="tpu_custom_call" | custom-call | tf_op jit(solution)/shard_map/unpack/pallas_call | solution.py:1366
  382.9 0.6 slice_reduce_fusion
  (12 shorter events, 0.1 us)
Async XLA Ops:
  7.5 4.4 %copy-start.1 = (f32[2,5,128,190,1,1]{2,3,1,0,5,4:T(8,128)S(1)}, f32[2,5,128,190,1,1]{2,3,1,0,5,4:T(8,128)}, u32[]{:S(2)}) copy-start(f32[2,5,128,190,1,1]{2,3,1,0,5,4:T(8,128)} %constant.34) | copy-start | bytes 2918404
  11.9 1.7 copy-start.3
  368.1 2.0 copy-start.2
  375.7 1.8 copy-start
